TPU v7x, 256 devices: a whole 4x4x8 slice. The times are simulated.
256 devices in a mesh: grp: 8 (over x, core), shard: 32 (over y, z).
Axes of the slice: x: 4, y: 4, z: 8, core: 2. Of those that a mesh axis runs over, the one named last changes fastest.
Arguments:
- cand_table: bfloat16 [4096, 512], P('grp'), may hold values from -6 to 6
- inverse: int32 [65536], P(('grp', 'shard')), may hold values from 0 to 4095
- cache_keys: bfloat16 [524288, 512], P(('grp', 'shard')), may hold values from -6 to 6
- cache_values: bfloat16 [524288, 512], P(('grp', 'shard')), may hold values from -6 to 6
- block_dest: int32 [4096, 1], P(('grp', 'shard')), may hold values from 0 to 31; in each aligned block of 16 rows (0 to 15, 16 to 31, ...) at most 2 rows name the same one
- w_in: bfloat16 [512, 1024], replicated, may hold values from -0.25 to 0.25
- w_out: bfloat16 [512, 512], replicated, may hold values from -0.25 to 0.25
Outputs:
- scored: bfloat16 [65536, 512], P(('grp', 'shard'))
Inputs may be any that keep to these rules, and one draw needn't show every extreme that they name: `block_dest`: among the 16 blocks held by one device, at most 2 name the same scorer.
All inputs are finite; a program needn't handle non-finite values.
Results may differ from a plain program's by a relative error of at most 0.0082.
Values may be sent and summed in bfloat16 or wider, within the bound.
No kernel may reach another device: no remote copies, remote signals or barrier semaphores. Data moves between devices by JAX's collectives and lax.ppermute only.
A program may use at most 128 MiB of HBM per device.

v0:
```python
import functools
import math

import jax
import jax.numpy as jnp
from jax import lax
from jax.experimental import pallas as pl
from jax.experimental.pallas import tpu as pltpu
from jax.sharding import PartitionSpec as P

H = 8
BLK = 128
LANES = 128
NY = 4
CORES = 2
TILE = 256


VMEM = pl.BlockSpec(memory_space=pltpu.VMEM)
SMEM = pl.BlockSpec(memory_space=pltpu.SMEM)


def layer_norm(inputs):
    center = inputs - jnp.mean(inputs, axis=-1, keepdims=True)
    spread = jnp.mean(center * center, axis=-1, keepdims=True)
    return center * lax.rsqrt(spread + 1e-05)


def half_silu(half):
    return half + half * jnp.tanh(half)


def norm_kernel(in_ref, out_ref):
    out_ref[...] = layer_norm(in_ref[...].astype(jnp.float32)).astype(out_ref.dtype)


def norm(rows):
    return pl.pallas_call(
        norm_kernel,
        out_shape=jax.ShapeDtypeStruct(rows.shape, jnp.bfloat16),
        in_specs=[VMEM],
        out_specs=VMEM,
        compiler_params=pltpu.CompilerParams(vmem_limit_bytes=8 << 20),
        name="norm",
    )(rows)


def project_kernel(first, scale, count, *refs):
    w_ref = refs[0]
    rows_in = refs[1 : 1 + count]
    out_ref = refs[-1]
    width = w_ref.shape[0]
    cuts = width // LANES
    at = first
    for row_ref in rows_in:
        rows = row_ref.shape[0]
        tile = math.gcd(rows, TILE)

        def step(i, carry, row_ref=row_ref, at=at, tile=tile):
            begin = pl.multiple_of(i * tile, tile)
            half = 0.5 * jnp.dot(
                row_ref[pl.ds(begin, tile), :], w_ref[:, width:], preferred_element_type=jnp.float32
            )
            query = half_silu(half).astype(jnp.bfloat16).astype(jnp.float32) * scale
            for c in range(cuts):
                out_ref[pl.ds((at + begin) * cuts + c, tile, stride=cuts), :] = query[:, c * LANES : (c + 1) * LANES]
            return carry

        lax.fori_loop(0, rows // tile, step, 0)
        at += rows


def project(table, first, total, pieces, w_in, scale):
    width = w_in.shape[0]
    rows = sum(p.shape[0] for p in pieces)
    ins = [w_in, *pieces]
    aliases = {}
    kernel = functools.partial(project_kernel, first, scale, len(pieces))
    if table is not None:
        aliases = {len(ins): 0}
        ins.append(table)
    return pl.pallas_call(
        kernel,
        out_shape=jax.ShapeDtypeStruct((total * width // LANES, LANES), jnp.float32),
        in_specs=[VMEM] * len(ins),
        out_specs=VMEM,
        input_output_aliases=aliases,
        cost_estimate=pl.CostEstimate(
            flops=2 * rows * width * width, bytes_accessed=rows * width * 6, transcendentals=rows * width
        ),
        compiler_params=pltpu.CompilerParams(vmem_limit_bytes=8 << 20),
        name="project",
    )(*ins)


def gate_kernel(count, index_ref, w_ref, *refs):
    pieces, out_ref = refs[:count], refs[-1]
    cand, width = out_ref.shape
    total = jnp.zeros((cand, width), jnp.float32)
    first = 0
    index = jnp.broadcast_to(index_ref[...], (LANES, cand)).T[:, :1]
    for piece in pieces:
        rows = piece.shape[0]
        ids = lax.broadcasted_iota(jnp.int32, (cand, rows), 1) + first
        pick = jnp.where(index == ids, 1.0, 0.0).astype(jnp.bfloat16)
        total = total + jnp.dot(pick, piece[...], preferred_element_type=jnp.float32)
        first += rows
    normed = total.astype(jnp.bfloat16)
    half = 0.5 * jnp.dot(normed, w_ref[:, :width], preferred_element_type=jnp.float32)
    out_ref[...] = half_silu(half).astype(jnp.bfloat16)


def gate_rows(index, pieces, w_in):
    width = w_in.shape[0]
    cand = index.shape[0]
    rows = sum(p.shape[0] for p in pieces)
    return pl.pallas_call(
        functools.partial(gate_kernel, len(pieces)),
        out_shape=jax.ShapeDtypeStruct((cand, width), jnp.bfloat16),
        in_specs=[VMEM] * (2 + len(pieces)),
        out_specs=VMEM,
        cost_estimate=pl.CostEstimate(
            flops=2 * cand * width * (rows + width), bytes_accessed=rows * width * 2, transcendentals=cand * width
        ),
        compiler_params=pltpu.CompilerParams(vmem_limit_bytes=8 << 20),
        name="gate",
    )(index[None, :], w_in, *pieces)


def attend_kernel(sizes, unroll, index_ref, count_ref, block_ref, order_ref, table_ref, k_ref, v_ref, *refs):
    outs, (rows_ref, query_ref, sum_ref) = refs[: len(sizes)], refs[len(sizes) :]
    rows, width = sum_ref.shape
    cuts = width // LANES
    low = lax.broadcasted_iota(jnp.int32, (BLK, LANES), 1) < LANES // 2

    def split(tile):
        zero = jnp.zeros_like(tile)
        return jnp.concatenate([jnp.where(low, tile, zero), jnp.where(low, zero, tile)], axis=0)

    def task(j, carry):
        scorer = order_ref[2 * j]
        start = order_ref[2 * j + 1]
        blocks = count_ref[scorer]
        sum_ref[...] = jnp.zeros_like(sum_ref)

        @pl.when(blocks > 0)
        def _():
            def fetch(i, inner_carry):
                begin = start + i * unroll
                to = i * (unroll * cuts)
                for k in range(unroll):
                    at = pl.multiple_of(index_ref[begin + k], cuts)
                    rows_ref[pl.ds(pl.multiple_of(to + k * cuts, cuts), cuts), :] = table_ref[pl.ds(at, cuts), :]
                return inner_carry

            lax.fori_loop(0, rows // unroll, fetch, 0)
            for c in range(cuts):
                query_ref[:, c * LANES : (c + 1) * LANES] = rows_ref[pl.ds(c, rows, stride=cuts), :].astype(jnp.bfloat16)

            def one_block(slot, inner_carry):
                begin = pl.multiple_of(block_ref[2 * scorer + slot] * BLK, BLK)
                for c in range(cuts):
                    lanes = slice(c * LANES, (c + 1) * LANES)
                    keys = split(k_ref[pl.ds(begin, BLK), lanes])
                    half = lax.dot_general(
                        query_ref[:, lanes], keys, (((1,), (1,)), ((), ())), preferred_element_type=jnp.float32
                    )
                    weight = half_silu(half).astype(jnp.bfloat16)
                    values = split(v_ref[pl.ds(begin, BLK), lanes])
                    sum_ref[:, lanes] += jnp.dot(weight, values, preferred_element_type=jnp.float32)
                return inner_carry

            lax.fori_loop(0, blocks, one_block, 0)

        at = 0
        for out_ref, number in zip(outs, sizes):
            here = j - at

            @pl.when((here >= 0) & (here < number))
            def _(out_ref=out_ref, here=here):
                out_ref[here] = sum_ref[...].astype(out_ref.dtype)

            at += number
        return carry

    lax.fori_loop(0, sum(sizes), task, 0)


def attend(sizes, rows, index, count, block, order, table, keys, values):
    width = keys.shape[1]
    number = sum(sizes)
    return pl.pallas_call(
        functools.partial(attend_kernel, tuple(sizes), 16 if rows % 16 == 0 else 8),
        out_shape=[jax.ShapeDtypeStruct((n, rows, width), jnp.bfloat16) for n in sizes],
        in_specs=[SMEM] * 4 + [VMEM] * 3,
        out_specs=[VMEM] * len(sizes),
        scratch_shapes=[
            pltpu.VMEM((rows * width // LANES, LANES), jnp.float32),
            pltpu.VMEM((rows, width), jnp.bfloat16),
            pltpu.VMEM((rows, width), jnp.float32),
        ],
        cost_estimate=pl.CostEstimate(
            flops=number * rows * BLK * width * 8,
            bytes_accessed=number * rows * width * 4,
            transcendentals=number * rows * BLK * H // 2,
        ),
        compiler_params=pltpu.CompilerParams(vmem_limit_bytes=6 << 20),
        name="attend",
    )(index, count, block, order, table, keys, values)


def finish_kernel(halves, *refs):
    gate_ref, w_ref, out_ref = refs[-3], refs[-2], refs[-1]
    at, first = 0, 0
    for number in halves:
        total = refs[at][...].astype(jnp.float32)
        for ref in refs[at + 1 : at + number]:
            total = total + ref[...].astype(jnp.float32)
        rows = total.shape[0]
        gated = (layer_norm(total) * gate_ref[first : first + rows, :].astype(jnp.float32)).astype(jnp.bfloat16)
        out_ref[first : first + rows, :] = jnp.dot(
            gated, w_ref[...], preferred_element_type=jnp.float32
        ).astype(out_ref.dtype)
        at += number
        first += rows


def finish(halves, gate_u, w_out):
    terms = [t for half in halves for t in half]
    return pl.pallas_call(
        functools.partial(finish_kernel, [len(half) for half in halves]),
        out_shape=jax.ShapeDtypeStruct(gate_u.shape, jnp.bfloat16),
        in_specs=[VMEM] * (len(terms) + 2),
        out_specs=VMEM,
        compiler_params=pltpu.CompilerParams(vmem_limit_bytes=8 << 20),
        name="finish",
    )(*terms, gate_u, w_out)


def add(*terms):
    total = terms[0].astype(jnp.float32)
    for term in terms[1:]:
        total = total + term.astype(jnp.float32)
    return total.astype(jnp.bfloat16)


def compute(cand_table, inverse, cache_keys, cache_values, block_dest, w_in, w_out):
    width = w_out.shape[0]
    cand = inverse.shape[0]
    groups, peers = lax.axis_size("grp"), lax.axis_size("shard")
    nx, nz = groups // CORES, peers // NY
    g, s = lax.axis_index("grp"), lax.axis_index("shard")
    part_rows = cand_table.shape[0]
    total_rows = groups * part_rows
    half_part = part_rows // 2
    cuts = width // LANES

    def x_shift(value, k):
        return lax.ppermute(
            value, "grp", [(x * CORES + c, (x + k) % nx * CORES + c) for x in range(nx) for c in range(CORES)]
        )

    def swap(value):
        return lax.ppermute(
            value, "grp", [(x * CORES + c, x * CORES + 1 - c) for x in range(nx) for c in range(CORES)]
        )

    def z_shift(value, k):
        return lax.ppermute(
            value, "shard", [(y * nz + z, y * nz + (z + k) % nz) for y in range(NY) for z in range(nz)]
        )

    def y_shift(value, k):
        return lax.ppermute(
            value, "shard", [(y * nz + z, (y + k) % NY * nz + z) for y in range(NY) for z in range(nz)]
        )

    normed = norm(cand_table)
    ahead = x_shift(normed, -1)
    behind = x_shift(normed, 1)
    other = swap(normed)
    far_top = x_shift(ahead[:half_part], -1)
    far_bottom = x_shift(behind[half_part:], 1)

    wanted = inverse
    step = 1
    while step < nz:
        wanted = jnp.concatenate([wanted, z_shift(wanted, -step)])
        step *= 2
    step = 1
    while step < NY:
        wanted = jnp.concatenate([wanted, y_shift(wanted, -step)])
        step *= 2

    def arrival(row):
        owner = row // part_rows
        place = (owner // CORES + nx - g // CORES) & (nx - 1)
        return (place * CORES + ((owner ^ g) & (CORES - 1))) * part_rows + row % part_rows

    index = arrival(wanted) * cuts
    own_relative = arrival(inverse)

    destination = block_dest[:, 0]
    blocks = destination.shape[0]
    block_ids = jnp.arange(blocks, dtype=jnp.int32)
    earlier = (destination[:, None] == destination[None, :]) & (block_ids[None, :] < block_ids[:, None])
    rank = jnp.sum(earlier.astype(jnp.int32), axis=1)
    rel_dest = ((destination // nz + NY - s // nz) & (NY - 1)) * nz + ((destination + nz - s) & (nz - 1))
    slots = jnp.arange(2 * peers, dtype=jnp.int32)
    match = (rel_dest * 2 + rank)[None, :] == slots[:, None]
    block = jnp.sum(jnp.where(match, block_ids[None, :], 0), axis=1)
    count = jnp.sum(
        (rel_dest[None, :] == jnp.arange(peers, dtype=jnp.int32)[:, None]).astype(jnp.int32), axis=1
    )

    scale = 0.5 / math.sqrt(width // H)
    chip = CORES * part_rows
    near_rows = [normed, other]
    table = project(None, 0, total_rows, near_rows, w_in, scale)
    ahead_rows = [ahead, swap(ahead)]
    behind_rows = [behind, swap(behind)]
    table = project(table, 1 * chip, total_rows, ahead_rows, w_in, scale)
    table = project(table, 3 * chip, total_rows, behind_rows, w_in, scale)
    far_rows = [far_top, far_bottom, swap(far_top), swap(far_bottom)]
    table = project(table, 2 * chip, total_rows, far_rows, w_in, scale)

    half = cand // 2
    half_z = nz // 2
    z_of = lambda dz, dys=range(NY): [(dy, dz, 0) for dy in dys]
    y_of = lambda dy, dzs=range(nz): [(dy, dz, half) for dz in dzs]
    calls = [
        [z_of(4, (0, 1)), z_of(4, (2, 3)), y_of(2, range(half_z)), y_of(2, range(half_z, nz))],
        [z_of(3), z_of(5), y_of(1), y_of(3)],
        [z_of(2), z_of(6), z_of(1), z_of(7), z_of(0), y_of(0)],
    ]
    flat = [t for call in calls for piece in call for t in piece]
    order = [v for dy, dz, start in flat for v in (dy * nz + dz, (dy * nz + dz) * cand + start)]
    parts, at = [], 0
    for call in calls:
        sizes = [len(piece) for piece in call]
        mine = jnp.asarray(order[2 * at : 2 * (at + sum(sizes))], jnp.int32)
        parts += attend(sizes, half, index, count, block, mine, table, cache_keys, cache_values)
        at += sum(sizes)
    z4a, z4b, y2a, y2b, z3, z5, y1, y3, z2, z6, z1, z7, z0, y0 = parts

    two = NY // 2
    up = z_shift(z4a, 1)
    down = z_shift(z4b, -1)
    far_y_up = y_shift(y2a, 1)
    far_y_down = y_shift(y2b, -1)
    up = jnp.concatenate([add(up, z3[:two]), z3[two:]], axis=0)
    down = jnp.concatenate([z5[:two], add(down, z5[two:])], axis=0)
    up = z_shift(up, 1)
    down = z_shift(down, -1)
    y_up = jnp.concatenate([add(far_y_up, y1[:half_z]), y1[half_z:]], axis=0)
    y_down = jnp.concatenate([y3[:half_z], add(far_y_down, y3[half_z:])], axis=0)
    y_up = y_shift(y_up, 1)
    y_down = y_shift(y_down, -1)
    up, down = z_shift(add(up, z2), 1), z_shift(add(down, z6), -1)
    up, down = z_shift(add(up, z1), 1), z_shift(add(down, z7), -1)

    quarter = half // 2

    def y_sum(dz, rows):
        return [y0[dz, rows], y_up[dz, rows], y_down[dz, rows]]

    first, last = slice(0, quarter), slice(quarter, half)
    both = slice(0, half)
    y_first = z_shift(add(*y_sum(4, first)), 1)
    y_last = z_shift(add(*y_sum(4, last)), -1)
    y_first = z_shift(jnp.concatenate([add(y_first, *y_sum(3, first)), add(*y_sum(3, last))], axis=0), 1)
    y_last = z_shift(jnp.concatenate([add(*y_sum(5, first)), add(y_last, *y_sum(5, last))], axis=0), -1)
    for k in (2, 1):
        y_first = z_shift(add(y_first, *y_sum(k, both)), 1)
        y_last = z_shift(add(y_last, *y_sum(nz - k, both)), -1)

    def z_sum(dy, rows):
        return [z0[dy, rows], up[dy, rows], down[dy, rows]]

    z_first = y_shift(add(*z_sum(2, first)), 1)
    z_last = y_shift(add(*z_sum(2, last)), -1)
    z_first = y_shift(jnp.concatenate([add(z_first, *z_sum(1, first)), add(*z_sum(1, last))], axis=0), 1)
    z_last = y_shift(jnp.concatenate([add(*z_sum(3, first)), add(z_last, *z_sum(3, last))], axis=0), -1)

    gate_u = gate_rows(own_relative, near_rows + ahead_rows + far_rows + behind_rows, w_in)
    return finish(
        [[*z_sum(0, both), z_first, z_last], [*y_sum(0, both), y_first, y_last]], gate_u, w_out
    )


def solution(mesh):
    in_specs = (
        P("grp", None),
        P(("grp", "shard")),
        P(("grp", "shard"), None),
        P(("grp", "shard"), None),
        P(("grp", "shard"), None),
        P(),
        P(),
    )
    out_specs = P(("grp", "shard"), None)
    return jax.shard_map(compute, mesh=mesh, in_specs=in_specs, out_specs=out_specs, check_vma=False)
```

profile of v0, /device:TPU:2, one launch (start us, length us, event | category | flops | bytes accessed | tf_op | source)
XLA Modules:
  0.0 167.9 jit_solution(3580846263784546661)
XLA Ops:
  0.0 1.0 copy-done.4
  1.5 1.6 collective-permute-start.7
  3.0 0.8 collective-permute-start.5
  3.9 5.5 %collective-permute-start = (s32[256]{0:T(256)}, s32[256]{0:T(256)S(1)}, u32[]{:S(2)}, u32[]{:S(2)}) collective-permute-start(s32[256]{0:T(256)} %param.11), channel_id=1, source_target_pairs={{0,7},{1,0},{2,1},{3,2},{4,3},{5,4},{6,5},{7,6},{8,15},{9,8},{10,9... | collective-permute-start | bytes 3080 | tf_op jit(solution)/shard_map/ppermute | solution.py:269
  9.4 0.9 convert_reduce_fusion
  12.4 1.9 %collective-permute-start.1 = (s32[512]{0:T(512)S(1)}, s32[512]{0:T(512)S(1)}, u32[]{:S(2)}, u32[]{:S(2)}) collective-permute-start(s32[512]{0:T(512)S(1)} %pad_add_fusion.2), channel_id=1, source_target_pairs={{0,6},{1,7},{2,0},{3,1},{4,2},{5,3},{6,4},{7,5},{8,14},{9,15},{10,... | collective-permute-start | bytes 6152 | tf_op jit(solution)/shard_map/ppermute | solution.py:269
  14.4 2.6 %collective-permute-done.1 = s32[512]{0:T(512)S(1)} collective-permute-done((s32[512]{0:T(512)S(1)}, s32[512]{0:T(512)S(1)}, u32[]{:S(2)}, u32[]{:S(2)}) %collective-permute-start.1) | collective-permute-done | bytes 2080 | tf_op jit(solution)/shard_map/ppermute | solution.py:269
  17.6 2.8 %collective-permute-start.2 = (s32[1024]{0:T(1024)S(1)}, s32[1024]{0:T(1024)S(1)}, u32[]{:S(2)}, u32[]{:S(2)}) collective-permute-start(s32[1024]{0:T(1024)S(1)} %pad_add_fusion.1), channel_id=1, source_target_pairs={{0,4},{1,5},{2,6},{3,7},{4,0},{5,1},{6,2},{7,3},{8,12},{9,13},{10,... | collective-permute-start | bytes 12296 | tf_op jit(solution)/shard_map/ppermute | solution.py:269
  20.4 4.7 %collective-permute-done.2 = s32[1024]{0:T(1024)S(1)} collective-permute-done((s32[1024]{0:T(1024)S(1)}, s32[1024]{0:T(1024)S(1)}, u32[]{:S(2)}, u32[]{:S(2)}) %collective-permute-start.2) | collective-permute-done | bytes 4128 | tf_op jit(solution)/shard_map/ppermute | solution.py:269
  25.8 3.0 %collective-permute-start.3 = (s32[2048]{0:T(1024)S(1)}, s32[2048]{0:T(1024)S(1)}, u32[]{:S(2)}, u32[]{:S(2)}) collective-permute-start(s32[2048]{0:T(1024)S(1)} %pad_add_fusion), channel_id=1, source_target_pairs={{0,24},{1,25},{2,26},{3,27},{4,28},{5,29},{6,30},{7,31},{8,0},{9,1... | collective-permute-start | bytes 24584 | tf_op jit(solution)/shard_map/ppermute | solution.py:274
  28.8 1.4 collective-permute-done.3
  30.2 2.5 %collective-permute-start.4 = (s32[4096]{0:T(1024)S(1)}, s32[4096]{0:T(1024)S(1)}, u32[]{:S(2)}, u32[]{:S(2)}) collective-permute-start(s32[4096]{0:T(1024)S(1)} %get-tuple-element.51), channel_id=1, source_target_pairs={{0,16},{1,17},{2,18},{3,19},{4,20},{5,21},{6,22},{7,23},{8,24},{9,... | collective-permute-start | bytes 49160 | tf_op jit(solution)/shard_map/ppermute | solution.py:274
  32.7 1.6 collective-permute-start.8
  35.7 3.5 %collective-permute-done.8.refs_2_.refs_5_ = bf16[256,512]{1,0:T(8,128)(2,1)S(1)} collective-permute-done((bf16[256,512]{1,0:T(8,128)(2,1)S(1)}, bf16[256,512]{1,0:T(8,128)(2,1)S(1)}, u32[]{:S(2)}, u32[]{:S(2)}) %collective-permute-start.8) | collective-permute-done | bytes 262176 | tf_op jit(solution)/shard_map/ppermute | solution.py:259
  39.1 1.6 collective-permute-done.6.refs_1_.refs_4_
  40.8 1.2 copy-done
  42.0 1.5 project.4.refs_3_
  43.6 1.5 project.5.refs_3_
  45.1 1.5 project.6.refs_5_
  46.6 0.9 project.7.table_ref
  48.8 4.7 %attend.4 = (bf16[2,128,512]{2,1,0:T(8,128)(2,1)S(1)}, bf16[2,128,512]{2,1,0:T(8,128)(2,1)S(1)}, bf16[4,128,512]{2,1,0:T(8,128)(2,1)S(1)}, bf16[4,128,512]{2,1,0:T(8,128)(2,1)S(1)}) custom-call(s32[8192]{0:T(1024)S(1)} %fusion.24.index_ref, s32[32]{0:T(128)S(1)} %convert_reduce_fusion.1.count_ref, s32[64]{0:T(128)S(1)} %select_reduce_fusion.block_ref, ...), custom_call_target="tpu_custom_call" | custom-call | flops 805306368 | bytes 3145728 | tf_op jit(solution)/shard_map/attend/pallas_call | solution.py:192
  53.5 1.8 %collective-permute-start.14 = (bf16[2,128,512]{2,1,0:T(8,128)(2,1)S(1)}, bf16[2,128,512]{2,1,0:T(8,128)(2,1)S(1)}, u32[]{:S(2)}, u32[]{:S(2)}) collective-permute-start(bf16[2,128,512]{2,1,0:T(8,128)(2,1)S(1)} %get-tuple-element.20), channel_id=1, source_target_pairs={{0,1},{1,2},{2,3},{3,4},{4,5},{5,6},{6,7},{7,0},{8,9},{9,10},{10,1... | collective-permute-start | bytes 786440 | tf_op jit(solution)/shard_map/ppermute | solution.py:269
  55.3 3.0 %collective-permute-start.18 = (bf16[2,128,512]{2,1,0:T(8,128)(2,1)S(1)}, bf16[2,128,512]{2,1,0:T(8,128)(2,1)S(1)}, u32[]{:S(2)}, u32[]{:S(2)}) collective-permute-start(bf16[2,128,512]{2,1,0:T(8,128)(2,1)S(1)} %get-tuple-element.25), channel_id=1, source_target_pairs={{0,7},{1,0},{2,1},{3,2},{4,3},{5,4},{6,5},{7,6},{8,15},{9,8},{10,9... | collective-permute-start | bytes 786440 | tf_op jit(solution)/shard_map/ppermute | solution.py:269
  58.3 3.7 %collective-permute-start.26 = (bf16[4,128,512]{2,1,0:T(8,128)(2,1)S(1)}, bf16[4,128,512]{2,1,0:T(8,128)(2,1)S(1)}, u32[]{:S(2)}, u32[]{:S(2)}) collective-permute-start(bf16[4,128,512]{2,1,0:T(8,128)(2,1)S(1)} %get-tuple-element.29), channel_id=1, source_target_pairs={{0,8},{1,9},{2,10},{3,11},{4,12},{5,13},{6,14},{7,15},{8,16},{9,17... | collective-permute-start | bytes 1572872 | tf_op jit(solution)/shard_map/ppermute | solution.py:274
  62.0 8.6 %attend.5 = (bf16[4,128,512]{2,1,0:T(8,128)(2,1)S(1)}, bf16[4,128,512]{2,1,0:T(8,128)(2,1)S(1)}, bf16[8,128,512]{2,1,0:T(8,128)(2,1)S(1)}, bf16[8,128,512]{2,1,0:T(8,128)(2,1)S(1)}) custom-call(s32[8192]{0:T(1024)S(1)} %fusion.24.index_ref, s32[32]{0:T(128)S(1)} %convert_reduce_fusion.1.count_ref, s32[64]{0:T(128)S(1)} %select_reduce_fusion.block_ref, ...), custom_call_target="tpu_custom_call" | custom-call | flops 1610612736 | bytes 6291456 | tf_op jit(solution)/shard_map/attend/pallas_call | solution.py:192
  70.7 16.4 %attend.3 = (bf16[4,128,512]{2,1,0:T(8,128)(2,1)S(1)}, bf16[4,128,512]{2,1,0:T(8,128)(2,1)S(1)}, bf16[4,128,512]{2,1,0:T(8,128)(2,1)S(1)}, bf16[4,128,512]{2,1,0...) custom-call(s32[8192]{0:T(1024)S(1)} %fusion.24.index_ref, ...), custom_call_target="tpu_custom_call" | custom-call | flops 1879048192 | bytes 7340032 | tf_op jit(solution)/shard_map/attend/pallas_call | solution.py:192
  87.3 0.9 collective-permute-start.19
  88.3 1.3 collective-permute-start.15
  89.9 2.4 %collective-permute-start.29 = (bf16[8,128,512]{2,1,0:T(8,128)(2,1)S(1)}, bf16[8,128,512]{2,1,0:T(8,128)(2,1)S(1)}, u32[]{:S(2)}, u32[]{:S(2)}) collective-permute-start(bf16[8,128,512]{2,1,0:T(8,128)(2,1)S(1)} %pad_maximum_fusion.1), channel_id=1, source_target_pairs={{0,24},{1,25},{2,26},{3,27},{4,28},{5,29},{6,30},{7,31},{8,0},{9,1... | collective-permute-start | bytes 3145736 | tf_op jit(solution)/shard_map/ppermute | solution.py:274
  92.6 8.8 %collective-permute-done.19 = bf16[4,128,512]{2,1,0:T(8,128)(2,1)S(1)} collective-permute-done((bf16[4,128,512]{2,1,0:T(8,128)(2,1)S(1)}, bf16[4,128,512]{2,1,0:T(8,128)(2,1)S(1)}, u32[]{:S(2)}, u32[]{:S(2)}) %collective-permute-start.19) | collective-permute-done | bytes 524320 | tf_op jit(solution)/shard_map/ppermute | solution.py:269
  102.1 2.0 %collective-permute-start.16 = (bf16[4,128,512]{2,1,0:T(8,128)(2,1)S(1)}, bf16[4,128,512]{2,1,0:T(8,128)(2,1)S(1)}, u32[]{:S(2)}, u32[]{:S(2)}) collective-permute-start(bf16[4,128,512]{2,1,0:T(8,128)(2,1)S(1)} %add_convert_fusion.5), channel_id=1, source_target_pairs={{0,1},{1,2},{2,3},{3,4},{4,5},{5,6},{6,7},{7,0},{8,9},{9,10},{10,1... | collective-permute-start | bytes 1572872 | tf_op jit(solution)/shard_map/ppermute | solution.py:269
  104.0 1.7 gate.1.refs_10_
  105.8 10.6 %collective-permute-done.20 = bf16[4,128,512]{2,1,0:T(8,128)(2,1)S(1)} collective-permute-done((bf16[4,128,512]{2,1,0:T(8,128)(2,1)S(1)}, bf16[4,128,512]{2,1,0:T(8,128)(2,1)S(1)}, u32[]{:S(2)}, u32[]{:S(2)}) %collective-permute-start.20) | collective-permute-done | bytes 524320 | tf_op jit(solution)/shard_map/ppermute | solution.py:269
  116.9 1.9 %collective-permute-start.17 = (bf16[4,128,512]{2,1,0:T(8,128)(2,1)S(1)}, bf16[4,128,512]{2,1,0:T(8,128)(2,1)S(1)}, u32[]{:S(2)}, u32[]{:S(2)}) collective-permute-start(bf16[4,128,512]{2,1,0:T(8,128)(2,1)S(1)} %add_convert_fusion.4), channel_id=1, source_target_pairs={{0,1},{1,2},{2,3},{3,4},{4,5},{5,6},{6,7},{7,0},{8,9},{9,10},{10,1... | collective-permute-start | bytes 1572872 | tf_op jit(solution)/shard_map/ppermute | solution.py:269
  118.9 1.6 collective-permute-start.34
  121.1 10.9 %collective-permute-done.34 = bf16[64,512]{1,0:T(8,128)(2,1)S(1)} collective-permute-done((bf16[64,512]{1,0:T(8,128)(2,1)S(1)}, bf16[64,512]{1,0:T(8,128)(2,1)S(1)}, u32[]{:S(2)}, u32[]{:S(2)}) %collective-permute-start.34) | collective-permute-done | bytes 65568 | tf_op jit(solution)/shard_map/ppermute | solution.py:269
  131.9 1.7 collective-permute-done.30
  134.4 2.7 %collective-permute-start.35 = (bf16[128,512]{1,0:T(8,128)(2,1)S(1)}, bf16[128,512]{1,0:T(8,128)(2,1)S(1)}, u32[]{:S(2)}, u32[]{:S(2)}) collective-permute-start(bf16[128,512]{1,0:T(8,128)(2,1)S(1)} %pad_maximum_fusion.7), channel_id=1, source_target_pairs={{0,7},{1,0},{2,1},{3,2},{4,3},{5,4},{6,5},{7,6},{8,15},{9,8},{10,9... | collective-permute-start | bytes 393224 | tf_op jit(solution)/shard_map/ppermute | solution.py:269
  137.1 3.9 %collective-permute-done.31 = bf16[128,512]{1,0:T(8,128)(2,1)S(1)} collective-permute-done((bf16[128,512]{1,0:T(8,128)(2,1)S(1)}, bf16[128,512]{1,0:T(8,128)(2,1)S(1)}, u32[]{:S(2)}, u32[]{:S(2)}) %collective-permute-start.31) | collective-permute-done | bytes 131104 | tf_op jit(solution)/shard_map/ppermute | solution.py:269
  141.1 3.1 %collective-permute-start.36 = (bf16[128,512]{1,0:T(8,128)(2,1)S(1)}, bf16[128,512]{1,0:T(8,128)(2,1)S(1)}, u32[]{:S(2)}, u32[]{:S(2)}) collective-permute-start(bf16[128,512]{1,0:T(8,128)(2,1)S(1)} %get-tuple-element.37), channel_id=1, source_target_pairs={{0,7},{1,0},{2,1},{3,2},{4,3},{5,4},{6,5},{7,6},{8,15},{9,8},{10,9... | collective-permute-start | bytes 393224 | tf_op jit(solution)/shard_map/ppermute | solution.py:269
  144.4 2.9 %collective-permute-start.24 = (bf16[64,512]{1,0:T(8,128)(2,1)S(1)}, bf16[64,512]{1,0:T(8,128)(2,1)S(1)}, u32[]{:S(2)}, u32[]{:S(2)}) collective-permute-start(bf16[64,512]{1,0:T(8,128)(2,1)S(1)} %get-tuple-element.46), channel_id=1, source_target_pairs={{0,24},{1,25},{2,26},{3,27},{4,28},{5,29},{6,30},{7,31},{8,0},{9,1... | collective-permute-start | bytes 196616 | tf_op jit(solution)/shard_map/ppermute | solution.py:274
  147.3 1.9 %collective-permute-done.24 = bf16[64,512]{1,0:T(8,128)(2,1)S(1)} collective-permute-done((bf16[64,512]{1,0:T(8,128)(2,1)S(1)}, bf16[64,512]{1,0:T(8,128)(2,1)S(1)}, u32[]{:S(2)}, u32[]{:S(2)}) %collective-permute-start.24) | collective-permute-done | bytes 65568 | tf_op jit(solution)/shard_map/ppermute | solution.py:274
  149.2 4.3 %collective-permute-done.22 = bf16[64,512]{1,0:T(8,128)(2,1)S(1)} collective-permute-done((bf16[64,512]{1,0:T(8,128)(2,1)S(1)}, bf16[64,512]{1,0:T(8,128)(2,1)S(1)}, u32[]{:S(2)}, u32[]{:S(2)}) %collective-permute-start.22) | collective-permute-done | bytes 65568 | tf_op jit(solution)/shard_map/ppermute | solution.py:274
  153.6 3.3 %collective-permute-start.25 = (bf16[128,512]{1,0:T(8,128)(2,1)S(1)}, bf16[128,512]{1,0:T(8,128)(2,1)S(1)}, u32[]{:S(2)}, u32[]{:S(2)}) collective-permute-start(bf16[128,512]{1,0:T(8,128)(2,1)S(1)} %pad_maximum_fusion.5), channel_id=1, source_target_pairs={{0,24},{1,25},{2,26},{3,27},{4,28},{5,29},{6,30},{7,31},{8,0},{9,1... | collective-permute-start | bytes 393224 | tf_op jit(solution)/shard_map/ppermute | solution.py:274
  157.1 3.3 %collective-permute-start.37 = (bf16[128,512]{1,0:T(8,128)(2,1)S(1)}, bf16[128,512]{1,0:T(8,128)(2,1)S(1)}, u32[]{:S(2)}, u32[]{:S(2)}) collective-permute-start(bf16[128,512]{1,0:T(8,128)(2,1)S(1)} %get-tuple-element.35), channel_id=1, source_target_pairs={{0,7},{1,0},{2,1},{3,2},{4,3},{5,4},{6,5},{7,6},{8,15},{9,8},{10,9... | collective-permute-start | bytes 393224 | tf_op jit(solution)/shard_map/ppermute | solution.py:269
  160.4 2.5 %collective-permute-done.37.refs_9_ = bf16[128,512]{1,0:T(8,128)(2,1)S(1)} collective-permute-done((bf16[128,512]{1,0:T(8,128)(2,1)S(1)}, bf16[128,512]{1,0:T(8,128)(2,1)S(1)}, u32[]{:S(2)}, u32[]{:S(2)}) %collective-permute-start.37) | collective-permute-done | bytes 131104 | tf_op jit(solution)/shard_map/ppermute | solution.py:269
  162.9 3.7 %collective-permute-done.33.refs_8_ = bf16[128,512]{1,0:T(8,128)(2,1)S(1)} collective-permute-done((bf16[128,512]{1,0:T(8,128)(2,1)S(1)}, bf16[128,512]{1,0:T(8,128)(2,1)S(1)}, u32[]{:S(2)}, u32[]{:S(2)}) %collective-permute-start.33) | collective-permute-done | bytes 131104 | tf_op jit(solution)/shard_map/ppermute | solution.py:269
  166.6 1.3 finish.1
  (105 shorter events, 10.9 us)
Async XLA Ops:
  0.0 1.0 copy-start.4
  1.4 39.4 %collective-permute-start.13 = (bf16[512,512]{1,0:T(8,128)(2,1)S(1)}, bf16[512,512]{1,0:T(8,128)(2,1)S(1)}, u32[]{:S(2)}, u32[]{:S(2)}) collective-permute-start(bf16[512,512]{1,0:T(8,128)(2,1)S(1)} %norm.1.refs_1_.refs_0_), channel_id=1, source_target_pairs={{0,32},{32,0},{64,96},{96,64},{128,160},{160,128},{192,224},{224,1... | collective-permute-start | bytes 1572872 | tf_op jit(solution)/shard_map/ppermute | solution.py:264
  1.5 31.2 %collective-permute-start.7 = (bf16[512,512]{1,0:T(8,128)(2,1)S(1)}, bf16[512,512]{1,0:T(8,128)(2,1)S(1)}, u32[]{:S(2)}, u32[]{:S(2)}) collective-permute-start(bf16[512,512]{1,0:T(8,128)(2,1)S(1)} %norm.1.refs_1_.refs_0_), channel_id=1, source_target_pairs={{0,64},{32,96},{64,128},{96,160},{128,192},{160,224},{192,0},{224,... | collective-permute-start | bytes 1572872 | tf_op jit(solution)/shard_map/ppermute | solution.py:259
  3.0 31.2 %collective-permute-start.5 = (bf16[512,512]{1,0:T(8,128)(2,1)S(1)}, bf16[512,512]{1,0:T(8,128)(2,1)S(1)}, u32[]{:S(2)}, u32[]{:S(2)}) collective-permute-start(bf16[512,512]{1,0:T(8,128)(2,1)S(1)} %norm.1.refs_1_.refs_0_), channel_id=1, source_target_pairs={{0,192},{32,224},{64,0},{96,32},{128,64},{160,96},{192,128},{224,1... | collective-permute-start | bytes 1572872 | tf_op jit(solution)/shard_map/ppermute | solution.py:259
  3.9 7.9 %collective-permute-start = (s32[256]{0:T(256)}, s32[256]{0:T(256)S(1)}, u32[]{:S(2)}, u32[]{:S(2)}) collective-permute-start(s32[256]{0:T(256)} %param.11), channel_id=1, source_target_pairs={{0,7},{1,0},{2,1},{3,2},{4,3},{5,4},{6,5},{7,6},{8,15},{9,8},{10,9... | collective-permute-start | bytes 3080 | tf_op jit(solution)/shard_map/ppermute | solution.py:269
  12.4 4.5 %collective-permute-start.1 = (s32[512]{0:T(512)S(1)}, s32[512]{0:T(512)S(1)}, u32[]{:S(2)}, u32[]{:S(2)}) collective-permute-start(s32[512]{0:T(512)S(1)} %pad_add_fusion.2), channel_id=1, source_target_pairs={{0,6},{1,7},{2,0},{3,1},{4,2},{5,3},{6,4},{7,5},{8,14},{9,15},{10,... | collective-permute-start | bytes 6152 | tf_op jit(solution)/shard_map/ppermute | solution.py:269
  17.6 7.5 %collective-permute-start.2 = (s32[1024]{0:T(1024)S(1)}, s32[1024]{0:T(1024)S(1)}, u32[]{:S(2)}, u32[]{:S(2)}) collective-permute-start(s32[1024]{0:T(1024)S(1)} %pad_add_fusion.1), channel_id=1, source_target_pairs={{0,4},{1,5},{2,6},{3,7},{4,0},{5,1},{6,2},{7,3},{8,12},{9,13},{10,... | collective-permute-start | bytes 12296 | tf_op jit(solution)/shard_map/ppermute | solution.py:269
  25.8 4.4 %collective-permute-start.3 = (s32[2048]{0:T(1024)S(1)}, s32[2048]{0:T(1024)S(1)}, u32[]{:S(2)}, u32[]{:S(2)}) collective-permute-start(s32[2048]{0:T(1024)S(1)} %pad_add_fusion), channel_id=1, source_target_pairs={{0,24},{1,25},{2,26},{3,27},{4,28},{5,29},{6,30},{7,31},{8,0},{9,1... | collective-permute-start | bytes 24584 | tf_op jit(solution)/shard_map/ppermute | solution.py:274
  30.2 5.2 %collective-permute-start.4 = (s32[4096]{0:T(1024)S(1)}, s32[4096]{0:T(1024)S(1)}, u32[]{:S(2)}, u32[]{:S(2)}) collective-permute-start(s32[4096]{0:T(1024)S(1)} %get-tuple-element.51), channel_id=1, source_target_pairs={{0,16},{1,17},{2,18},{3,19},{4,20},{5,21},{6,22},{7,23},{8,24},{9,... | collective-permute-start | bytes 49160 | tf_op jit(solution)/shard_map/ppermute | solution.py:274
  32.7 6.4 %collective-permute-start.8 = (bf16[256,512]{1,0:T(8,128)(2,1)S(1)}, bf16[256,512]{1,0:T(8,128)(2,1)S(1)}, u32[]{:S(2)}, u32[]{:S(2)}) collective-permute-start(bf16[256,512]{1,0:T(8,128)(2,1)S(1)} %slice.257), channel_id=1, source_target_pairs={{0,64},{32,96},{64,128},{96,160},{128,192},{160,224},{192,0},{224,... | collective-permute-start | bytes 786440 | tf_op jit(solution)/shard_map/ppermute | solution.py:259
  34.3 6.4 %collective-permute-start.6 = (bf16[256,512]{1,0:T(8,128)(2,1)S(1)}, bf16[256,512]{1,0:T(8,128)(2,1)S(1)}, u32[]{:S(2)}, u32[]{:S(2)}) collective-permute-start(bf16[256,512]{1,0:T(8,128)(2,1)S(1)} %slice.256), channel_id=1, source_target_pairs={{0,192},{32,224},{64,0},{96,32},{128,64},{160,96},{192,128},{224,1... | collective-permute-start | bytes 786440 | tf_op jit(solution)/shard_map/ppermute | solution.py:259
  34.9 8.7 %collective-permute-start.12 = (bf16[512,512]{1,0:T(8,128)(2,1)S(1)}, bf16[512,512]{1,0:T(8,128)(2,1)S(1)}, u32[]{:S(2)}, u32[]{:S(2)}) collective-permute-start(bf16[512,512]{1,0:T(8,128)(2,1)S(1)} %collective-permute-done.5.refs_1_.refs_2_), channel_id=1, source_target_pairs={{0,32},{32,0},{64,96},{96,64},{128,160},{160,128},{192,224},{224,1... | collective-permute-start | bytes 1572872 | tf_op jit(solution)/shard_map/ppermute | solution.py:264
  35.4 9.6 %collective-permute-start.11 = (bf16[512,512]{1,0:T(8,128)(2,1)S(1)}, bf16[512,512]{1,0:T(8,128)(2,1)S(1)}, u32[]{:S(2)}, u32[]{:S(2)}) collective-permute-start(bf16[512,512]{1,0:T(8,128)(2,1)S(1)} %collective-permute-done.7.refs_1_.refs_8_), channel_id=1, source_target_pairs={{0,32},{32,0},{64,96},{96,64},{128,160},{160,128},{192,224},{224,1... | collective-permute-start | bytes 1572872 | tf_op jit(solution)/shard_map/ppermute | solution.py:264
  39.1 7.5 %collective-permute-start.10 = (bf16[256,512]{1,0:T(8,128)(2,1)S(1)}, bf16[256,512]{1,0:T(8,128)(2,1)S(1)}, u32[]{:S(2)}, u32[]{:S(2)}) collective-permute-start(bf16[256,512]{1,0:T(8,128)(2,1)S(1)} %collective-permute-done.8.refs_2_.refs_5_), channel_id=1, source_target_pairs={{0,32},{32,0},{64,96},{96,64},{128,160},{160,128},{192,224},{224,1... | collective-permute-start | bytes 786440 | tf_op jit(solution)/shard_map/ppermute | solution.py:264
  40.7 5.9 %collective-permute-start.9 = (bf16[256,512]{1,0:T(8,128)(2,1)S(1)}, bf16[256,512]{1,0:T(8,128)(2,1)S(1)}, u32[]{:S(2)}, u32[]{:S(2)}) collective-permute-start(bf16[256,512]{1,0:T(8,128)(2,1)S(1)} %collective-permute-done.6.refs_1_.refs_4_), channel_id=1, source_target_pairs={{0,32},{32,0},{64,96},{96,64},{128,160},{160,128},{192,224},{224,1... | collective-permute-start | bytes 786440 | tf_op jit(solution)/shard_map/ppermute | solution.py:264
  40.8 1.2 copy-start
  46.6 1.6 copy-start.2
  46.6 2.2 %copy-start.3 = (bf16[2048,512]{1,0:T(8,128)(2,1)S(1)}, bf16[2048,512]{1,0:T(8,128)(2,1)}, u32[]{:S(2)}) copy-start(bf16[2048,512]{1,0:T(8,128)(2,1)} %v_ref.5) | copy-start | bytes 6291460
  46.6 2.2 %copy-start.8 = (s32[24]{0:T(128)S(1)}, s32[24]{0:T(128)}, u32[]{:S(2)}) copy-start(s32[24]{0:T(128)} %constant.126.clone.order_ref) | copy-start | bytes 292
  48.8 13.1 %copy-start.7 = (s32[48]{0:T(128)S(1)}, s32[48]{0:T(128)}, u32[]{:S(2)}) copy-start(s32[48]{0:T(128)} %constant.127.clone.order_ref) | copy-start | bytes 580
  53.5 17.2 %copy-start.6 = (s32[56]{0:T(128)S(1)}, s32[56]{0:T(128)}, u32[]{:S(2)}) copy-start(s32[56]{0:T(128)} %constant.128.clone.order_ref) | copy-start | bytes 676
  53.5 34.7 %collective-permute-start.14 = (bf16[2,128,512]{2,1,0:T(8,128)(2,1)S(1)}, bf16[2,128,512]{2,1,0:T(8,128)(2,1)S(1)}, u32[]{:S(2)}, u32[]{:S(2)}) collective-permute-start(bf16[2,128,512]{2,1,0:T(8,128)(2,1)S(1)} %get-tuple-element.20), channel_id=1, source_target_pairs={{0,1},{1,2},{2,3},{3,4},{4,5},{5,6},{6,7},{7,0},{8,9},{9,10},{10,1... | collective-permute-start | bytes 786440 | tf_op jit(solution)/shard_map/ppermute | solution.py:269
  55.3 31.9 %collective-permute-start.18 = (bf16[2,128,512]{2,1,0:T(8,128)(2,1)S(1)}, bf16[2,128,512]{2,1,0:T(8,128)(2,1)S(1)}, u32[]{:S(2)}, u32[]{:S(2)}) collective-permute-start(bf16[2,128,512]{2,1,0:T(8,128)(2,1)S(1)} %get-tuple-element.25), channel_id=1, source_target_pairs={{0,7},{1,0},{2,1},{3,2},{4,3},{5,4},{6,5},{7,6},{8,15},{9,8},{10,9... | collective-permute-start | bytes 786440 | tf_op jit(solution)/shard_map/ppermute | solution.py:269
  58.3 34.0 %collective-permute-start.26 = (bf16[4,128,512]{2,1,0:T(8,128)(2,1)S(1)}, bf16[4,128,512]{2,1,0:T(8,128)(2,1)S(1)}, u32[]{:S(2)}, u32[]{:S(2)}) collective-permute-start(bf16[4,128,512]{2,1,0:T(8,128)(2,1)S(1)} %get-tuple-element.29), channel_id=1, source_target_pairs={{0,8},{1,9},{2,10},{3,11},{4,12},{5,13},{6,14},{7,15},{8,16},{9,17... | collective-permute-start | bytes 1572872 | tf_op jit(solution)/shard_map/ppermute | solution.py:274
  62.0 27.7 %collective-permute-start.28 = (bf16[4,128,512]{2,1,0:T(8,128)(2,1)S(1)}, bf16[4,128,512]{2,1,0:T(8,128)(2,1)S(1)}, u32[]{:S(2)}, u32[]{:S(2)}) collective-permute-start(bf16[4,128,512]{2,1,0:T(8,128)(2,1)S(1)} %get-tuple-element.32), channel_id=1, source_target_pairs={{0,24},{1,25},{2,26},{3,27},{4,28},{5,29},{6,30},{7,31},{8,0},{9,1... | collective-permute-start | bytes 1572872 | tf_op jit(solution)/shard_map/ppermute | solution.py:274
  87.2 16.9 %copy-start.1 = (bf16[512,1024]{1,0:T(8,128)(2,1)S(1)}, bf16[512,1024]{1,0:T(8,128)(2,1)}, u32[]{:S(2)}) copy-start(bf16[512,1024]{1,0:T(8,128)(2,1)} %w_ref.1) | copy-start | bytes 3145732
  87.3 14.0 %collective-permute-start.19 = (bf16[4,128,512]{2,1,0:T(8,128)(2,1)S(1)}, bf16[4,128,512]{2,1,0:T(8,128)(2,1)S(1)}, u32[]{:S(2)}, u32[]{:S(2)}) collective-permute-start(bf16[4,128,512]{2,1,0:T(8,128)(2,1)S(1)} %pad_maximum_fusion.3), channel_id=1, source_target_pairs={{0,7},{1,0},{2,1},{3,2},{4,3},{5,4},{6,5},{7,6},{8,15},{9,8},{10,9... | collective-permute-start | bytes 1572872 | tf_op jit(solution)/shard_map/ppermute | solution.py:269
  88.3 13.6 %collective-permute-start.15 = (bf16[4,128,512]{2,1,0:T(8,128)(2,1)S(1)}, bf16[4,128,512]{2,1,0:T(8,128)(2,1)S(1)}, u32[]{:S(2)}, u32[]{:S(2)}) collective-permute-start(bf16[4,128,512]{2,1,0:T(8,128)(2,1)S(1)} %pad_maximum_fusion.2), channel_id=1, source_target_pairs={{0,1},{1,2},{2,3},{3,4},{4,5},{5,6},{6,7},{7,0},{8,9},{9,10},{10,1... | collective-permute-start | bytes 1572872 | tf_op jit(solution)/shard_map/ppermute | solution.py:269
  89.9 28.9 %collective-permute-start.29 = (bf16[8,128,512]{2,1,0:T(8,128)(2,1)S(1)}, bf16[8,128,512]{2,1,0:T(8,128)(2,1)S(1)}, u32[]{:S(2)}, u32[]{:S(2)}) collective-permute-start(bf16[8,128,512]{2,1,0:T(8,128)(2,1)S(1)} %pad_maximum_fusion.1), channel_id=1, source_target_pairs={{0,24},{1,25},{2,26},{3,27},{4,28},{5,29},{6,30},{7,31},{8,0},{9,1... | collective-permute-start | bytes 3145736 | tf_op jit(solution)/shard_map/ppermute | solution.py:274
  92.5 26.3 %collective-permute-start.27 = (bf16[8,128,512]{2,1,0:T(8,128)(2,1)S(1)}, bf16[8,128,512]{2,1,0:T(8,128)(2,1)S(1)}, u32[]{:S(2)}, u32[]{:S(2)}) collective-permute-start(bf16[8,128,512]{2,1,0:T(8,128)(2,1)S(1)} %pad_maximum_fusion), channel_id=1, source_target_pairs={{0,8},{1,9},{2,10},{3,11},{4,12},{5,13},{6,14},{7,15},{8,16},{9,17... | collective-permute-start | bytes 3145736 | tf_op jit(solution)/shard_map/ppermute | solution.py:274
  101.5 14.9 %collective-permute-start.20 = (bf16[4,128,512]{2,1,0:T(8,128)(2,1)S(1)}, bf16[4,128,512]{2,1,0:T(8,128)(2,1)S(1)}, u32[]{:S(2)}, u32[]{:S(2)}) collective-permute-start(bf16[4,128,512]{2,1,0:T(8,128)(2,1)S(1)} %add_convert_fusion.3), channel_id=1, source_target_pairs={{0,7},{1,0},{2,1},{3,2},{4,3},{5,4},{6,5},{7,6},{8,15},{9,8},{10,9... | collective-permute-start | bytes 1572872 | tf_op jit(solution)/shard_map/ppermute | solution.py:269
  102.1 14.7 %collective-permute-start.16 = (bf16[4,128,512]{2,1,0:T(8,128)(2,1)S(1)}, bf16[4,128,512]{2,1,0:T(8,128)(2,1)S(1)}, u32[]{:S(2)}, u32[]{:S(2)}) collective-permute-start(bf16[4,128,512]{2,1,0:T(8,128)(2,1)S(1)} %add_convert_fusion.5), channel_id=1, source_target_pairs={{0,1},{1,2},{2,3},{3,4},{4,5},{5,6},{6,7},{7,0},{8,9},{9,10},{10,1... | collective-permute-start | bytes 1572872 | tf_op jit(solution)/shard_map/ppermute | solution.py:269
  104.0 62.5 %copy-start.5 = (bf16[512,512]{1,0:T(8,128)(2,1)S(1)}, bf16[512,512]{1,0:T(8,128)(2,1)}, u32[]{:S(2)}) copy-start(bf16[512,512]{1,0:T(8,128)(2,1)} %refs_11_.1) | copy-start | bytes 1572868
  116.5 27.8 %collective-permute-start.21 = (bf16[4,128,512]{2,1,0:T(8,128)(2,1)S(1)}, bf16[4,128,512]{2,1,0:T(8,128)(2,1)S(1)}, u32[]{:S(2)}, u32[]{:S(2)}) collective-permute-start(bf16[4,128,512]{2,1,0:T(8,128)(2,1)S(1)} %add_convert_fusion.2), channel_id=1, source_target_pairs={{0,7},{1,0},{2,1},{3,2},{4,3},{5,4},{6,5},{7,6},{8,15},{9,8},{10,9... | collective-permute-start | bytes 1572872 | tf_op jit(solution)/shard_map/ppermute | solution.py:269
  116.9 27.4 %collective-permute-start.17 = (bf16[4,128,512]{2,1,0:T(8,128)(2,1)S(1)}, bf16[4,128,512]{2,1,0:T(8,128)(2,1)S(1)}, u32[]{:S(2)}, u32[]{:S(2)}) collective-permute-start(bf16[4,128,512]{2,1,0:T(8,128)(2,1)S(1)} %add_convert_fusion.4), channel_id=1, source_target_pairs={{0,1},{1,2},{2,3},{3,4},{4,5},{5,6},{6,7},{7,0},{8,9},{9,10},{10,1... | collective-permute-start | bytes 1572872 | tf_op jit(solution)/shard_map/ppermute | solution.py:269
  118.9 13.0 %collective-permute-start.34 = (bf16[64,512]{1,0:T(8,128)(2,1)S(1)}, bf16[64,512]{1,0:T(8,128)(2,1)S(1)}, u32[]{:S(2)}, u32[]{:S(2)}) collective-permute-start(bf16[64,512]{1,0:T(8,128)(2,1)S(1)} %get-tuple-element.40), channel_id=1, source_target_pairs={{0,7},{1,0},{2,1},{3,2},{4,3},{5,4},{6,5},{7,6},{8,15},{9,8},{10,9... | collective-permute-start | bytes 196616 | tf_op jit(solution)/shard_map/ppermute | solution.py:269
  120.6 13.0 %collective-permute-start.30 = (bf16[64,512]{1,0:T(8,128)(2,1)S(1)}, bf16[64,512]{1,0:T(8,128)(2,1)S(1)}, u32[]{:S(2)}, u32[]{:S(2)}) collective-permute-start(bf16[64,512]{1,0:T(8,128)(2,1)S(1)} %get-tuple-element.42), channel_id=1, source_target_pairs={{0,1},{1,2},{2,3},{3,4},{4,5},{5,6},{6,7},{7,0},{8,9},{9,10},{10,1... | collective-permute-start | bytes 196616 | tf_op jit(solution)/shard_map/ppermute | solution.py:269
  133.7 7.3 %collective-permute-start.31 = (bf16[128,512]{1,0:T(8,128)(2,1)S(1)}, bf16[128,512]{1,0:T(8,128)(2,1)S(1)}, u32[]{:S(2)}, u32[]{:S(2)}) collective-permute-start(bf16[128,512]{1,0:T(8,128)(2,1)S(1)} %pad_maximum_fusion.6), channel_id=1, source_target_pairs={{0,1},{1,2},{2,3},{3,4},{4,5},{5,6},{6,7},{7,0},{8,9},{9,10},{10,1... | collective-permute-start | bytes 393224 | tf_op jit(solution)/shard_map/ppermute | solution.py:269
  134.4 6.6 %collective-permute-start.35 = (bf16[128,512]{1,0:T(8,128)(2,1)S(1)}, bf16[128,512]{1,0:T(8,128)(2,1)S(1)}, u32[]{:S(2)}, u32[]{:S(2)}) collective-permute-start(bf16[128,512]{1,0:T(8,128)(2,1)S(1)} %pad_maximum_fusion.7), channel_id=1, source_target_pairs={{0,7},{1,0},{2,1},{3,2},{4,3},{5,4},{6,5},{7,6},{8,15},{9,8},{10,9... | collective-permute-start | bytes 393224 | tf_op jit(solution)/shard_map/ppermute | solution.py:269
  141.1 15.8 %collective-permute-start.36 = (bf16[128,512]{1,0:T(8,128)(2,1)S(1)}, bf16[128,512]{1,0:T(8,128)(2,1)S(1)}, u32[]{:S(2)}, u32[]{:S(2)}) collective-permute-start(bf16[128,512]{1,0:T(8,128)(2,1)S(1)} %get-tuple-element.37), channel_id=1, source_target_pairs={{0,7},{1,0},{2,1},{3,2},{4,3},{5,4},{6,5},{7,6},{8,15},{9,8},{10,9... | collective-permute-start | bytes 393224 | tf_op jit(solution)/shard_map/ppermute | solution.py:269
  144.2 12.7 %collective-permute-start.32 = (bf16[128,512]{1,0:T(8,128)(2,1)S(1)}, bf16[128,512]{1,0:T(8,128)(2,1)S(1)}, u32[]{:S(2)}, u32[]{:S(2)}) collective-permute-start(bf16[128,512]{1,0:T(8,128)(2,1)S(1)} %get-tuple-element.38), channel_id=1, source_target_pairs={{0,1},{1,2},{2,3},{3,4},{4,5},{5,6},{6,7},{7,0},{8,9},{9,10},{10,1... | collective-permute-start | bytes 393224 | tf_op jit(solution)/shard_map/ppermute | solution.py:269
  144.4 4.8 %collective-permute-start.24 = (bf16[64,512]{1,0:T(8,128)(2,1)S(1)}, bf16[64,512]{1,0:T(8,128)(2,1)S(1)}, u32[]{:S(2)}, u32[]{:S(2)}) collective-permute-start(bf16[64,512]{1,0:T(8,128)(2,1)S(1)} %get-tuple-element.46), channel_id=1, source_target_pairs={{0,24},{1,25},{2,26},{3,27},{4,28},{5,29},{6,30},{7,31},{8,0},{9,1... | collective-permute-start | bytes 196616 | tf_op jit(solution)/shard_map/ppermute | solution.py:274
  147.2 6.2 %collective-permute-start.22 = (bf16[64,512]{1,0:T(8,128)(2,1)S(1)}, bf16[64,512]{1,0:T(8,128)(2,1)S(1)}, u32[]{:S(2)}, u32[]{:S(2)}) collective-permute-start(bf16[64,512]{1,0:T(8,128)(2,1)S(1)} %get-tuple-element.48), channel_id=1, source_target_pairs={{0,8},{1,9},{2,10},{3,11},{4,12},{5,13},{6,14},{7,15},{8,16},{9,17... | collective-permute-start | bytes 196616 | tf_op jit(solution)/shard_map/ppermute | solution.py:274
  153.5 6.9 %collective-permute-start.23 = (bf16[128,512]{1,0:T(8,128)(2,1)S(1)}, bf16[128,512]{1,0:T(8,128)(2,1)S(1)}, u32[]{:S(2)}, u32[]{:S(2)}) collective-permute-start(bf16[128,512]{1,0:T(8,128)(2,1)S(1)} %pad_maximum_fusion.4), channel_id=1, source_target_pairs={{0,8},{1,9},{2,10},{3,11},{4,12},{5,13},{6,14},{7,15},{8,16},{9,17... | collective-permute-start | bytes 393224 | tf_op jit(solution)/shard_map/ppermute | solution.py:274
  153.6 6.8 %collective-permute-start.25 = (bf16[128,512]{1,0:T(8,128)(2,1)S(1)}, bf16[128,512]{1,0:T(8,128)(2,1)S(1)}, u32[]{:S(2)}, u32[]{:S(2)}) collective-permute-start(bf16[128,512]{1,0:T(8,128)(2,1)S(1)} %pad_maximum_fusion.5), channel_id=1, source_target_pairs={{0,24},{1,25},{2,26},{3,27},{4,28},{5,29},{6,30},{7,31},{8,0},{9,1... | collective-permute-start | bytes 393224 | tf_op jit(solution)/shard_map/ppermute | solution.py:274
  157.1 5.8 %collective-permute-start.37 = (bf16[128,512]{1,0:T(8,128)(2,1)S(1)}, bf16[128,512]{1,0:T(8,128)(2,1)S(1)}, u32[]{:S(2)}, u32[]{:S(2)}) collective-permute-start(bf16[128,512]{1,0:T(8,128)(2,1)S(1)} %get-tuple-element.35), channel_id=1, source_target_pairs={{0,7},{1,0},{2,1},{3,2},{4,3},{5,4},{6,5},{7,6},{8,15},{9,8},{10,9... | collective-permute-start | bytes 393224 | tf_op jit(solution)/shard_map/ppermute | solution.py:269
  160.4 6.2 %collective-permute-start.33 = (bf16[128,512]{1,0:T(8,128)(2,1)S(1)}, bf16[128,512]{1,0:T(8,128)(2,1)S(1)}, u32[]{:S(2)}, u32[]{:S(2)}) collective-permute-start(bf16[128,512]{1,0:T(8,128)(2,1)S(1)} %get-tuple-element.36), channel_id=1, source_target_pairs={{0,1},{1,2},{2,3},{3,4},{4,5},{5,6},{6,7},{7,0},{8,9},{9,10},{10,1... | collective-permute-start | bytes 393224 | tf_op jit(solution)/shard_map/ppermute | solution.py:269
where the time goes:
time: 168 us
  waiting for transfers between devices  62.6 us (37%)
  starting transfers between devices  56 us (33%)
  Pallas kernels  38.4 us (23%)
  other arithmetic  6.55 us (4%)
  local copies, waits for them, and re-layouts  3.75 us (2%)
    ppermute x19, waiting for transfers between devices, z_shift(): lax.ppermute(value, 'shard', [(y * nz + z, y * nz + (z + k) % nz) for y i...  49.6 us
    ppermute x19, starting transfers between devices, z_shift(): lax.ppermute(value, 'shard', [(y * nz + z, y * nz + (z + k) % nz) for y i...  33.3 us
    pallas_call x3, Pallas kernels, attend(): pl.pallas_call(functools.partial(attend_kernel, tuple(sizes), 16 if rows...  29.7 us
    ppermute x10, starting transfers between devices, y_shift(): lax.ppermute(value, 'shard', [(y * nz + z, (y + k) % NY * nz + z) for y i...  17.9 us
    ppermute x10, waiting for transfers between devices, y_shift(): lax.ppermute(value, 'shard', [(y * nz + z, (y + k) % NY * nz + z) for y i...  7.99 us
    pallas_call x4, Pallas kernels, project(): pl.pallas_call(kernel, out_shape=jax.ShapeDtypeStruct((total * width // L...  5.44 us
    ppermute x4, waiting for transfers between devices, x_shift(): lax.ppermute(value, 'grp', [(x * CORES + c, (x + k) % nx * CORES + c) for...  5.06 us
    ppermute x4, starting transfers between devices, x_shift(): lax.ppermute(value, 'grp', [(x * CORES + c, (x + k) % nx * CORES + c) for...  4.59 us
  transfers between devices with their start and end apart: 38, of which 17 were waited for; matrix products, arithmetic and copies ran while one was open for 4% of the time, Pallas kernels for 19%

commit v1 on v0

--- a/solution.py
+++ b/solution.py
@@ -13,7 +13,7 @@
 LANES = 128
 NY = 4
 CORES = 2
-TILE = 256
+TILE = 128
 
 
 VMEM = pl.BlockSpec(memory_space=pltpu.VMEM)
@@ -31,7 +31,14 @@
 
 
 def norm_kernel(in_ref, out_ref):
-    out_ref[...] = layer_norm(in_ref[...].astype(jnp.float32)).astype(out_ref.dtype)
+    tile = math.gcd(in_ref.shape[0], TILE)
+
+    def step(i, carry):
+        rows = pl.ds(pl.multiple_of(i * tile, tile), tile)
+        out_ref[rows, :] = layer_norm(in_ref[rows, :].astype(jnp.float32)).astype(out_ref.dtype)
+        return carry
+
+    lax.fori_loop(0, in_ref.shape[0] // tile, step, 0)
 
 
 def norm(rows):
@@ -190,7 +197,7 @@
     width = keys.shape[1]
     number = sum(sizes)
     return pl.pallas_call(
-        functools.partial(attend_kernel, tuple(sizes), 16 if rows % 16 == 0 else 8),
+        functools.partial(attend_kernel, tuple(sizes), math.gcd(rows, 32)),
         out_shape=[jax.ShapeDtypeStruct((n, rows, width), jnp.bfloat16) for n in sizes],
         in_specs=[SMEM] * 4 + [VMEM] * 3,
         out_specs=[VMEM] * len(sizes),
@@ -279,14 +286,16 @@
     ahead = x_shift(normed, -1)
     behind = x_shift(normed, 1)
     other = swap(normed)
-    far_top = x_shift(ahead[:half_part], -1)
-    far_bottom = x_shift(behind[half_part:], 1)
-
     wanted = inverse
     step = 1
     while step < nz:
         wanted = jnp.concatenate([wanted, z_shift(wanted, -step)])
         step *= 2
+    wanted, ahead, behind = lax.optimization_barrier((wanted, ahead, behind))
+    far_top = x_shift(ahead[:half_part], -1)
+    far_bottom = x_shift(behind[half_part:], 1)
+    ahead_rows = [ahead, swap(ahead)]
+    behind_rows = [behind, swap(behind)]
     step = 1
     while step < NY:
         wanted = jnp.concatenate([wanted, y_shift(wanted, -step)])
@@ -317,8 +326,6 @@
     chip = CORES * part_rows
     near_rows = [normed, other]
     table = project(None, 0, total_rows, near_rows, w_in, scale)
-    ahead_rows = [ahead, swap(ahead)]
-    behind_rows = [behind, swap(behind)]
     table = project(table, 1 * chip, total_rows, ahead_rows, w_in, scale)
     table = project(table, 3 * chip, total_rows, behind_rows, w_in, scale)
     far_rows = [far_top, far_bottom, swap(far_top), swap(far_bottom)]
@@ -330,8 +337,10 @@
     y_of = lambda dy, dzs=range(nz): [(dy, dz, half) for dz in dzs]
     calls = [
         [z_of(4, (0, 1)), z_of(4, (2, 3)), y_of(2, range(half_z)), y_of(2, range(half_z, nz))],
-        [z_of(3), z_of(5), y_of(1), y_of(3)],
-        [z_of(2), z_of(6), z_of(1), z_of(7), z_of(0), y_of(0)],
+        [z_of(3), z_of(5)],
+        [y_of(1), y_of(3)],
+        [z_of(2), z_of(6)],
+        [z_of(1), z_of(7), z_of(0), y_of(0)],
     ]
     flat = [t for call in calls for piece in call for t in piece]
     order = [v for dy, dz, start in flat for v in (dy * nz + dz, (dy * nz + dz) * cand + start)]
@@ -356,8 +365,10 @@
     y_down = jnp.concatenate([y3[:half_z], add(far_y_down, y3[half_z:])], axis=0)
     y_up = y_shift(y_up, 1)
     y_down = y_shift(y_down, -1)
-    up, down = z_shift(add(up, z2), 1), z_shift(add(down, z6), -1)
-    up, down = z_shift(add(up, z1), 1), z_shift(add(down, z7), -1)
+    up = z_shift(add(up, z2), 1)
+    down = z_shift(add(down, z6), -1)
+    up = z_shift(add(up, z1), 1)
+    down = z_shift(add(down, z7), -1)
 
     quarter = half // 2
 

time: 168 us -> 167 us (level)
  waiting for transfers between devices: 62.6 us -> 52.4 us
  starting transfers between devices: 56 us -> 61.3 us
  Pallas kernels: 38.4 us -> 42.9 us
    ppermute x19, waiting for transfers between devices: 49.6 us -> 42.1 us  [z_shift(): lax.ppermute(value, 'shard', [(y * nz + z, y * nz + (z + k) % nz) for y i...]
    ppermute x19, starting transfers between devices: 33.3 us -> 40.3 us  [z_shift(): lax.ppermute(value, 'shard', [(y * nz + z, y * nz + (z + k) % nz) for y i...]
    ppermute x4, waiting for transfers between devices: 5.06 us -> 0.01 us  [x_shift(): lax.ppermute(value, 'grp', [(x * CORES + c, (x + k) % nx * CORES + c) for...]
    pallas_call x4, Pallas kernels: 5.44 us -> 8.9 us  [project(): pl.pallas_call(kernel, out_shape=jax.ShapeDtypeStruct((total * width // L...]
    ppermute x10, starting transfers between devices: 17.9 us -> 15.3 us  [y_shift(): lax.ppermute(value, 'shard', [(y * nz + z, (y + k) % NY * nz + z) for y i...]
    ppermute x10, waiting for transfers between devices: 7.99 us -> 10.2 us  [y_shift(): lax.ppermute(value, 'shard', [(y * nz + z, (y + k) % NY * nz + z) for y i...]
    unnamed x21 -> x24, local copies, waits for them, and re-layouts: 3.54 us -> 2.41 us
    pallas_call x3 -> x5, Pallas kernels: 29.7 us -> 30.3 us  [attend(): pl.pallas_call(functools.partial(attend_kernel, tuple(sizes), math.gcd(ro...]
  transfers between devices with their start and end apart: 38 -> 38, of which waited for: 17 -> 12; matrix products, arithmetic and copies ran while one was open for 4% -> 4% of each run, Pallas kernels for 19% -> 19%
where the time goes in v1:
time: 167 us; the launch traced here: 166 us
  starting transfers between devices  61.3 us (37%)
  waiting for transfers between devices  52.4 us (31%)
  Pallas kernels  42.9 us (26%)
  other arithmetic  6.55 us (4%)
  local copies, waits for them, and re-layouts  2.62 us (2%)
    ppermute x19, waiting for transfers between devices, z_shift(): lax.ppermute(value, 'shard', [(y * nz + z, y * nz + (z + k) % nz) for y i...  42.1 us
    ppermute x19, starting transfers between devices, z_shift(): lax.ppermute(value, 'shard', [(y * nz + z, y * nz + (z + k) % nz) for y i...  40.3 us
    pallas_call x5, Pallas kernels, attend(): pl.pallas_call(functools.partial(attend_kernel, tuple(sizes), math.gcd(ro...  30.3 us
    ppermute x10, starting transfers between devices, y_shift(): lax.ppermute(value, 'shard', [(y * nz + z, (y + k) % NY * nz + z) for y i...  15.3 us
    ppermute x10, waiting for transfers between devices, y_shift(): lax.ppermute(value, 'shard', [(y * nz + z, (y + k) % NY * nz + z) for y i...  10.2 us
    pallas_call x4, Pallas kernels, project(): pl.pallas_call(kernel, out_shape=jax.ShapeDtypeStruct((total * width // L...  8.9 us
    ppermute x4, starting transfers between devices, x_shift(): lax.ppermute(value, 'grp', [(x * CORES + c, (x + k) % nx * CORES + c) for...  4.44 us
  transfers between devices with their start and end apart: 38, of which 12 were waited for; matrix products, arithmetic and copies ran while one was open for 4% of the time, Pallas kernels for 19%

profile of v1, /device:TPU:2, one launch (start us, length us, event | category | flops | bytes accessed | tf_op | source)
XLA Modules:
  0.0 166.4 jit_solution(13307513212876261516)
XLA Ops:
  0.0 1.1 copy-done.4
  1.1 0.8 norm.1.refs_1_.refs_0_
  2.0 1.6 collective-permute-start.4
  3.6 0.8 collective-permute-start.3
  4.5 5.5 %collective-permute-start = (s32[256]{0:T(256)}, s32[256]{0:T(256)S(1)}, u32[]{:S(2)}, u32[]{:S(2)}) collective-permute-start(s32[256]{0:T(256)} %param.13), channel_id=1, source_target_pairs={{0,7},{1,0},{2,1},{3,2},{4,3},{5,4},{6,5},{7,6},{8,15},{9,8},{10,9... | collective-permute-start | bytes 3080 | tf_op jit(solution)/shard_map/ppermute | solution.py:276
  10.0 0.9 convert_reduce_fusion
  13.0 1.9 %collective-permute-start.1 = (s32[512]{0:T(512)S(1)}, s32[512]{0:T(512)S(1)}, u32[]{:S(2)}, u32[]{:S(2)}) collective-permute-start(s32[512]{0:T(512)S(1)} %pad_add_fusion.3), channel_id=1, source_target_pairs={{0,6},{1,7},{2,0},{3,1},{4,2},{5,3},{6,4},{7,5},{8,14},{9,15},{10,... | collective-permute-start | bytes 6152 | tf_op jit(solution)/shard_map/ppermute | solution.py:276
  15.0 2.5 %collective-permute-done.1 = s32[512]{0:T(512)S(1)} collective-permute-done((s32[512]{0:T(512)S(1)}, s32[512]{0:T(512)S(1)}, u32[]{:S(2)}, u32[]{:S(2)}) %collective-permute-start.1) | collective-permute-done | bytes 2080 | tf_op jit(solution)/shard_map/ppermute | solution.py:276
  18.2 2.8 %collective-permute-start.2 = (s32[1024]{0:T(1024)S(1)}, s32[1024]{0:T(1024)S(1)}, u32[]{:S(2)}, u32[]{:S(2)}) collective-permute-start(s32[1024]{0:T(1024)S(1)} %pad_add_fusion.2), channel_id=1, source_target_pairs={{0,4},{1,5},{2,6},{3,7},{4,0},{5,1},{6,2},{7,3},{8,12},{9,13},{10,... | collective-permute-start | bytes 12296 | tf_op jit(solution)/shard_map/ppermute | solution.py:276
  21.1 4.6 %collective-permute-done.2 = s32[1024]{0:T(1024)S(1)} collective-permute-done((s32[1024]{0:T(1024)S(1)}, s32[1024]{0:T(1024)S(1)}, u32[]{:S(2)}, u32[]{:S(2)}) %collective-permute-start.2) | collective-permute-done | bytes 4128 | tf_op jit(solution)/shard_map/ppermute | solution.py:276
  27.1 3.0 %collective-permute-start.5 = (s32[2048]{0:T(1024)S(1)}, s32[2048]{0:T(1024)S(1)}, u32[]{:S(2)}, u32[]{:S(2)}) collective-permute-start(s32[2048]{0:T(1024)S(1)} %pad_add_fusion.1), channel_id=1, source_target_pairs={{0,24},{1,25},{2,26},{3,27},{4,28},{5,29},{6,30},{7,31},{8,0},{9,1... | collective-permute-start | bytes 24584 | tf_op jit(solution)/shard_map/ppermute | solution.py:281
  30.1 1.5 collective-permute-start.8
  32.2 1.2 copy-done.2
  33.4 2.2 %project.4.refs_3_ = f32[16384,128]{1,0:T(8,128)S(1)} custom-call(bf16[512,1024]{1,0:T(8,128)(2,1)S(1)} %copy-done.2, bf16[512,512]{1,0:T(8,128)(2,1)S(1)} %norm.1.refs_1_.refs_0_, bf16[512,512]{1,0:T(8,128)(2,1)S(1)} %collective-permute-done.13.refs_2_.refs_1_), custom_call_target="tpu_custom_call" | custom-call | flops 536870912 | bytes 3145728 | tf_op jit(solution)/shard_map/project/pallas_call | solution.py:89
  35.6 0.7 collective-permute-start.6
  36.4 4.6 %collective-permute-done.6 = s32[4096]{0:T(1024)S(1)} collective-permute-done((s32[4096]{0:T(1024)S(1)}, s32[4096]{0:T(1024)S(1)}, u32[]{:S(2)}, u32[]{:S(2)}) %collective-permute-start.6) | collective-permute-done | bytes 16416 | tf_op jit(solution)/shard_map/ppermute | solution.py:281
  41.6 2.2 %project.5.refs_3_ = f32[16384,128]{1,0:T(8,128)S(1)} custom-call(bf16[512,1024]{1,0:T(8,128)(2,1)S(1)} %copy-done.3, bf16[512,512]{1,0:T(8,128)(2,1)S(1)} %collective-permute-done.3.refs_1_.refs_2_, bf16[512,512]{1,0:T(8,128)(2,1)S(1)} %collective-permute-done.12.refs_2_.refs_3_, f32[16384,128]{1,0:T(8,128)S(1)} %project.4.refs_3_), custom_call_target="tpu_custom_call", output_to_operand_aliasing={{}: (3, {})} | custom-call | flops 536870912 | bytes 3145728 | tf_op jit(solution)/shard_map/project/pallas_call | solution.py:89
  43.8 2.2 %project.6.refs_5_ = f32[16384,128]{1,0:T(8,128)S(1)} custom-call(bf16[512,1024]{1,0:T(8,128)(2,1)S(1)} %copy-done.3, bf16[512,512]{1,0:T(8,128)(2,1)S(1)} %collective-permute-done.4.refs_1_.refs_8_, bf16[512,512]{1,0:T(8,128)(2,1)S(1)} %collective-permute-done.11.refs_2_.refs_9_, f32[16384,128]{1,0:T(8,128)S(1)} %project.5.refs_3_), custom_call_target="tpu_custom_call", output_to_operand_aliasing={{}: (3, {})} | custom-call | flops 536870912 | bytes 3145728 | tf_op jit(solution)/shard_map/project/pallas_call | solution.py:89
  46.1 2.2 %project.7.table_ref = f32[16384,128]{1,0:T(8,128)S(1)} custom-call(bf16[512,1024]{1,0:T(8,128)(2,1)S(1)} %copy-done.3, bf16[256,512]{1,0:T(8,128)(2,1)S(1)} %collective-permute-done.7.refs_1_.refs_4_, bf16[256,512]{1,0:T(8,128)(2,1)S(1)} %collective-permute-done.8.refs_2_.refs_5_, ...), custom_call_target="tpu_custom_call", output_to_operand_aliasing={{}: (5, {})} | custom-call | flops 536870912 | bytes 3145728 | tf_op jit(solution)/shard_map/project/pallas_call | solution.py:89
  48.4 2.8 %attend.7 = (bf16[4,128,512]{2,1,0:T(8,128)(2,1)S(1)}, bf16[4,128,512]{2,1,0:T(8,128)(2,1)S(1)}) custom-call(s32[8192]{0:T(1024)S(1)} %fusion.24.index_ref, s32[32]{0:T(128)S(1)} %convert_reduce_fusion.1.count_ref, s32[64]{0:T(128)S(1)} %select_reduce_fusion.block_ref, s32[16]{0:T(128)S(1)} %copy-done.10, f32[16384,128]{1,0:T(8,128)S(1)} %project.7.table_ref, ...), custom_call_target="tpu_custom_call" | custom-call | flops 536870912 | bytes 2097152 | tf_op jit(solution)/shard_map/attend/pallas_call | solution.py:199
  51.3 4.6 %attend.6 = (bf16[2,128,512]{2,1,0:T(8,128)(2,1)S(1)}, bf16[2,128,512]{2,1,0:T(8,128)(2,1)S(1)}, bf16[4,128,512]{2,1,0:T(8,128)(2,1)S(1)}, bf16[4,128,512]{2,1,0:T(8,128)(2,1)S(1)}) custom-call(s32[8192]{0:T(1024)S(1)} %fusion.24.index_ref, s32[32]{0:T(128)S(1)} %convert_reduce_fusion.1.count_ref, s32[64]{0:T(128)S(1)} %select_reduce_fusion.block_ref, ...), custom_call_target="tpu_custom_call" | custom-call | flops 805306368 | bytes 3145728 | tf_op jit(solution)/shard_map/attend/pallas_call | solution.py:199
  55.9 1.7 %collective-permute-start.14 = (bf16[2,128,512]{2,1,0:T(8,128)(2,1)S(1)}, bf16[2,128,512]{2,1,0:T(8,128)(2,1)S(1)}, u32[]{:S(2)}, u32[]{:S(2)}) collective-permute-start(bf16[2,128,512]{2,1,0:T(8,128)(2,1)S(1)} %get-tuple-element.26), channel_id=1, source_target_pairs={{0,1},{1,2},{2,3},{3,4},{4,5},{5,6},{6,7},{7,0},{8,9},{9,10},{10,1... | collective-permute-start | bytes 786440 | tf_op jit(solution)/shard_map/ppermute | solution.py:276
  57.6 4.9 %collective-permute-start.18 = (bf16[2,128,512]{2,1,0:T(8,128)(2,1)S(1)}, bf16[2,128,512]{2,1,0:T(8,128)(2,1)S(1)}, u32[]{:S(2)}, u32[]{:S(2)}) collective-permute-start(bf16[2,128,512]{2,1,0:T(8,128)(2,1)S(1)} %get-tuple-element.31), channel_id=1, source_target_pairs={{0,7},{1,0},{2,1},{3,2},{4,3},{5,4},{6,5},{7,6},{8,15},{9,8},{10,9... | collective-permute-start | bytes 786440 | tf_op jit(solution)/shard_map/ppermute | solution.py:276
  62.8 3.0 %collective-permute-start.28 = (bf16[4,128,512]{2,1,0:T(8,128)(2,1)S(1)}, bf16[4,128,512]{2,1,0:T(8,128)(2,1)S(1)}, u32[]{:S(2)}, u32[]{:S(2)}) collective-permute-start(bf16[4,128,512]{2,1,0:T(8,128)(2,1)S(1)} %get-tuple-element.38), channel_id=1, source_target_pairs={{0,24},{1,25},{2,26},{3,27},{4,28},{5,29},{6,30},{7,31},{8,0},{9,1... | collective-permute-start | bytes 1572872 | tf_op jit(solution)/shard_map/ppermute | solution.py:281
  65.8 6.3 %attend.9 = (bf16[8,128,512]{2,1,0:T(8,128)(2,1)S(1)}, bf16[8,128,512]{2,1,0:T(8,128)(2,1)S(1)}) custom-call(s32[8192]{0:T(1024)S(1)} %fusion.24.index_ref, s32[32]{0:T(128)S(1)} %convert_reduce_fusion.1.count_ref, s32[64]{0:T(128)S(1)} %select_reduce_fusion.block_ref, s32[32]{0:T(128)S(1)} %copy-done.8, f32[16384,128]{1,0:T(8,128)S(1)} %project.7.table_ref, ...), custom_call_target="tpu_custom_call" | custom-call | flops 1073741824 | bytes 4194304 | tf_op jit(solution)/shard_map/attend/pallas_call | solution.py:199
  72.3 5.4 %attend.8 = (bf16[4,128,512]{2,1,0:T(8,128)(2,1)S(1)}, bf16[4,128,512]{2,1,0:T(8,128)(2,1)S(1)}) custom-call(s32[8192]{0:T(1024)S(1)} %fusion.24.index_ref, s32[32]{0:T(128)S(1)} %convert_reduce_fusion.1.count_ref, s32[64]{0:T(128)S(1)} %select_reduce_fusion.block_ref, s32[16]{0:T(128)S(1)} %copy-done.7, f32[16384,128]{1,0:T(8,128)S(1)} %project.7.table_ref, ...), custom_call_target="tpu_custom_call" | custom-call | flops 536870912 | bytes 2097152 | tf_op jit(solution)/shard_map/attend/pallas_call | solution.py:199
  77.7 11.1 %attend.5 = (bf16[4,128,512]{2,1,0:T(8,128)(2,1)S(1)}, bf16[4,128,512]{2,1,0:T(8,128)(2,1)S(1)}, bf16[4,128,512]{2,1,0:T(8,128)(2,1)S(1)}, bf16[8,128,512]{2,1,0:T(8,128)(2,1)S(1)}) custom-call(s32[8192]{0:T(1024)S(1)} %fusion.24.index_ref, s32[32]{0:T(128)S(1)} %convert_reduce_fusion.1.count_ref, s32[64]{0:T(128)S(1)} %select_reduce_fusion.block_ref, ...), custom_call_target="tpu_custom_call" | custom-call | flops 1342177280 | bytes 5242880 | tf_op jit(solution)/shard_map/attend/pallas_call | solution.py:199
  89.2 2.1 %collective-permute-start.15 = (bf16[4,128,512]{2,1,0:T(8,128)(2,1)S(1)}, bf16[4,128,512]{2,1,0:T(8,128)(2,1)S(1)}, u32[]{:S(2)}, u32[]{:S(2)}) collective-permute-start(bf16[4,128,512]{2,1,0:T(8,128)(2,1)S(1)} %pad_maximum_fusion.2), channel_id=1, source_target_pairs={{0,1},{1,2},{2,3},{3,4},{4,5},{5,6},{6,7},{7,0},{8,9},{9,10},{10,1... | collective-permute-start | bytes 1572872 | tf_op jit(solution)/shard_map/ppermute | solution.py:276
  91.5 2.4 %collective-permute-start.29 = (bf16[8,128,512]{2,1,0:T(8,128)(2,1)S(1)}, bf16[8,128,512]{2,1,0:T(8,128)(2,1)S(1)}, u32[]{:S(2)}, u32[]{:S(2)}) collective-permute-start(bf16[8,128,512]{2,1,0:T(8,128)(2,1)S(1)} %pad_maximum_fusion.1), channel_id=1, source_target_pairs={{0,24},{1,25},{2,26},{3,27},{4,28},{5,29},{6,30},{7,31},{8,0},{9,1... | collective-permute-start | bytes 3145736 | tf_op jit(solution)/shard_map/ppermute | solution.py:281
  94.2 6.6 %collective-permute-done.19 = bf16[4,128,512]{2,1,0:T(8,128)(2,1)S(1)} collective-permute-done((bf16[4,128,512]{2,1,0:T(8,128)(2,1)S(1)}, bf16[4,128,512]{2,1,0:T(8,128)(2,1)S(1)}, u32[]{:S(2)}, u32[]{:S(2)}) %collective-permute-start.19) | collective-permute-done | bytes 524320 | tf_op jit(solution)/shard_map/ppermute | solution.py:276
  101.0 3.4 %collective-permute-start.20 = (bf16[4,128,512]{2,1,0:T(8,128)(2,1)S(1)}, bf16[4,128,512]{2,1,0:T(8,128)(2,1)S(1)}, u32[]{:S(2)}, u32[]{:S(2)}) collective-permute-start(bf16[4,128,512]{2,1,0:T(8,128)(2,1)S(1)} %add_convert_fusion.3), channel_id=1, source_target_pairs={{0,7},{1,0},{2,1},{3,2},{4,3},{5,4},{6,5},{7,6},{8,15},{9,8},{10,9... | collective-permute-start | bytes 1572872 | tf_op jit(solution)/shard_map/ppermute | solution.py:276
  104.9 1.7 %gate.1.refs_10_ = bf16[256,512]{1,0:T(8,128)(2,1)S(1)} custom-call(s32[1,256]{1,0:T(1,128)S(1)} %bitcast.136, bf16[512,1024]{1,0:T(8,128)(2,1)S(1)} %copy-done.3, bf16[512,512]{1,0:T(8,128)(2,1)S(1)} %norm.1.refs_1_.refs_0_, bf16[512,512]{1,0:T(8,128)(2,1)S(1)} %collective-permute-done.13.refs_2_.refs_1_, ...), custom_call_target="tpu_custom_call" | custom-call | flops 1207959552 | bytes 4194304 | tf_op jit(solution)/shard_map/gate/pallas_call | solution.py:124
  106.6 8.4 %collective-permute-done.20 = bf16[4,128,512]{2,1,0:T(8,128)(2,1)S(1)} collective-permute-done((bf16[4,128,512]{2,1,0:T(8,128)(2,1)S(1)}, bf16[4,128,512]{2,1,0:T(8,128)(2,1)S(1)}, u32[]{:S(2)}, u32[]{:S(2)}) %collective-permute-start.20) | collective-permute-done | bytes 524320 | tf_op jit(solution)/shard_map/ppermute | solution.py:276
  115.1 3.8 %collective-permute-start.21 = (bf16[4,128,512]{2,1,0:T(8,128)(2,1)S(1)}, bf16[4,128,512]{2,1,0:T(8,128)(2,1)S(1)}, u32[]{:S(2)}, u32[]{:S(2)}) collective-permute-start(bf16[4,128,512]{2,1,0:T(8,128)(2,1)S(1)} %add_convert_fusion.2), channel_id=1, source_target_pairs={{0,7},{1,0},{2,1},{3,2},{4,3},{5,4},{6,5},{7,6},{8,15},{9,8},{10,9... | collective-permute-start | bytes 1572872 | tf_op jit(solution)/shard_map/ppermute | solution.py:276
  119.2 3.3 %collective-permute-start.34 = (bf16[64,512]{1,0:T(8,128)(2,1)S(1)}, bf16[64,512]{1,0:T(8,128)(2,1)S(1)}, u32[]{:S(2)}, u32[]{:S(2)}) collective-permute-start(bf16[64,512]{1,0:T(8,128)(2,1)S(1)} %get-tuple-element.46), channel_id=1, source_target_pairs={{0,7},{1,0},{2,1},{3,2},{4,3},{5,4},{6,5},{7,6},{8,15},{9,8},{10,9... | collective-permute-start | bytes 196616 | tf_op jit(solution)/shard_map/ppermute | solution.py:276
  122.5 7.4 %collective-permute-done.34 = bf16[64,512]{1,0:T(8,128)(2,1)S(1)} collective-permute-done((bf16[64,512]{1,0:T(8,128)(2,1)S(1)}, bf16[64,512]{1,0:T(8,128)(2,1)S(1)}, u32[]{:S(2)}, u32[]{:S(2)}) %collective-permute-start.34) | collective-permute-done | bytes 65568 | tf_op jit(solution)/shard_map/ppermute | solution.py:276
  129.9 3.6 %collective-permute-done.30 = bf16[64,512]{1,0:T(8,128)(2,1)S(1)} collective-permute-done((bf16[64,512]{1,0:T(8,128)(2,1)S(1)}, bf16[64,512]{1,0:T(8,128)(2,1)S(1)}, u32[]{:S(2)}, u32[]{:S(2)}) %collective-permute-start.30) | collective-permute-done | bytes 65568 | tf_op jit(solution)/shard_map/ppermute | solution.py:276
  133.8 3.3 %collective-permute-start.35 = (bf16[128,512]{1,0:T(8,128)(2,1)S(1)}, bf16[128,512]{1,0:T(8,128)(2,1)S(1)}, u32[]{:S(2)}, u32[]{:S(2)}) collective-permute-start(bf16[128,512]{1,0:T(8,128)(2,1)S(1)} %pad_maximum_fusion.7), channel_id=1, source_target_pairs={{0,7},{1,0},{2,1},{3,2},{4,3},{5,4},{6,5},{7,6},{8,15},{9,8},{10,9... | collective-permute-start | bytes 393224 | tf_op jit(solution)/shard_map/ppermute | solution.py:276
  137.1 2.8 %collective-permute-done.31 = bf16[128,512]{1,0:T(8,128)(2,1)S(1)} collective-permute-done((bf16[128,512]{1,0:T(8,128)(2,1)S(1)}, bf16[128,512]{1,0:T(8,128)(2,1)S(1)}, u32[]{:S(2)}, u32[]{:S(2)}) %collective-permute-start.31) | collective-permute-done | bytes 131104 | tf_op jit(solution)/shard_map/ppermute | solution.py:276
  140.1 3.6 %collective-permute-start.36 = (bf16[128,512]{1,0:T(8,128)(2,1)S(1)}, bf16[128,512]{1,0:T(8,128)(2,1)S(1)}, u32[]{:S(2)}, u32[]{:S(2)}) collective-permute-start(bf16[128,512]{1,0:T(8,128)(2,1)S(1)} %get-tuple-element.43), channel_id=1, source_target_pairs={{0,7},{1,0},{2,1},{3,2},{4,3},{5,4},{6,5},{7,6},{8,15},{9,8},{10,9... | collective-permute-start | bytes 393224 | tf_op jit(solution)/shard_map/ppermute | solution.py:276
  143.8 2.5 %collective-permute-start.24 = (bf16[64,512]{1,0:T(8,128)(2,1)S(1)}, bf16[64,512]{1,0:T(8,128)(2,1)S(1)}, u32[]{:S(2)}, u32[]{:S(2)}) collective-permute-start(bf16[64,512]{1,0:T(8,128)(2,1)S(1)} %get-tuple-element.52), channel_id=1, source_target_pairs={{0,24},{1,25},{2,26},{3,27},{4,28},{5,29},{6,30},{7,31},{8,0},{9,1... | collective-permute-start | bytes 196616 | tf_op jit(solution)/shard_map/ppermute | solution.py:281
  146.3 1.9 %collective-permute-done.24 = bf16[64,512]{1,0:T(8,128)(2,1)S(1)} collective-permute-done((bf16[64,512]{1,0:T(8,128)(2,1)S(1)}, bf16[64,512]{1,0:T(8,128)(2,1)S(1)}, u32[]{:S(2)}, u32[]{:S(2)}) %collective-permute-start.24) | collective-permute-done | bytes 65568 | tf_op jit(solution)/shard_map/ppermute | solution.py:281
  148.2 3.7 %collective-permute-done.22 = bf16[64,512]{1,0:T(8,128)(2,1)S(1)} collective-permute-done((bf16[64,512]{1,0:T(8,128)(2,1)S(1)}, bf16[64,512]{1,0:T(8,128)(2,1)S(1)}, u32[]{:S(2)}, u32[]{:S(2)}) %collective-permute-start.22) | collective-permute-done | bytes 65568 | tf_op jit(solution)/shard_map/ppermute | solution.py:281
  152.1 3.3 %collective-permute-start.25 = (bf16[128,512]{1,0:T(8,128)(2,1)S(1)}, bf16[128,512]{1,0:T(8,128)(2,1)S(1)}, u32[]{:S(2)}, u32[]{:S(2)}) collective-permute-start(bf16[128,512]{1,0:T(8,128)(2,1)S(1)} %pad_maximum_fusion.5), channel_id=1, source_target_pairs={{0,24},{1,25},{2,26},{3,27},{4,28},{5,29},{6,30},{7,31},{8,0},{9,1... | collective-permute-start | bytes 393224 | tf_op jit(solution)/shard_map/ppermute | solution.py:281
  155.6 3.3 %collective-permute-start.37 = (bf16[128,512]{1,0:T(8,128)(2,1)S(1)}, bf16[128,512]{1,0:T(8,128)(2,1)S(1)}, u32[]{:S(2)}, u32[]{:S(2)}) collective-permute-start(bf16[128,512]{1,0:T(8,128)(2,1)S(1)} %get-tuple-element.41), channel_id=1, source_target_pairs={{0,7},{1,0},{2,1},{3,2},{4,3},{5,4},{6,5},{7,6},{8,15},{9,8},{10,9... | collective-permute-start | bytes 393224 | tf_op jit(solution)/shard_map/ppermute | solution.py:276
  158.9 2.5 %collective-permute-done.37.refs_9_ = bf16[128,512]{1,0:T(8,128)(2,1)S(1)} collective-permute-done((bf16[128,512]{1,0:T(8,128)(2,1)S(1)}, bf16[128,512]{1,0:T(8,128)(2,1)S(1)}, u32[]{:S(2)}, u32[]{:S(2)}) %collective-permute-start.37) | collective-permute-done | bytes 131104 | tf_op jit(solution)/shard_map/ppermute | solution.py:276
  161.4 3.7 %collective-permute-done.33.refs_8_ = bf16[128,512]{1,0:T(8,128)(2,1)S(1)} collective-permute-done((bf16[128,512]{1,0:T(8,128)(2,1)S(1)}, bf16[128,512]{1,0:T(8,128)(2,1)S(1)}, u32[]{:S(2)}, u32[]{:S(2)}) %collective-permute-start.33) | collective-permute-done | bytes 131104 | tf_op jit(solution)/shard_map/ppermute | solution.py:276
  165.1 1.3 finish.1
  (108 shorter events, 8.7 us)
Async XLA Ops:
  0.0 41.6 %copy-start.3 = (bf16[512,1024]{1,0:T(8,128)(2,1)S(1)}, bf16[512,1024]{1,0:T(8,128)(2,1)}, u32[]{:S(2)}) copy-start(bf16[512,1024]{1,0:T(8,128)(2,1)} %w_ref.1) | copy-start | bytes 3145732
  1.9 29.7 %collective-permute-start.13 = (bf16[512,512]{1,0:T(8,128)(2,1)S(1)}, bf16[512,512]{1,0:T(8,128)(2,1)S(1)}, u32[]{:S(2)}, u32[]{:S(2)}) collective-permute-start(bf16[512,512]{1,0:T(8,128)(2,1)S(1)} %norm.1.refs_1_.refs_0_), channel_id=1, source_target_pairs={{0,32},{32,0},{64,96},{96,64},{128,160},{160,128},{192,224},{224,1... | collective-permute-start | bytes 1572872 | tf_op jit(solution)/shard_map/ppermute | solution.py:271
  2.0 24.3 %collective-permute-start.4 = (bf16[512,512]{1,0:T(8,128)(2,1)S(1)}, bf16[512,512]{1,0:T(8,128)(2,1)S(1)}, u32[]{:S(2)}, u32[]{:S(2)}) collective-permute-start(bf16[512,512]{1,0:T(8,128)(2,1)S(1)} %norm.1.refs_1_.refs_0_), channel_id=1, source_target_pairs={{0,64},{32,96},{64,128},{96,160},{128,192},{160,224},{192,0},{224,... | collective-permute-start | bytes 1572872 | tf_op jit(solution)/shard_map/ppermute | solution.py:266
  3.6 22.8 %collective-permute-start.3 = (bf16[512,512]{1,0:T(8,128)(2,1)S(1)}, bf16[512,512]{1,0:T(8,128)(2,1)S(1)}, u32[]{:S(2)}, u32[]{:S(2)}) collective-permute-start(bf16[512,512]{1,0:T(8,128)(2,1)S(1)} %norm.1.refs_1_.refs_0_), channel_id=1, source_target_pairs={{0,192},{32,224},{64,0},{96,32},{128,64},{160,96},{192,128},{224,1... | collective-permute-start | bytes 1572872 | tf_op jit(solution)/shard_map/ppermute | solution.py:266
  4.5 7.9 %collective-permute-start = (s32[256]{0:T(256)}, s32[256]{0:T(256)S(1)}, u32[]{:S(2)}, u32[]{:S(2)}) collective-permute-start(s32[256]{0:T(256)} %param.13), channel_id=1, source_target_pairs={{0,7},{1,0},{2,1},{3,2},{4,3},{5,4},{6,5},{7,6},{8,15},{9,8},{10,9... | collective-permute-start | bytes 3080 | tf_op jit(solution)/shard_map/ppermute | solution.py:276
  13.0 4.5 %collective-permute-start.1 = (s32[512]{0:T(512)S(1)}, s32[512]{0:T(512)S(1)}, u32[]{:S(2)}, u32[]{:S(2)}) collective-permute-start(s32[512]{0:T(512)S(1)} %pad_add_fusion.3), channel_id=1, source_target_pairs={{0,6},{1,7},{2,0},{3,1},{4,2},{5,3},{6,4},{7,5},{8,14},{9,15},{10,... | collective-permute-start | bytes 6152 | tf_op jit(solution)/shard_map/ppermute | solution.py:276
  18.2 7.5 %collective-permute-start.2 = (s32[1024]{0:T(1024)S(1)}, s32[1024]{0:T(1024)S(1)}, u32[]{:S(2)}, u32[]{:S(2)}) collective-permute-start(s32[1024]{0:T(1024)S(1)} %pad_add_fusion.2), channel_id=1, source_target_pairs={{0,4},{1,5},{2,6},{3,7},{4,0},{5,1},{6,2},{7,3},{8,12},{9,13},{10,... | collective-permute-start | bytes 12296 | tf_op jit(solution)/shard_map/ppermute | solution.py:276
  26.4 15.1 %collective-permute-start.12 = (bf16[512,512]{1,0:T(8,128)(2,1)S(1)}, bf16[512,512]{1,0:T(8,128)(2,1)S(1)}, u32[]{:S(2)}, u32[]{:S(2)}) collective-permute-start(bf16[512,512]{1,0:T(8,128)(2,1)S(1)} %collective-permute-done.3.refs_1_.refs_2_), channel_id=1, source_target_pairs={{0,32},{32,0},{64,96},{96,64},{128,160},{160,128},{192,224},{224,1... | collective-permute-start | bytes 1572872 | tf_op jit(solution)/shard_map/ppermute | solution.py:271
  26.6 17.3 %collective-permute-start.11 = (bf16[512,512]{1,0:T(8,128)(2,1)S(1)}, bf16[512,512]{1,0:T(8,128)(2,1)S(1)}, u32[]{:S(2)}, u32[]{:S(2)}) collective-permute-start(bf16[512,512]{1,0:T(8,128)(2,1)S(1)} %collective-permute-done.4.refs_1_.refs_8_), channel_id=1, source_target_pairs={{0,32},{32,0},{64,96},{96,64},{128,160},{160,128},{192,224},{224,1... | collective-permute-start | bytes 1572872 | tf_op jit(solution)/shard_map/ppermute | solution.py:271
  27.1 8.5 %collective-permute-start.5 = (s32[2048]{0:T(1024)S(1)}, s32[2048]{0:T(1024)S(1)}, u32[]{:S(2)}, u32[]{:S(2)}) collective-permute-start(s32[2048]{0:T(1024)S(1)} %pad_add_fusion.1), channel_id=1, source_target_pairs={{0,24},{1,25},{2,26},{3,27},{4,28},{5,29},{6,30},{7,31},{8,0},{9,1... | collective-permute-start | bytes 24584 | tf_op jit(solution)/shard_map/ppermute | solution.py:281
  30.1 10.8 %collective-permute-start.8 = (bf16[256,512]{1,0:T(8,128)(2,1)S(1)}, bf16[256,512]{1,0:T(8,128)(2,1)S(1)}, u32[]{:S(2)}, u32[]{:S(2)}) collective-permute-start(bf16[256,512]{1,0:T(8,128)(2,1)S(1)} %slice.193), channel_id=1, source_target_pairs={{0,64},{32,96},{64,128},{96,160},{128,192},{160,224},{192,0},{224,... | collective-permute-start | bytes 786440 | tf_op jit(solution)/shard_map/ppermute | solution.py:266
  31.6 9.4 %collective-permute-start.7 = (bf16[256,512]{1,0:T(8,128)(2,1)S(1)}, bf16[256,512]{1,0:T(8,128)(2,1)S(1)}, u32[]{:S(2)}, u32[]{:S(2)}) collective-permute-start(bf16[256,512]{1,0:T(8,128)(2,1)S(1)} %slice.192), channel_id=1, source_target_pairs={{0,192},{32,224},{64,0},{96,32},{128,64},{160,96},{192,128},{224,1... | collective-permute-start | bytes 786440 | tf_op jit(solution)/shard_map/ppermute | solution.py:266
  32.2 1.2 copy-start.2
  35.6 5.3 %collective-permute-start.6 = (s32[4096]{0:T(1024)S(1)}, s32[4096]{0:T(1024)S(1)}, u32[]{:S(2)}, u32[]{:S(2)}) collective-permute-start(s32[4096]{0:T(1024)S(1)} %pad_add_fusion), channel_id=1, source_target_pairs={{0,16},{1,17},{2,18},{3,19},{4,20},{5,21},{6,22},{7,23},{8,24},{9,... | collective-permute-start | bytes 49160 | tf_op jit(solution)/shard_map/ppermute | solution.py:281
  41.0 5.1 %collective-permute-start.10 = (bf16[256,512]{1,0:T(8,128)(2,1)S(1)}, bf16[256,512]{1,0:T(8,128)(2,1)S(1)}, u32[]{:S(2)}, u32[]{:S(2)}) collective-permute-start(bf16[256,512]{1,0:T(8,128)(2,1)S(1)} %collective-permute-done.8.refs_2_.refs_5_), channel_id=1, source_target_pairs={{0,32},{32,0},{64,96},{96,64},{128,160},{160,128},{192,224},{224,1... | collective-permute-start | bytes 786440 | tf_op jit(solution)/shard_map/ppermute | solution.py:271
  41.0 5.1 %collective-permute-start.9 = (bf16[256,512]{1,0:T(8,128)(2,1)S(1)}, bf16[256,512]{1,0:T(8,128)(2,1)S(1)}, u32[]{:S(2)}, u32[]{:S(2)}) collective-permute-start(bf16[256,512]{1,0:T(8,128)(2,1)S(1)} %collective-permute-done.7.refs_1_.refs_4_), channel_id=1, source_target_pairs={{0,32},{32,0},{64,96},{96,64},{128,160},{160,128},{192,224},{224,1... | collective-permute-start | bytes 786440 | tf_op jit(solution)/shard_map/ppermute | solution.py:271
  46.1 2.3 %copy-start = (bf16[2048,512]{1,0:T(8,128)(2,1)S(1)}, bf16[2048,512]{1,0:T(8,128)(2,1)}, u32[]{:S(2)}) copy-start(bf16[2048,512]{1,0:T(8,128)(2,1)} %k_ref.9) | copy-start | bytes 6291460
  46.1 2.3 %copy-start.1 = (bf16[2048,512]{1,0:T(8,128)(2,1)S(1)}, bf16[2048,512]{1,0:T(8,128)(2,1)}, u32[]{:S(2)}) copy-start(bf16[2048,512]{1,0:T(8,128)(2,1)} %v_ref.9) | copy-start | bytes 6291460
  46.1 2.3 %copy-start.10 = (s32[16]{0:T(128)S(1)}, s32[16]{0:T(128)}, u32[]{:S(2)}) copy-start(s32[16]{0:T(128)} %constant.131.clone.order_ref) | copy-start | bytes 196
  48.4 2.9 %copy-start.9 = (s32[24]{0:T(128)S(1)}, s32[24]{0:T(128)}, u32[]{:S(2)}) copy-start(s32[24]{0:T(128)} %constant.130.clone.order_ref) | copy-start | bytes 292
  51.2 14.6 %copy-start.8 = (s32[32]{0:T(128)S(1)}, s32[32]{0:T(128)}, u32[]{:S(2)}) copy-start(s32[32]{0:T(128)} %constant.132.clone.order_ref) | copy-start | bytes 388
  55.9 16.4 %copy-start.7 = (s32[16]{0:T(128)S(1)}, s32[16]{0:T(128)}, u32[]{:S(2)}) copy-start(s32[16]{0:T(128)} %constant.133.clone.order_ref) | copy-start | bytes 196
  55.9 33.2 %collective-permute-start.14 = (bf16[2,128,512]{2,1,0:T(8,128)(2,1)S(1)}, bf16[2,128,512]{2,1,0:T(8,128)(2,1)S(1)}, u32[]{:S(2)}, u32[]{:S(2)}) collective-permute-start(bf16[2,128,512]{2,1,0:T(8,128)(2,1)S(1)} %get-tuple-element.26), channel_id=1, source_target_pairs={{0,1},{1,2},{2,3},{3,4},{4,5},{5,6},{6,7},{7,0},{8,9},{9,10},{10,1... | collective-permute-start | bytes 786440 | tf_op jit(solution)/shard_map/ppermute | solution.py:276
  57.6 31.2 %collective-permute-start.18 = (bf16[2,128,512]{2,1,0:T(8,128)(2,1)S(1)}, bf16[2,128,512]{2,1,0:T(8,128)(2,1)S(1)}, u32[]{:S(2)}, u32[]{:S(2)}) collective-permute-start(bf16[2,128,512]{2,1,0:T(8,128)(2,1)S(1)} %get-tuple-element.31), channel_id=1, source_target_pairs={{0,7},{1,0},{2,1},{3,2},{4,3},{5,4},{6,5},{7,6},{8,15},{9,8},{10,9... | collective-permute-start | bytes 786440 | tf_op jit(solution)/shard_map/ppermute | solution.py:276
  62.6 31.3 %collective-permute-start.26 = (bf16[4,128,512]{2,1,0:T(8,128)(2,1)S(1)}, bf16[4,128,512]{2,1,0:T(8,128)(2,1)S(1)}, u32[]{:S(2)}, u32[]{:S(2)}) collective-permute-start(bf16[4,128,512]{2,1,0:T(8,128)(2,1)S(1)} %get-tuple-element.35), channel_id=1, source_target_pairs={{0,8},{1,9},{2,10},{3,11},{4,12},{5,13},{6,14},{7,15},{8,16},{9,17... | collective-permute-start | bytes 1572872 | tf_op jit(solution)/shard_map/ppermute | solution.py:281
  62.8 28.5 %collective-permute-start.28 = (bf16[4,128,512]{2,1,0:T(8,128)(2,1)S(1)}, bf16[4,128,512]{2,1,0:T(8,128)(2,1)S(1)}, u32[]{:S(2)}, u32[]{:S(2)}) collective-permute-start(bf16[4,128,512]{2,1,0:T(8,128)(2,1)S(1)} %get-tuple-element.38), channel_id=1, source_target_pairs={{0,24},{1,25},{2,26},{3,27},{4,28},{5,29},{6,30},{7,31},{8,0},{9,1... | collective-permute-start | bytes 1572872 | tf_op jit(solution)/shard_map/ppermute | solution.py:281
  72.1 5.5 %copy-start.6 = (s32[40]{0:T(128)S(1)}, s32[40]{0:T(128)}, u32[]{:S(2)}) copy-start(s32[40]{0:T(128)} %constant.134.clone.order_ref) | copy-start | bytes 484
  89.0 11.8 %collective-permute-start.19 = (bf16[4,128,512]{2,1,0:T(8,128)(2,1)S(1)}, bf16[4,128,512]{2,1,0:T(8,128)(2,1)S(1)}, u32[]{:S(2)}, u32[]{:S(2)}) collective-permute-start(bf16[4,128,512]{2,1,0:T(8,128)(2,1)S(1)} %pad_maximum_fusion.3), channel_id=1, source_target_pairs={{0,7},{1,0},{2,1},{3,2},{4,3},{5,4},{6,5},{7,6},{8,15},{9,8},{10,9... | collective-permute-start | bytes 1572872 | tf_op jit(solution)/shard_map/ppermute | solution.py:276
  89.2 15.2 %collective-permute-start.15 = (bf16[4,128,512]{2,1,0:T(8,128)(2,1)S(1)}, bf16[4,128,512]{2,1,0:T(8,128)(2,1)S(1)}, u32[]{:S(2)}, u32[]{:S(2)}) collective-permute-start(bf16[4,128,512]{2,1,0:T(8,128)(2,1)S(1)} %pad_maximum_fusion.2), channel_id=1, source_target_pairs={{0,1},{1,2},{2,3},{3,4},{4,5},{5,6},{6,7},{7,0},{8,9},{9,10},{10,1... | collective-permute-start | bytes 1572872 | tf_op jit(solution)/shard_map/ppermute | solution.py:276
  91.5 27.5 %collective-permute-start.29 = (bf16[8,128,512]{2,1,0:T(8,128)(2,1)S(1)}, bf16[8,128,512]{2,1,0:T(8,128)(2,1)S(1)}, u32[]{:S(2)}, u32[]{:S(2)}) collective-permute-start(bf16[8,128,512]{2,1,0:T(8,128)(2,1)S(1)} %pad_maximum_fusion.1), channel_id=1, source_target_pairs={{0,24},{1,25},{2,26},{3,27},{4,28},{5,29},{6,30},{7,31},{8,0},{9,1... | collective-permute-start | bytes 3145736 | tf_op jit(solution)/shard_map/ppermute | solution.py:281
  94.1 24.9 %collective-permute-start.27 = (bf16[8,128,512]{2,1,0:T(8,128)(2,1)S(1)}, bf16[8,128,512]{2,1,0:T(8,128)(2,1)S(1)}, u32[]{:S(2)}, u32[]{:S(2)}) collective-permute-start(bf16[8,128,512]{2,1,0:T(8,128)(2,1)S(1)} %pad_maximum_fusion), channel_id=1, source_target_pairs={{0,8},{1,9},{2,10},{3,11},{4,12},{5,13},{6,14},{7,15},{8,16},{9,17... | collective-permute-start | bytes 3145736 | tf_op jit(solution)/shard_map/ppermute | solution.py:281
  101.0 14.0 %collective-permute-start.20 = (bf16[4,128,512]{2,1,0:T(8,128)(2,1)S(1)}, bf16[4,128,512]{2,1,0:T(8,128)(2,1)S(1)}, u32[]{:S(2)}, u32[]{:S(2)}) collective-permute-start(bf16[4,128,512]{2,1,0:T(8,128)(2,1)S(1)} %add_convert_fusion.3), channel_id=1, source_target_pairs={{0,7},{1,0},{2,1},{3,2},{4,3},{5,4},{6,5},{7,6},{8,15},{9,8},{10,9... | collective-permute-start | bytes 1572872 | tf_op jit(solution)/shard_map/ppermute | solution.py:276
  104.5 14.3 %collective-permute-start.16 = (bf16[4,128,512]{2,1,0:T(8,128)(2,1)S(1)}, bf16[4,128,512]{2,1,0:T(8,128)(2,1)S(1)}, u32[]{:S(2)}, u32[]{:S(2)}) collective-permute-start(bf16[4,128,512]{2,1,0:T(8,128)(2,1)S(1)} %add_convert_fusion.5), channel_id=1, source_target_pairs={{0,1},{1,2},{2,3},{3,4},{4,5},{5,6},{6,7},{7,0},{8,9},{9,10},{10,1... | collective-permute-start | bytes 1572872 | tf_op jit(solution)/shard_map/ppermute | solution.py:276
  104.8 60.2 %copy-start.5 = (bf16[512,512]{1,0:T(8,128)(2,1)S(1)}, bf16[512,512]{1,0:T(8,128)(2,1)}, u32[]{:S(2)}) copy-start(bf16[512,512]{1,0:T(8,128)(2,1)} %refs_11_.1) | copy-start | bytes 1572868
  115.1 28.6 %collective-permute-start.21 = (bf16[4,128,512]{2,1,0:T(8,128)(2,1)S(1)}, bf16[4,128,512]{2,1,0:T(8,128)(2,1)S(1)}, u32[]{:S(2)}, u32[]{:S(2)}) collective-permute-start(bf16[4,128,512]{2,1,0:T(8,128)(2,1)S(1)} %add_convert_fusion.2), channel_id=1, source_target_pairs={{0,7},{1,0},{2,1},{3,2},{4,3},{5,4},{6,5},{7,6},{8,15},{9,8},{10,9... | collective-permute-start | bytes 1572872 | tf_op jit(solution)/shard_map/ppermute | solution.py:276
  119.0 24.7 %collective-permute-start.17 = (bf16[4,128,512]{2,1,0:T(8,128)(2,1)S(1)}, bf16[4,128,512]{2,1,0:T(8,128)(2,1)S(1)}, u32[]{:S(2)}, u32[]{:S(2)}) collective-permute-start(bf16[4,128,512]{2,1,0:T(8,128)(2,1)S(1)} %add_convert_fusion.4), channel_id=1, source_target_pairs={{0,1},{1,2},{2,3},{3,4},{4,5},{5,6},{6,7},{7,0},{8,9},{9,10},{10,1... | collective-permute-start | bytes 1572872 | tf_op jit(solution)/shard_map/ppermute | solution.py:276
  119.2 10.7 %collective-permute-start.34 = (bf16[64,512]{1,0:T(8,128)(2,1)S(1)}, bf16[64,512]{1,0:T(8,128)(2,1)S(1)}, u32[]{:S(2)}, u32[]{:S(2)}) collective-permute-start(bf16[64,512]{1,0:T(8,128)(2,1)S(1)} %get-tuple-element.46), channel_id=1, source_target_pairs={{0,7},{1,0},{2,1},{3,2},{4,3},{5,4},{6,5},{7,6},{8,15},{9,8},{10,9... | collective-permute-start | bytes 196616 | tf_op jit(solution)/shard_map/ppermute | solution.py:276
  122.5 11.1 %collective-permute-start.30 = (bf16[64,512]{1,0:T(8,128)(2,1)S(1)}, bf16[64,512]{1,0:T(8,128)(2,1)S(1)}, u32[]{:S(2)}, u32[]{:S(2)}) collective-permute-start(bf16[64,512]{1,0:T(8,128)(2,1)S(1)} %get-tuple-element.48), channel_id=1, source_target_pairs={{0,1},{1,2},{2,3},{3,4},{4,5},{5,6},{6,7},{7,0},{8,9},{9,10},{10,1... | collective-permute-start | bytes 196616 | tf_op jit(solution)/shard_map/ppermute | solution.py:276
  133.7 6.3 %collective-permute-start.31 = (bf16[128,512]{1,0:T(8,128)(2,1)S(1)}, bf16[128,512]{1,0:T(8,128)(2,1)S(1)}, u32[]{:S(2)}, u32[]{:S(2)}) collective-permute-start(bf16[128,512]{1,0:T(8,128)(2,1)S(1)} %pad_maximum_fusion.6), channel_id=1, source_target_pairs={{0,1},{1,2},{2,3},{3,4},{4,5},{5,6},{6,7},{7,0},{8,9},{9,10},{10,1... | collective-permute-start | bytes 393224 | tf_op jit(solution)/shard_map/ppermute | solution.py:276
  133.8 6.1 %collective-permute-start.35 = (bf16[128,512]{1,0:T(8,128)(2,1)S(1)}, bf16[128,512]{1,0:T(8,128)(2,1)S(1)}, u32[]{:S(2)}, u32[]{:S(2)}) collective-permute-start(bf16[128,512]{1,0:T(8,128)(2,1)S(1)} %pad_maximum_fusion.7), channel_id=1, source_target_pairs={{0,7},{1,0},{2,1},{3,2},{4,3},{5,4},{6,5},{7,6},{8,15},{9,8},{10,9... | collective-permute-start | bytes 393224 | tf_op jit(solution)/shard_map/ppermute | solution.py:276
  140.1 15.4 %collective-permute-start.36 = (bf16[128,512]{1,0:T(8,128)(2,1)S(1)}, bf16[128,512]{1,0:T(8,128)(2,1)S(1)}, u32[]{:S(2)}, u32[]{:S(2)}) collective-permute-start(bf16[128,512]{1,0:T(8,128)(2,1)S(1)} %get-tuple-element.43), channel_id=1, source_target_pairs={{0,7},{1,0},{2,1},{3,2},{4,3},{5,4},{6,5},{7,6},{8,15},{9,8},{10,9... | collective-permute-start | bytes 393224 | tf_op jit(solution)/shard_map/ppermute | solution.py:276
  143.7 11.8 %collective-permute-start.32 = (bf16[128,512]{1,0:T(8,128)(2,1)S(1)}, bf16[128,512]{1,0:T(8,128)(2,1)S(1)}, u32[]{:S(2)}, u32[]{:S(2)}) collective-permute-start(bf16[128,512]{1,0:T(8,128)(2,1)S(1)} %get-tuple-element.44), channel_id=1, source_target_pairs={{0,1},{1,2},{2,3},{3,4},{4,5},{5,6},{6,7},{7,0},{8,9},{9,10},{10,1... | collective-permute-start | bytes 393224 | tf_op jit(solution)/shard_map/ppermute | solution.py:276
  143.8 4.4 %collective-permute-start.24 = (bf16[64,512]{1,0:T(8,128)(2,1)S(1)}, bf16[64,512]{1,0:T(8,128)(2,1)S(1)}, u32[]{:S(2)}, u32[]{:S(2)}) collective-permute-start(bf16[64,512]{1,0:T(8,128)(2,1)S(1)} %get-tuple-element.52), channel_id=1, source_target_pairs={{0,24},{1,25},{2,26},{3,27},{4,28},{5,29},{6,30},{7,31},{8,0},{9,1... | collective-permute-start | bytes 196616 | tf_op jit(solution)/shard_map/ppermute | solution.py:281
  146.3 5.6 %collective-permute-start.22 = (bf16[64,512]{1,0:T(8,128)(2,1)S(1)}, bf16[64,512]{1,0:T(8,128)(2,1)S(1)}, u32[]{:S(2)}, u32[]{:S(2)}) collective-permute-start(bf16[64,512]{1,0:T(8,128)(2,1)S(1)} %get-tuple-element.54), channel_id=1, source_target_pairs={{0,8},{1,9},{2,10},{3,11},{4,12},{5,13},{6,14},{7,15},{8,16},{9,17... | collective-permute-start | bytes 196616 | tf_op jit(solution)/shard_map/ppermute | solution.py:281
  152.0 6.9 %collective-permute-start.23 = (bf16[128,512]{1,0:T(8,128)(2,1)S(1)}, bf16[128,512]{1,0:T(8,128)(2,1)S(1)}, u32[]{:S(2)}, u32[]{:S(2)}) collective-permute-start(bf16[128,512]{1,0:T(8,128)(2,1)S(1)} %pad_maximum_fusion.4), channel_id=1, source_target_pairs={{0,8},{1,9},{2,10},{3,11},{4,12},{5,13},{6,14},{7,15},{8,16},{9,17... | collective-permute-start | bytes 393224 | tf_op jit(solution)/shard_map/ppermute | solution.py:281
  152.1 6.8 %collective-permute-start.25 = (bf16[128,512]{1,0:T(8,128)(2,1)S(1)}, bf16[128,512]{1,0:T(8,128)(2,1)S(1)}, u32[]{:S(2)}, u32[]{:S(2)}) collective-permute-start(bf16[128,512]{1,0:T(8,128)(2,1)S(1)} %pad_maximum_fusion.5), channel_id=1, source_target_pairs={{0,24},{1,25},{2,26},{3,27},{4,28},{5,29},{6,30},{7,31},{8,0},{9,1... | collective-permute-start | bytes 393224 | tf_op jit(solution)/shard_map/ppermute | solution.py:281
  155.6 5.8 %collective-permute-start.37 = (bf16[128,512]{1,0:T(8,128)(2,1)S(1)}, bf16[128,512]{1,0:T(8,128)(2,1)S(1)}, u32[]{:S(2)}, u32[]{:S(2)}) collective-permute-start(bf16[128,512]{1,0:T(8,128)(2,1)S(1)} %get-tuple-element.41), channel_id=1, source_target_pairs={{0,7},{1,0},{2,1},{3,2},{4,3},{5,4},{6,5},{7,6},{8,15},{9,8},{10,9... | collective-permute-start | bytes 393224 | tf_op jit(solution)/shard_map/ppermute | solution.py:276
  158.9 6.2 %collective-permute-start.33 = (bf16[128,512]{1,0:T(8,128)(2,1)S(1)}, bf16[128,512]{1,0:T(8,128)(2,1)S(1)}, u32[]{:S(2)}, u32[]{:S(2)}) collective-permute-start(bf16[128,512]{1,0:T(8,128)(2,1)S(1)} %get-tuple-element.42), channel_id=1, source_target_pairs={{0,1},{1,2},{2,3},{3,4},{4,5},{5,6},{6,7},{7,0},{8,9},{9,10},{10,1... | collective-permute-start | bytes 393224 | tf_op jit(solution)/shard_map/ppermute | solution.py:276
  (1 other events, 1.1 us)

commit v2 on v1

--- a/solution.py
+++ b/solution.py
@@ -13,7 +13,7 @@
 LANES = 128
 NY = 4
 CORES = 2
-TILE = 128
+TILE = 256
 
 
 VMEM = pl.BlockSpec(memory_space=pltpu.VMEM)
@@ -52,29 +52,39 @@
     )(rows)
 
 
+def pack_rows(pieces, rows_ref):
+    at = 0
+    for piece in pieces:
+        tile = math.gcd(piece.shape[0], LANES)
+
+        def step(i, carry, piece=piece, at=at, tile=tile):
+            begin = pl.multiple_of(i * tile, tile)
+            rows_ref[pl.ds(at + begin, tile), :] = piece[pl.ds(begin, tile), :]
+            return carry
+
+        lax.fori_loop(0, piece.shape[0] // tile, step, 0)
+        at += piece.shape[0]
+
+
 def project_kernel(first, scale, count, *refs):
     w_ref = refs[0]
-    rows_in = refs[1 : 1 + count]
-    out_ref = refs[-1]
-    width = w_ref.shape[0]
+    out_ref, rows_ref = refs[-2], refs[-1]
+    rows, width = rows_ref.shape
     cuts = width // LANES
-    at = first
-    for row_ref in rows_in:
-        rows = row_ref.shape[0]
-        tile = math.gcd(rows, TILE)
-
-        def step(i, carry, row_ref=row_ref, at=at, tile=tile):
-            begin = pl.multiple_of(i * tile, tile)
-            half = 0.5 * jnp.dot(
-                row_ref[pl.ds(begin, tile), :], w_ref[:, width:], preferred_element_type=jnp.float32
-            )
-            query = half_silu(half).astype(jnp.bfloat16).astype(jnp.float32) * scale
-            for c in range(cuts):
-                out_ref[pl.ds((at + begin) * cuts + c, tile, stride=cuts), :] = query[:, c * LANES : (c + 1) * LANES]
-            return carry
-
-        lax.fori_loop(0, rows // tile, step, 0)
-        at += rows
+    tile = math.gcd(rows, TILE)
+    pack_rows(refs[1 : 1 + count], rows_ref)
+
+    def step(i, carry):
+        begin = pl.multiple_of(i * tile, tile)
+        half = 0.5 * jnp.dot(
+            rows_ref[pl.ds(begin, tile), :], w_ref[:, width:], preferred_element_type=jnp.float32
+        )
+        query = half_silu(half).astype(jnp.bfloat16).astype(jnp.float32) * scale
+        for c in range(cuts):
+            out_ref[pl.ds((first + begin) * cuts + c, tile, stride=cuts), :] = query[:, c * LANES : (c + 1) * LANES]
+        return carry
+
+    lax.fori_loop(0, rows // tile, step, 0)
 
 
 def project(table, first, total, pieces, w_in, scale):
@@ -91,6 +101,7 @@
         out_shape=jax.ShapeDtypeStruct((total * width // LANES, LANES), jnp.float32),
         in_specs=[VMEM] * len(ins),
         out_specs=VMEM,
+        scratch_shapes=[pltpu.VMEM((rows, width), jnp.bfloat16)],
         input_output_aliases=aliases,
         cost_estimate=pl.CostEstimate(
             flops=2 * rows * width * width, bytes_accessed=rows * width * 6, transcendentals=rows * width
@@ -101,18 +112,22 @@
 
 
 def gate_kernel(count, index_ref, w_ref, *refs):
-    pieces, out_ref = refs[:count], refs[-1]
+    pieces, out_ref, rows_ref, sum_ref = refs[:count], refs[-3], refs[-2], refs[-1]
     cand, width = out_ref.shape
-    total = jnp.zeros((cand, width), jnp.float32)
-    first = 0
+    tile = math.gcd(rows_ref.shape[0], TILE)
+    pack_rows(pieces, rows_ref)
+    sum_ref[...] = jnp.zeros_like(sum_ref)
     index = jnp.broadcast_to(index_ref[...], (LANES, cand)).T[:, :1]
-    for piece in pieces:
-        rows = piece.shape[0]
-        ids = lax.broadcasted_iota(jnp.int32, (cand, rows), 1) + first
-        pick = jnp.where(index == ids, 1.0, 0.0).astype(jnp.bfloat16)
-        total = total + jnp.dot(pick, piece[...], preferred_element_type=jnp.float32)
-        first += rows
-    normed = total.astype(jnp.bfloat16)
+    ids = lax.broadcasted_iota(jnp.int32, (cand, tile), 1)
+
+    def step(i, carry):
+        begin = pl.multiple_of(i * tile, tile)
+        pick = jnp.where(index - begin == ids, 1.0, 0.0).astype(jnp.bfloat16)
+        sum_ref[...] += jnp.dot(pick, rows_ref[pl.ds(begin, tile), :], preferred_element_type=jnp.float32)
+        return carry
+
+    lax.fori_loop(0, rows_ref.shape[0] // tile, step, 0)
+    normed = sum_ref[...].astype(jnp.bfloat16)
     half = 0.5 * jnp.dot(normed, w_ref[:, :width], preferred_element_type=jnp.float32)
     out_ref[...] = half_silu(half).astype(jnp.bfloat16)
 
@@ -126,6 +141,7 @@
         out_shape=jax.ShapeDtypeStruct((cand, width), jnp.bfloat16),
         in_specs=[VMEM] * (2 + len(pieces)),
         out_specs=VMEM,
+        scratch_shapes=[pltpu.VMEM((rows, width), jnp.bfloat16), pltpu.VMEM((cand, width), jnp.float32)],
         cost_estimate=pl.CostEstimate(
             flops=2 * cand * width * (rows + width), bytes_accessed=rows * width * 2, transcendentals=cand * width
         ),
@@ -135,7 +151,7 @@
 
 
 def attend_kernel(sizes, unroll, index_ref, count_ref, block_ref, order_ref, table_ref, k_ref, v_ref, *refs):
-    outs, (rows_ref, query_ref, sum_ref) = refs[: len(sizes)], refs[len(sizes) :]
+    outs, (rows_ref, query_ref, sum_ref, weight_ref) = refs[: len(sizes)], refs[len(sizes) :]
     rows, width = sum_ref.shape
     cuts = width // LANES
     low = lax.broadcasted_iota(jnp.int32, (BLK, LANES), 1) < LANES // 2
@@ -172,9 +188,11 @@
                     half = lax.dot_general(
                         query_ref[:, lanes], keys, (((1,), (1,)), ((), ())), preferred_element_type=jnp.float32
                     )
-                    weight = half_silu(half).astype(jnp.bfloat16)
+                    weight_ref[c] = half_silu(half).astype(jnp.bfloat16)
+                for c in range(cuts):
+                    lanes = slice(c * LANES, (c + 1) * LANES)
                     values = split(v_ref[pl.ds(begin, BLK), lanes])
-                    sum_ref[:, lanes] += jnp.dot(weight, values, preferred_element_type=jnp.float32)
+                    sum_ref[:, lanes] += jnp.dot(weight_ref[c], values, preferred_element_type=jnp.float32)
                 return inner_carry
 
             lax.fori_loop(0, blocks, one_block, 0)
@@ -205,6 +223,7 @@
             pltpu.VMEM((rows * width // LANES, LANES), jnp.float32),
             pltpu.VMEM((rows, width), jnp.bfloat16),
             pltpu.VMEM((rows, width), jnp.float32),
+            pltpu.VMEM((width // LANES, rows, 2 * BLK), jnp.bfloat16),
         ],
         cost_estimate=pl.CostEstimate(
             flops=number * rows * BLK * width * 8,

time: 167 us -> 157 us (0.940)
  Pallas kernels: 42.9 us -> 38.3 us
  waiting for transfers between devices: 52.4 us -> 48.2 us
    pallas_call x5, Pallas kernels: 30.3 us -> 25.1 us  [attend(): pl.pallas_call(functools.partial(attend_kernel, tuple(sizes), math.gcd(ro...]
    ppermute x19, waiting for transfers between devices: 42.1 us -> 38.1 us  [z_shift(): lax.ppermute(value, 'shard', [(y * nz + z, y * nz + (z + k) % nz) for y i...]
    pallas_call x1, Pallas kernels: 1.67 us -> 5.1 us  [gate_rows(): pl.pallas_call(functools.partial(gate_kernel, len(pieces)), out_shape=jax...]
    pallas_call x4, Pallas kernels: 8.9 us -> 6.36 us  [project(): pl.pallas_call(kernel, out_shape=jax.ShapeDtypeStruct((total * width // L...]
  transfers between devices with their start and end apart: 38 -> 38, of which waited for: 12 -> 13; matrix products, arithmetic and copies ran while one was open for 4% -> 4% of each run, Pallas kernels for 19% -> 18%
where the time goes in v2:
time: 157 us
  starting transfers between devices  60.4 us (38%)
  waiting for transfers between devices  48.2 us (31%)
  Pallas kernels  38.3 us (24%)
  other arithmetic  6.55 us (4%)
  local copies, waits for them, and re-layouts  3.17 us (2%)
    ppermute x19, starting transfers between devices, z_shift(): lax.ppermute(value, 'shard', [(y * nz + z, y * nz + (z + k) % nz) for y i...  39.9 us
    ppermute x19, waiting for transfers between devices, z_shift(): lax.ppermute(value, 'shard', [(y * nz + z, y * nz + (z + k) % nz) for y i...  38.1 us
    pallas_call x5, Pallas kernels, attend(): pl.pallas_call(functools.partial(attend_kernel, tuple(sizes), math.gcd(ro...  25.1 us
    ppermute x10, starting transfers between devices, y_shift(): lax.ppermute(value, 'shard', [(y * nz + z, (y + k) % NY * nz + z) for y i...  14.8 us
    ppermute x10, waiting for transfers between devices, y_shift(): lax.ppermute(value, 'shard', [(y * nz + z, (y + k) % NY * nz + z) for y i...  10.1 us
    pallas_call x4, Pallas kernels, project(): pl.pallas_call(kernel, out_shape=jax.ShapeDtypeStruct((total * width // L...  6.36 us
    pallas_call x1, Pallas kernels, gate_rows(): pl.pallas_call(functools.partial(gate_kernel, len(pieces)), out_shape=jax...  5.1 us
    ppermute x4, starting transfers between devices, x_shift(): lax.ppermute(value, 'grp', [(x * CORES + c, (x + k) % nx * CORES + c) for...  4.44 us
  transfers between devices with their start and end apart: 38, of which 13 were waited for; matrix products, arithmetic and copies ran while one was open for 4% of the time, Pallas kernels for 18%

profile of v2, /device:TPU:2, one launch (start us, length us, event | category | flops | bytes accessed | tf_op | source)
XLA Modules:
  0.0 157.3 jit_solution(12241371639596400278)
XLA Ops:
  0.0 1.1 copy-done.4
  1.7 1.6 collective-permute-start.4
  3.3 0.8 collective-permute-start.3
  4.1 5.5 %collective-permute-start = (s32[256]{0:T(256)}, s32[256]{0:T(256)S(1)}, u32[]{:S(2)}, u32[]{:S(2)}) collective-permute-start(s32[256]{0:T(256)} %param.13), channel_id=1, source_target_pairs={{0,7},{1,0},{2,1},{3,2},{4,3},{5,4},{6,5},{7,6},{8,15},{9,8},{10,9... | collective-permute-start | bytes 3080 | tf_op jit(solution)/shard_map/ppermute | solution.py:295
  9.7 0.9 convert_reduce_fusion
  10.6 0.7 fusion.29
  12.7 1.9 %collective-permute-start.1 = (s32[512]{0:T(512)S(1)}, s32[512]{0:T(512)S(1)}, u32[]{:S(2)}, u32[]{:S(2)}) collective-permute-start(s32[512]{0:T(512)S(1)} %pad_add_fusion.3), channel_id=1, source_target_pairs={{0,6},{1,7},{2,0},{3,1},{4,2},{5,3},{6,4},{7,5},{8,14},{9,15},{10,... | collective-permute-start | bytes 6152 | tf_op jit(solution)/shard_map/ppermute | solution.py:295
  14.7 2.5 %collective-permute-done.1 = s32[512]{0:T(512)S(1)} collective-permute-done((s32[512]{0:T(512)S(1)}, s32[512]{0:T(512)S(1)}, u32[]{:S(2)}, u32[]{:S(2)}) %collective-permute-start.1) | collective-permute-done | bytes 2080 | tf_op jit(solution)/shard_map/ppermute | solution.py:295
  17.9 2.8 %collective-permute-start.2 = (s32[1024]{0:T(1024)S(1)}, s32[1024]{0:T(1024)S(1)}, u32[]{:S(2)}, u32[]{:S(2)}) collective-permute-start(s32[1024]{0:T(1024)S(1)} %pad_add_fusion.2), channel_id=1, source_target_pairs={{0,4},{1,5},{2,6},{3,7},{4,0},{5,1},{6,2},{7,3},{8,12},{9,13},{10,... | collective-permute-start | bytes 12296 | tf_op jit(solution)/shard_map/ppermute | solution.py:295
  20.7 4.6 %collective-permute-done.2 = s32[1024]{0:T(1024)S(1)} collective-permute-done((s32[1024]{0:T(1024)S(1)}, s32[1024]{0:T(1024)S(1)}, u32[]{:S(2)}, u32[]{:S(2)}) %collective-permute-start.2) | collective-permute-done | bytes 4128 | tf_op jit(solution)/shard_map/ppermute | solution.py:295
  26.8 3.0 %collective-permute-start.5 = (s32[2048]{0:T(1024)S(1)}, s32[2048]{0:T(1024)S(1)}, u32[]{:S(2)}, u32[]{:S(2)}) collective-permute-start(s32[2048]{0:T(1024)S(1)} %pad_add_fusion.1), channel_id=1, source_target_pairs={{0,24},{1,25},{2,26},{3,27},{4,28},{5,29},{6,30},{7,31},{8,0},{9,1... | collective-permute-start | bytes 24584 | tf_op jit(solution)/shard_map/ppermute | solution.py:300
  29.8 1.5 collective-permute-start.8
  31.9 1.2 copy-done.2
  33.1 1.6 %project.4.refs_3_ = f32[16384,128]{1,0:T(8,128)S(1)} custom-call(bf16[512,1024]{1,0:T(8,128)(2,1)S(1)} %copy-done.2, bf16[512,512]{1,0:T(8,128)(2,1)S(1)} %norm.1.refs_1_.refs_0_, bf16[512,512]{1,0:T(8,128)(2,1)S(1)} %collective-permute-done.13.refs_2_.refs_1_), custom_call_target="tpu_custom_call" | custom-call | flops 536870912 | bytes 3145728 | tf_op jit(solution)/shard_map/project/pallas_call | solution.py:99
  34.7 0.7 collective-permute-start.6
  35.4 4.6 %collective-permute-done.6 = s32[4096]{0:T(1024)S(1)} collective-permute-done((s32[4096]{0:T(1024)S(1)}, s32[4096]{0:T(1024)S(1)}, u32[]{:S(2)}, u32[]{:S(2)}) %collective-permute-start.6) | collective-permute-done | bytes 16416 | tf_op jit(solution)/shard_map/ppermute | solution.py:300
  40.6 1.6 %project.5.refs_3_ = f32[16384,128]{1,0:T(8,128)S(1)} custom-call(bf16[512,1024]{1,0:T(8,128)(2,1)S(1)} %copy-done.3, bf16[512,512]{1,0:T(8,128)(2,1)S(1)} %collective-permute-done.3.refs_1_.refs_2_, bf16[512,512]{1,0:T(8,128)(2,1)S(1)} %collective-permute-done.12.refs_2_.refs_3_, f32[16384,128]{1,0:T(8,128)S(1)} %project.4.refs_3_), custom_call_target="tpu_custom_call", output_to_operand_aliasing={{}: (3, {})} | custom-call | flops 536870912 | bytes 3145728 | tf_op jit(solution)/shard_map/project/pallas_call | solution.py:99
  42.2 1.6 %project.6.refs_5_ = f32[16384,128]{1,0:T(8,128)S(1)} custom-call(bf16[512,1024]{1,0:T(8,128)(2,1)S(1)} %copy-done.3, bf16[512,512]{1,0:T(8,128)(2,1)S(1)} %collective-permute-done.4.refs_1_.refs_8_, bf16[512,512]{1,0:T(8,128)(2,1)S(1)} %collective-permute-done.11.refs_2_.refs_9_, f32[16384,128]{1,0:T(8,128)S(1)} %project.5.refs_3_), custom_call_target="tpu_custom_call", output_to_operand_aliasing={{}: (3, {})} | custom-call | flops 536870912 | bytes 3145728 | tf_op jit(solution)/shard_map/project/pallas_call | solution.py:99
  43.9 1.6 %project.7.table_ref = f32[16384,128]{1,0:T(8,128)S(1)} custom-call(bf16[512,1024]{1,0:T(8,128)(2,1)S(1)} %copy-done.3, bf16[256,512]{1,0:T(8,128)(2,1)S(1)} %collective-permute-done.7.refs_1_.refs_4_, bf16[256,512]{1,0:T(8,128)(2,1)S(1)} %collective-permute-done.8.refs_2_.refs_5_, ...), custom_call_target="tpu_custom_call", output_to_operand_aliasing={{}: (5, {})} | custom-call | flops 536870912 | bytes 3145728 | tf_op jit(solution)/shard_map/project/pallas_call | solution.py:99
  46.1 2.5 %attend.7 = (bf16[4,128,512]{2,1,0:T(8,128)(2,1)S(1)}, bf16[4,128,512]{2,1,0:T(8,128)(2,1)S(1)}) custom-call(s32[8192]{0:T(1024)S(1)} %fusion.24.index_ref, s32[32]{0:T(128)S(1)} %convert_reduce_fusion.1.count_ref, s32[64]{0:T(128)S(1)} %select_reduce_fusion.block_ref, s32[16]{0:T(128)S(1)} %copy-done.10, f32[16384,128]{1,0:T(8,128)S(1)} %project.7.table_ref, ...), custom_call_target="tpu_custom_call" | custom-call | flops 536870912 | bytes 2097152 | tf_op jit(solution)/shard_map/attend/pallas_call | solution.py:217
  48.7 3.9 %attend.6 = (bf16[2,128,512]{2,1,0:T(8,128)(2,1)S(1)}, bf16[2,128,512]{2,1,0:T(8,128)(2,1)S(1)}, bf16[4,128,512]{2,1,0:T(8,128)(2,1)S(1)}, bf16[4,128,512]{2,1,0:T(8,128)(2,1)S(1)}) custom-call(s32[8192]{0:T(1024)S(1)} %fusion.24.index_ref, s32[32]{0:T(128)S(1)} %convert_reduce_fusion.1.count_ref, s32[64]{0:T(128)S(1)} %select_reduce_fusion.block_ref, ...), custom_call_target="tpu_custom_call" | custom-call | flops 805306368 | bytes 3145728 | tf_op jit(solution)/shard_map/attend/pallas_call | solution.py:217
  52.6 1.8 %collective-permute-start.14 = (bf16[2,128,512]{2,1,0:T(8,128)(2,1)S(1)}, bf16[2,128,512]{2,1,0:T(8,128)(2,1)S(1)}, u32[]{:S(2)}, u32[]{:S(2)}) collective-permute-start(bf16[2,128,512]{2,1,0:T(8,128)(2,1)S(1)} %get-tuple-element.26), channel_id=1, source_target_pairs={{0,1},{1,2},{2,3},{3,4},{4,5},{5,6},{6,7},{7,0},{8,9},{9,10},{10,1... | collective-permute-start | bytes 786440 | tf_op jit(solution)/shard_map/ppermute | solution.py:295
  54.4 4.4 %collective-permute-start.18 = (bf16[2,128,512]{2,1,0:T(8,128)(2,1)S(1)}, bf16[2,128,512]{2,1,0:T(8,128)(2,1)S(1)}, u32[]{:S(2)}, u32[]{:S(2)}) collective-permute-start(bf16[2,128,512]{2,1,0:T(8,128)(2,1)S(1)} %get-tuple-element.31), channel_id=1, source_target_pairs={{0,7},{1,0},{2,1},{3,2},{4,3},{5,4},{6,5},{7,6},{8,15},{9,8},{10,9... | collective-permute-start | bytes 786440 | tf_op jit(solution)/shard_map/ppermute | solution.py:295
  58.8 3.2 %collective-permute-start.28 = (bf16[4,128,512]{2,1,0:T(8,128)(2,1)S(1)}, bf16[4,128,512]{2,1,0:T(8,128)(2,1)S(1)}, u32[]{:S(2)}, u32[]{:S(2)}) collective-permute-start(bf16[4,128,512]{2,1,0:T(8,128)(2,1)S(1)} %get-tuple-element.38), channel_id=1, source_target_pairs={{0,24},{1,25},{2,26},{3,27},{4,28},{5,29},{6,30},{7,31},{8,0},{9,1... | collective-permute-start | bytes 1572872 | tf_op jit(solution)/shard_map/ppermute | solution.py:300
  62.0 5.2 %attend.9 = (bf16[8,128,512]{2,1,0:T(8,128)(2,1)S(1)}, bf16[8,128,512]{2,1,0:T(8,128)(2,1)S(1)}) custom-call(s32[8192]{0:T(1024)S(1)} %fusion.24.index_ref, s32[32]{0:T(128)S(1)} %convert_reduce_fusion.1.count_ref, s32[64]{0:T(128)S(1)} %select_reduce_fusion.block_ref, s32[32]{0:T(128)S(1)} %copy-done.8, f32[16384,128]{1,0:T(8,128)S(1)} %project.7.table_ref, ...), custom_call_target="tpu_custom_call" | custom-call | flops 1073741824 | bytes 4194304 | tf_op jit(solution)/shard_map/attend/pallas_call | solution.py:217
  67.4 4.5 %attend.8 = (bf16[4,128,512]{2,1,0:T(8,128)(2,1)S(1)}, bf16[4,128,512]{2,1,0:T(8,128)(2,1)S(1)}) custom-call(s32[8192]{0:T(1024)S(1)} %fusion.24.index_ref, s32[32]{0:T(128)S(1)} %convert_reduce_fusion.1.count_ref, s32[64]{0:T(128)S(1)} %select_reduce_fusion.block_ref, s32[16]{0:T(128)S(1)} %copy-done.7, f32[16384,128]{1,0:T(8,128)S(1)} %project.7.table_ref, ...), custom_call_target="tpu_custom_call" | custom-call | flops 536870912 | bytes 2097152 | tf_op jit(solution)/shard_map/attend/pallas_call | solution.py:217
  71.8 9.0 %attend.5 = (bf16[4,128,512]{2,1,0:T(8,128)(2,1)S(1)}, bf16[4,128,512]{2,1,0:T(8,128)(2,1)S(1)}, bf16[4,128,512]{2,1,0:T(8,128)(2,1)S(1)}, bf16[8,128,512]{2,1,0:T(8,128)(2,1)S(1)}) custom-call(s32[8192]{0:T(1024)S(1)} %fusion.24.index_ref, s32[32]{0:T(128)S(1)} %convert_reduce_fusion.1.count_ref, s32[64]{0:T(128)S(1)} %select_reduce_fusion.block_ref, ...), custom_call_target="tpu_custom_call" | custom-call | flops 1342177280 | bytes 5242880 | tf_op jit(solution)/shard_map/attend/pallas_call | solution.py:217
  81.3 2.1 %collective-permute-start.15 = (bf16[4,128,512]{2,1,0:T(8,128)(2,1)S(1)}, bf16[4,128,512]{2,1,0:T(8,128)(2,1)S(1)}, u32[]{:S(2)}, u32[]{:S(2)}) collective-permute-start(bf16[4,128,512]{2,1,0:T(8,128)(2,1)S(1)} %pad_maximum_fusion.2), channel_id=1, source_target_pairs={{0,1},{1,2},{2,3},{3,4},{4,5},{5,6},{6,7},{7,0},{8,9},{9,10},{10,1... | collective-permute-start | bytes 1572872 | tf_op jit(solution)/shard_map/ppermute | solution.py:295
  83.6 1.7 %collective-permute-start.29 = (bf16[8,128,512]{2,1,0:T(8,128)(2,1)S(1)}, bf16[8,128,512]{2,1,0:T(8,128)(2,1)S(1)}, u32[]{:S(2)}, u32[]{:S(2)}) collective-permute-start(bf16[8,128,512]{2,1,0:T(8,128)(2,1)S(1)} %pad_maximum_fusion.1), channel_id=1, source_target_pairs={{0,24},{1,25},{2,26},{3,27},{4,28},{5,29},{6,30},{7,31},{8,0},{9,1... | collective-permute-start | bytes 3145736 | tf_op jit(solution)/shard_map/ppermute | solution.py:300
  86.0 6.5 %collective-permute-done.19 = bf16[4,128,512]{2,1,0:T(8,128)(2,1)S(1)} collective-permute-done((bf16[4,128,512]{2,1,0:T(8,128)(2,1)S(1)}, bf16[4,128,512]{2,1,0:T(8,128)(2,1)S(1)}, u32[]{:S(2)}, u32[]{:S(2)}) %collective-permute-start.19) | collective-permute-done | bytes 524320 | tf_op jit(solution)/shard_map/ppermute | solution.py:295
  92.7 3.4 %collective-permute-start.20 = (bf16[4,128,512]{2,1,0:T(8,128)(2,1)S(1)}, bf16[4,128,512]{2,1,0:T(8,128)(2,1)S(1)}, u32[]{:S(2)}, u32[]{:S(2)}) collective-permute-start(bf16[4,128,512]{2,1,0:T(8,128)(2,1)S(1)} %add_convert_fusion.3), channel_id=1, source_target_pairs={{0,7},{1,0},{2,1},{3,2},{4,3},{5,4},{6,5},{7,6},{8,15},{9,8},{10,9... | collective-permute-start | bytes 1572872 | tf_op jit(solution)/shard_map/ppermute | solution.py:295
  96.3 5.1 %gate.1.refs_10_ = bf16[256,512]{1,0:T(8,128)(2,1)S(1)} custom-call(s32[1,256]{1,0:T(1,128)S(1)} %bitcast.136, bf16[512,1024]{1,0:T(8,128)(2,1)S(1)} %copy-done.3, bf16[512,512]{1,0:T(8,128)(2,1)S(1)} %norm.1.refs_1_.refs_0_, bf16[512,512]{1,0:T(8,128)(2,1)S(1)} %collective-permute-done.13.refs_2_.refs_1_, ...), custom_call_target="tpu_custom_call" | custom-call | flops 1207959552 | bytes 4194304 | tf_op jit(solution)/shard_map/gate/pallas_call | solution.py:139
  101.5 4.8 %collective-permute-done.20 = bf16[4,128,512]{2,1,0:T(8,128)(2,1)S(1)} collective-permute-done((bf16[4,128,512]{2,1,0:T(8,128)(2,1)S(1)}, bf16[4,128,512]{2,1,0:T(8,128)(2,1)S(1)}, u32[]{:S(2)}, u32[]{:S(2)}) %collective-permute-start.20) | collective-permute-done | bytes 524320 | tf_op jit(solution)/shard_map/ppermute | solution.py:295
  106.4 3.8 %collective-permute-start.21 = (bf16[4,128,512]{2,1,0:T(8,128)(2,1)S(1)}, bf16[4,128,512]{2,1,0:T(8,128)(2,1)S(1)}, u32[]{:S(2)}, u32[]{:S(2)}) collective-permute-start(bf16[4,128,512]{2,1,0:T(8,128)(2,1)S(1)} %add_convert_fusion.2), channel_id=1, source_target_pairs={{0,7},{1,0},{2,1},{3,2},{4,3},{5,4},{6,5},{7,6},{8,15},{9,8},{10,9... | collective-permute-start | bytes 1572872 | tf_op jit(solution)/shard_map/ppermute | solution.py:295
  110.6 3.5 %collective-permute-start.34 = (bf16[64,512]{1,0:T(8,128)(2,1)S(1)}, bf16[64,512]{1,0:T(8,128)(2,1)S(1)}, u32[]{:S(2)}, u32[]{:S(2)}) collective-permute-start(bf16[64,512]{1,0:T(8,128)(2,1)S(1)} %get-tuple-element.46), channel_id=1, source_target_pairs={{0,7},{1,0},{2,1},{3,2},{4,3},{5,4},{6,5},{7,6},{8,15},{9,8},{10,9... | collective-permute-start | bytes 196616 | tf_op jit(solution)/shard_map/ppermute | solution.py:295
  114.1 6.9 %collective-permute-done.34 = bf16[64,512]{1,0:T(8,128)(2,1)S(1)} collective-permute-done((bf16[64,512]{1,0:T(8,128)(2,1)S(1)}, bf16[64,512]{1,0:T(8,128)(2,1)S(1)}, u32[]{:S(2)}, u32[]{:S(2)}) %collective-permute-start.34) | collective-permute-done | bytes 65568 | tf_op jit(solution)/shard_map/ppermute | solution.py:295
  120.9 3.6 %collective-permute-done.30 = bf16[64,512]{1,0:T(8,128)(2,1)S(1)} collective-permute-done((bf16[64,512]{1,0:T(8,128)(2,1)S(1)}, bf16[64,512]{1,0:T(8,128)(2,1)S(1)}, u32[]{:S(2)}, u32[]{:S(2)}) %collective-permute-start.30) | collective-permute-done | bytes 65568 | tf_op jit(solution)/shard_map/ppermute | solution.py:295
  124.8 3.3 %collective-permute-start.35 = (bf16[128,512]{1,0:T(8,128)(2,1)S(1)}, bf16[128,512]{1,0:T(8,128)(2,1)S(1)}, u32[]{:S(2)}, u32[]{:S(2)}) collective-permute-start(bf16[128,512]{1,0:T(8,128)(2,1)S(1)} %pad_maximum_fusion.7), channel_id=1, source_target_pairs={{0,7},{1,0},{2,1},{3,2},{4,3},{5,4},{6,5},{7,6},{8,15},{9,8},{10,9... | collective-permute-start | bytes 393224 | tf_op jit(solution)/shard_map/ppermute | solution.py:295
  128.1 2.8 %collective-permute-done.31 = bf16[128,512]{1,0:T(8,128)(2,1)S(1)} collective-permute-done((bf16[128,512]{1,0:T(8,128)(2,1)S(1)}, bf16[128,512]{1,0:T(8,128)(2,1)S(1)}, u32[]{:S(2)}, u32[]{:S(2)}) %collective-permute-start.31) | collective-permute-done | bytes 131104 | tf_op jit(solution)/shard_map/ppermute | solution.py:295
  131.2 3.8 %collective-permute-start.36 = (bf16[128,512]{1,0:T(8,128)(2,1)S(1)}, bf16[128,512]{1,0:T(8,128)(2,1)S(1)}, u32[]{:S(2)}, u32[]{:S(2)}) collective-permute-start(bf16[128,512]{1,0:T(8,128)(2,1)S(1)} %get-tuple-element.43), channel_id=1, source_target_pairs={{0,7},{1,0},{2,1},{3,2},{4,3},{5,4},{6,5},{7,6},{8,15},{9,8},{10,9... | collective-permute-start | bytes 393224 | tf_op jit(solution)/shard_map/ppermute | solution.py:295
  135.1 2.2 %collective-permute-start.24 = (bf16[64,512]{1,0:T(8,128)(2,1)S(1)}, bf16[64,512]{1,0:T(8,128)(2,1)S(1)}, u32[]{:S(2)}, u32[]{:S(2)}) collective-permute-start(bf16[64,512]{1,0:T(8,128)(2,1)S(1)} %get-tuple-element.52), channel_id=1, source_target_pairs={{0,24},{1,25},{2,26},{3,27},{4,28},{5,29},{6,30},{7,31},{8,0},{9,1... | collective-permute-start | bytes 196616 | tf_op jit(solution)/shard_map/ppermute | solution.py:300
  137.4 2.2 %collective-permute-done.24 = bf16[64,512]{1,0:T(8,128)(2,1)S(1)} collective-permute-done((bf16[64,512]{1,0:T(8,128)(2,1)S(1)}, bf16[64,512]{1,0:T(8,128)(2,1)S(1)}, u32[]{:S(2)}, u32[]{:S(2)}) %collective-permute-start.24) | collective-permute-done | bytes 65568 | tf_op jit(solution)/shard_map/ppermute | solution.py:300
  139.6 3.3 %collective-permute-done.22 = bf16[64,512]{1,0:T(8,128)(2,1)S(1)} collective-permute-done((bf16[64,512]{1,0:T(8,128)(2,1)S(1)}, bf16[64,512]{1,0:T(8,128)(2,1)S(1)}, u32[]{:S(2)}, u32[]{:S(2)}) %collective-permute-start.22) | collective-permute-done | bytes 65568 | tf_op jit(solution)/shard_map/ppermute | solution.py:300
  143.0 3.3 %collective-permute-start.25 = (bf16[128,512]{1,0:T(8,128)(2,1)S(1)}, bf16[128,512]{1,0:T(8,128)(2,1)S(1)}, u32[]{:S(2)}, u32[]{:S(2)}) collective-permute-start(bf16[128,512]{1,0:T(8,128)(2,1)S(1)} %pad_maximum_fusion.5), channel_id=1, source_target_pairs={{0,24},{1,25},{2,26},{3,27},{4,28},{5,29},{6,30},{7,31},{8,0},{9,1... | collective-permute-start | bytes 393224 | tf_op jit(solution)/shard_map/ppermute | solution.py:300
  146.5 3.3 %collective-permute-start.37 = (bf16[128,512]{1,0:T(8,128)(2,1)S(1)}, bf16[128,512]{1,0:T(8,128)(2,1)S(1)}, u32[]{:S(2)}, u32[]{:S(2)}) collective-permute-start(bf16[128,512]{1,0:T(8,128)(2,1)S(1)} %get-tuple-element.41), channel_id=1, source_target_pairs={{0,7},{1,0},{2,1},{3,2},{4,3},{5,4},{6,5},{7,6},{8,15},{9,8},{10,9... | collective-permute-start | bytes 393224 | tf_op jit(solution)/shard_map/ppermute | solution.py:295
  149.8 2.5 %collective-permute-done.37.refs_9_ = bf16[128,512]{1,0:T(8,128)(2,1)S(1)} collective-permute-done((bf16[128,512]{1,0:T(8,128)(2,1)S(1)}, bf16[128,512]{1,0:T(8,128)(2,1)S(1)}, u32[]{:S(2)}, u32[]{:S(2)}) %collective-permute-start.37) | collective-permute-done | bytes 131104 | tf_op jit(solution)/shard_map/ppermute | solution.py:295
  152.3 3.7 %collective-permute-done.33.refs_8_ = bf16[128,512]{1,0:T(8,128)(2,1)S(1)} collective-permute-done((bf16[128,512]{1,0:T(8,128)(2,1)S(1)}, bf16[128,512]{1,0:T(8,128)(2,1)S(1)}, u32[]{:S(2)}, u32[]{:S(2)}) %collective-permute-start.33) | collective-permute-done | bytes 131104 | tf_op jit(solution)/shard_map/ppermute | solution.py:295
  156.0 1.3 finish.1
  (108 shorter events, 9.2 us)
Async XLA Ops:
  0.0 40.6 %copy-start.3 = (bf16[512,1024]{1,0:T(8,128)(2,1)S(1)}, bf16[512,1024]{1,0:T(8,128)(2,1)}, u32[]{:S(2)}) copy-start(bf16[512,1024]{1,0:T(8,128)(2,1)} %w_ref.1) | copy-start | bytes 3145732
  1.6 29.7 %collective-permute-start.13 = (bf16[512,512]{1,0:T(8,128)(2,1)S(1)}, bf16[512,512]{1,0:T(8,128)(2,1)S(1)}, u32[]{:S(2)}, u32[]{:S(2)}) collective-permute-start(bf16[512,512]{1,0:T(8,128)(2,1)S(1)} %norm.1.refs_1_.refs_0_), channel_id=1, source_target_pairs={{0,32},{32,0},{64,96},{96,64},{128,160},{160,128},{192,224},{224,1... | collective-permute-start | bytes 1572872 | tf_op jit(solution)/shard_map/ppermute | solution.py:290
  1.7 24.3 %collective-permute-start.4 = (bf16[512,512]{1,0:T(8,128)(2,1)S(1)}, bf16[512,512]{1,0:T(8,128)(2,1)S(1)}, u32[]{:S(2)}, u32[]{:S(2)}) collective-permute-start(bf16[512,512]{1,0:T(8,128)(2,1)S(1)} %norm.1.refs_1_.refs_0_), channel_id=1, source_target_pairs={{0,64},{32,96},{64,128},{96,160},{128,192},{160,224},{192,0},{224,... | collective-permute-start | bytes 1572872 | tf_op jit(solution)/shard_map/ppermute | solution.py:285
  3.3 22.8 %collective-permute-start.3 = (bf16[512,512]{1,0:T(8,128)(2,1)S(1)}, bf16[512,512]{1,0:T(8,128)(2,1)S(1)}, u32[]{:S(2)}, u32[]{:S(2)}) collective-permute-start(bf16[512,512]{1,0:T(8,128)(2,1)S(1)} %norm.1.refs_1_.refs_0_), channel_id=1, source_target_pairs={{0,192},{32,224},{64,0},{96,32},{128,64},{160,96},{192,128},{224,1... | collective-permute-start | bytes 1572872 | tf_op jit(solution)/shard_map/ppermute | solution.py:285
  4.1 7.9 %collective-permute-start = (s32[256]{0:T(256)}, s32[256]{0:T(256)S(1)}, u32[]{:S(2)}, u32[]{:S(2)}) collective-permute-start(s32[256]{0:T(256)} %param.13), channel_id=1, source_target_pairs={{0,7},{1,0},{2,1},{3,2},{4,3},{5,4},{6,5},{7,6},{8,15},{9,8},{10,9... | collective-permute-start | bytes 3080 | tf_op jit(solution)/shard_map/ppermute | solution.py:295
  12.7 4.5 %collective-permute-start.1 = (s32[512]{0:T(512)S(1)}, s32[512]{0:T(512)S(1)}, u32[]{:S(2)}, u32[]{:S(2)}) collective-permute-start(s32[512]{0:T(512)S(1)} %pad_add_fusion.3), channel_id=1, source_target_pairs={{0,6},{1,7},{2,0},{3,1},{4,2},{5,3},{6,4},{7,5},{8,14},{9,15},{10,... | collective-permute-start | bytes 6152 | tf_op jit(solution)/shard_map/ppermute | solution.py:295
  17.9 7.5 %collective-permute-start.2 = (s32[1024]{0:T(1024)S(1)}, s32[1024]{0:T(1024)S(1)}, u32[]{:S(2)}, u32[]{:S(2)}) collective-permute-start(s32[1024]{0:T(1024)S(1)} %pad_add_fusion.2), channel_id=1, source_target_pairs={{0,4},{1,5},{2,6},{3,7},{4,0},{5,1},{6,2},{7,3},{8,12},{9,13},{10,... | collective-permute-start | bytes 12296 | tf_op jit(solution)/shard_map/ppermute | solution.py:295
  26.1 14.5 %collective-permute-start.12 = (bf16[512,512]{1,0:T(8,128)(2,1)S(1)}, bf16[512,512]{1,0:T(8,128)(2,1)S(1)}, u32[]{:S(2)}, u32[]{:S(2)}) collective-permute-start(bf16[512,512]{1,0:T(8,128)(2,1)S(1)} %collective-permute-done.3.refs_1_.refs_2_), channel_id=1, source_target_pairs={{0,32},{32,0},{64,96},{96,64},{128,160},{160,128},{192,224},{224,1... | collective-permute-start | bytes 1572872 | tf_op jit(solution)/shard_map/ppermute | solution.py:290
  26.2 16.0 %collective-permute-start.11 = (bf16[512,512]{1,0:T(8,128)(2,1)S(1)}, bf16[512,512]{1,0:T(8,128)(2,1)S(1)}, u32[]{:S(2)}, u32[]{:S(2)}) collective-permute-start(bf16[512,512]{1,0:T(8,128)(2,1)S(1)} %collective-permute-done.4.refs_1_.refs_8_), channel_id=1, source_target_pairs={{0,32},{32,0},{64,96},{96,64},{128,160},{160,128},{192,224},{224,1... | collective-permute-start | bytes 1572872 | tf_op jit(solution)/shard_map/ppermute | solution.py:290
  26.8 7.9 %collective-permute-start.5 = (s32[2048]{0:T(1024)S(1)}, s32[2048]{0:T(1024)S(1)}, u32[]{:S(2)}, u32[]{:S(2)}) collective-permute-start(s32[2048]{0:T(1024)S(1)} %pad_add_fusion.1), channel_id=1, source_target_pairs={{0,24},{1,25},{2,26},{3,27},{4,28},{5,29},{6,30},{7,31},{8,0},{9,1... | collective-permute-start | bytes 24584 | tf_op jit(solution)/shard_map/ppermute | solution.py:300
  29.8 10.2 %collective-permute-start.8 = (bf16[256,512]{1,0:T(8,128)(2,1)S(1)}, bf16[256,512]{1,0:T(8,128)(2,1)S(1)}, u32[]{:S(2)}, u32[]{:S(2)}) collective-permute-start(bf16[256,512]{1,0:T(8,128)(2,1)S(1)} %slice.193), channel_id=1, source_target_pairs={{0,64},{32,96},{64,128},{96,160},{128,192},{160,224},{192,0},{224,... | collective-permute-start | bytes 786440 | tf_op jit(solution)/shard_map/ppermute | solution.py:285
  31.3 8.7 %collective-permute-start.7 = (bf16[256,512]{1,0:T(8,128)(2,1)S(1)}, bf16[256,512]{1,0:T(8,128)(2,1)S(1)}, u32[]{:S(2)}, u32[]{:S(2)}) collective-permute-start(bf16[256,512]{1,0:T(8,128)(2,1)S(1)} %slice.192), channel_id=1, source_target_pairs={{0,192},{32,224},{64,0},{96,32},{128,64},{160,96},{192,128},{224,1... | collective-permute-start | bytes 786440 | tf_op jit(solution)/shard_map/ppermute | solution.py:285
  31.9 1.2 copy-start.2
  34.7 5.3 %collective-permute-start.6 = (s32[4096]{0:T(1024)S(1)}, s32[4096]{0:T(1024)S(1)}, u32[]{:S(2)}, u32[]{:S(2)}) collective-permute-start(s32[4096]{0:T(1024)S(1)} %pad_add_fusion), channel_id=1, source_target_pairs={{0,16},{1,17},{2,18},{3,19},{4,20},{5,21},{6,22},{7,23},{8,24},{9,... | collective-permute-start | bytes 49160 | tf_op jit(solution)/shard_map/ppermute | solution.py:300
  40.0 3.9 %collective-permute-start.10 = (bf16[256,512]{1,0:T(8,128)(2,1)S(1)}, bf16[256,512]{1,0:T(8,128)(2,1)S(1)}, u32[]{:S(2)}, u32[]{:S(2)}) collective-permute-start(bf16[256,512]{1,0:T(8,128)(2,1)S(1)} %collective-permute-done.8.refs_2_.refs_5_), channel_id=1, source_target_pairs={{0,32},{32,0},{64,96},{96,64},{128,160},{160,128},{192,224},{224,1... | collective-permute-start | bytes 786440 | tf_op jit(solution)/shard_map/ppermute | solution.py:290
  40.0 3.8 %collective-permute-start.9 = (bf16[256,512]{1,0:T(8,128)(2,1)S(1)}, bf16[256,512]{1,0:T(8,128)(2,1)S(1)}, u32[]{:S(2)}, u32[]{:S(2)}) collective-permute-start(bf16[256,512]{1,0:T(8,128)(2,1)S(1)} %collective-permute-done.7.refs_1_.refs_4_), channel_id=1, source_target_pairs={{0,32},{32,0},{64,96},{96,64},{128,160},{160,128},{192,224},{224,1... | collective-permute-start | bytes 786440 | tf_op jit(solution)/shard_map/ppermute | solution.py:290
  43.8 1.7 %copy-start = (bf16[2048,512]{1,0:T(8,128)(2,1)S(1)}, bf16[2048,512]{1,0:T(8,128)(2,1)}, u32[]{:S(2)}) copy-start(bf16[2048,512]{1,0:T(8,128)(2,1)} %k_ref.9) | copy-start | bytes 6291460
  43.9 2.2 %copy-start.1 = (bf16[2048,512]{1,0:T(8,128)(2,1)S(1)}, bf16[2048,512]{1,0:T(8,128)(2,1)}, u32[]{:S(2)}) copy-start(bf16[2048,512]{1,0:T(8,128)(2,1)} %v_ref.9) | copy-start | bytes 6291460
  43.9 2.2 %copy-start.10 = (s32[16]{0:T(128)S(1)}, s32[16]{0:T(128)}, u32[]{:S(2)}) copy-start(s32[16]{0:T(128)} %constant.131.clone.order_ref) | copy-start | bytes 196
  46.1 2.6 %copy-start.9 = (s32[24]{0:T(128)S(1)}, s32[24]{0:T(128)}, u32[]{:S(2)}) copy-start(s32[24]{0:T(128)} %constant.130.clone.order_ref) | copy-start | bytes 292
  48.6 13.5 %copy-start.8 = (s32[32]{0:T(128)S(1)}, s32[32]{0:T(128)}, u32[]{:S(2)}) copy-start(s32[32]{0:T(128)} %constant.132.clone.order_ref) | copy-start | bytes 388
  52.6 14.8 %copy-start.7 = (s32[16]{0:T(128)S(1)}, s32[16]{0:T(128)}, u32[]{:S(2)}) copy-start(s32[16]{0:T(128)} %constant.133.clone.order_ref) | copy-start | bytes 196
  52.6 28.5 %collective-permute-start.14 = (bf16[2,128,512]{2,1,0:T(8,128)(2,1)S(1)}, bf16[2,128,512]{2,1,0:T(8,128)(2,1)S(1)}, u32[]{:S(2)}, u32[]{:S(2)}) collective-permute-start(bf16[2,128,512]{2,1,0:T(8,128)(2,1)S(1)} %get-tuple-element.26), channel_id=1, source_target_pairs={{0,1},{1,2},{2,3},{3,4},{4,5},{5,6},{6,7},{7,0},{8,9},{9,10},{10,1... | collective-permute-start | bytes 786440 | tf_op jit(solution)/shard_map/ppermute | solution.py:295
  54.4 26.5 %collective-permute-start.18 = (bf16[2,128,512]{2,1,0:T(8,128)(2,1)S(1)}, bf16[2,128,512]{2,1,0:T(8,128)(2,1)S(1)}, u32[]{:S(2)}, u32[]{:S(2)}) collective-permute-start(bf16[2,128,512]{2,1,0:T(8,128)(2,1)S(1)} %get-tuple-element.31), channel_id=1, source_target_pairs={{0,7},{1,0},{2,1},{3,2},{4,3},{5,4},{6,5},{7,6},{8,15},{9,8},{10,9... | collective-permute-start | bytes 786440 | tf_op jit(solution)/shard_map/ppermute | solution.py:295
  58.8 26.5 %collective-permute-start.26 = (bf16[4,128,512]{2,1,0:T(8,128)(2,1)S(1)}, bf16[4,128,512]{2,1,0:T(8,128)(2,1)S(1)}, u32[]{:S(2)}, u32[]{:S(2)}) collective-permute-start(bf16[4,128,512]{2,1,0:T(8,128)(2,1)S(1)} %get-tuple-element.35), channel_id=1, source_target_pairs={{0,8},{1,9},{2,10},{3,11},{4,12},{5,13},{6,14},{7,15},{8,16},{9,17... | collective-permute-start | bytes 1572872 | tf_op jit(solution)/shard_map/ppermute | solution.py:300
  58.8 24.5 %collective-permute-start.28 = (bf16[4,128,512]{2,1,0:T(8,128)(2,1)S(1)}, bf16[4,128,512]{2,1,0:T(8,128)(2,1)S(1)}, u32[]{:S(2)}, u32[]{:S(2)}) collective-permute-start(bf16[4,128,512]{2,1,0:T(8,128)(2,1)S(1)} %get-tuple-element.38), channel_id=1, source_target_pairs={{0,24},{1,25},{2,26},{3,27},{4,28},{5,29},{6,30},{7,31},{8,0},{9,1... | collective-permute-start | bytes 1572872 | tf_op jit(solution)/shard_map/ppermute | solution.py:300
  67.2 4.6 %copy-start.6 = (s32[40]{0:T(128)S(1)}, s32[40]{0:T(128)}, u32[]{:S(2)}) copy-start(s32[40]{0:T(128)} %constant.134.clone.order_ref) | copy-start | bytes 484
  81.0 11.5 %collective-permute-start.19 = (bf16[4,128,512]{2,1,0:T(8,128)(2,1)S(1)}, bf16[4,128,512]{2,1,0:T(8,128)(2,1)S(1)}, u32[]{:S(2)}, u32[]{:S(2)}) collective-permute-start(bf16[4,128,512]{2,1,0:T(8,128)(2,1)S(1)} %pad_maximum_fusion.3), channel_id=1, source_target_pairs={{0,7},{1,0},{2,1},{3,2},{4,3},{5,4},{6,5},{7,6},{8,15},{9,8},{10,9... | collective-permute-start | bytes 1572872 | tf_op jit(solution)/shard_map/ppermute | solution.py:295
  81.3 14.8 %collective-permute-start.15 = (bf16[4,128,512]{2,1,0:T(8,128)(2,1)S(1)}, bf16[4,128,512]{2,1,0:T(8,128)(2,1)S(1)}, u32[]{:S(2)}, u32[]{:S(2)}) collective-permute-start(bf16[4,128,512]{2,1,0:T(8,128)(2,1)S(1)} %pad_maximum_fusion.2), channel_id=1, source_target_pairs={{0,1},{1,2},{2,3},{3,4},{4,5},{5,6},{6,7},{7,0},{8,9},{9,10},{10,1... | collective-permute-start | bytes 1572872 | tf_op jit(solution)/shard_map/ppermute | solution.py:295
  83.6 26.8 %collective-permute-start.29 = (bf16[8,128,512]{2,1,0:T(8,128)(2,1)S(1)}, bf16[8,128,512]{2,1,0:T(8,128)(2,1)S(1)}, u32[]{:S(2)}, u32[]{:S(2)}) collective-permute-start(bf16[8,128,512]{2,1,0:T(8,128)(2,1)S(1)} %pad_maximum_fusion.1), channel_id=1, source_target_pairs={{0,24},{1,25},{2,26},{3,27},{4,28},{5,29},{6,30},{7,31},{8,0},{9,1... | collective-permute-start | bytes 3145736 | tf_op jit(solution)/shard_map/ppermute | solution.py:300
  85.5 24.9 %collective-permute-start.27 = (bf16[8,128,512]{2,1,0:T(8,128)(2,1)S(1)}, bf16[8,128,512]{2,1,0:T(8,128)(2,1)S(1)}, u32[]{:S(2)}, u32[]{:S(2)}) collective-permute-start(bf16[8,128,512]{2,1,0:T(8,128)(2,1)S(1)} %pad_maximum_fusion), channel_id=1, source_target_pairs={{0,8},{1,9},{2,10},{3,11},{4,12},{5,13},{6,14},{7,15},{8,16},{9,17... | collective-permute-start | bytes 3145736 | tf_op jit(solution)/shard_map/ppermute | solution.py:300
  92.7 13.6 %collective-permute-start.20 = (bf16[4,128,512]{2,1,0:T(8,128)(2,1)S(1)}, bf16[4,128,512]{2,1,0:T(8,128)(2,1)S(1)}, u32[]{:S(2)}, u32[]{:S(2)}) collective-permute-start(bf16[4,128,512]{2,1,0:T(8,128)(2,1)S(1)} %add_convert_fusion.3), channel_id=1, source_target_pairs={{0,7},{1,0},{2,1},{3,2},{4,3},{5,4},{6,5},{7,6},{8,15},{9,8},{10,9... | collective-permute-start | bytes 1572872 | tf_op jit(solution)/shard_map/ppermute | solution.py:295
  96.2 14.0 %collective-permute-start.16 = (bf16[4,128,512]{2,1,0:T(8,128)(2,1)S(1)}, bf16[4,128,512]{2,1,0:T(8,128)(2,1)S(1)}, u32[]{:S(2)}, u32[]{:S(2)}) collective-permute-start(bf16[4,128,512]{2,1,0:T(8,128)(2,1)S(1)} %add_convert_fusion.5), channel_id=1, source_target_pairs={{0,1},{1,2},{2,3},{3,4},{4,5},{5,6},{6,7},{7,0},{8,9},{9,10},{10,1... | collective-permute-start | bytes 1572872 | tf_op jit(solution)/shard_map/ppermute | solution.py:295
  96.3 59.6 %copy-start.5 = (bf16[512,512]{1,0:T(8,128)(2,1)S(1)}, bf16[512,512]{1,0:T(8,128)(2,1)}, u32[]{:S(2)}) copy-start(bf16[512,512]{1,0:T(8,128)(2,1)} %refs_11_.1) | copy-start | bytes 1572868
  106.4 28.6 %collective-permute-start.21 = (bf16[4,128,512]{2,1,0:T(8,128)(2,1)S(1)}, bf16[4,128,512]{2,1,0:T(8,128)(2,1)S(1)}, u32[]{:S(2)}, u32[]{:S(2)}) collective-permute-start(bf16[4,128,512]{2,1,0:T(8,128)(2,1)S(1)} %add_convert_fusion.2), channel_id=1, source_target_pairs={{0,7},{1,0},{2,1},{3,2},{4,3},{5,4},{6,5},{7,6},{8,15},{9,8},{10,9... | collective-permute-start | bytes 1572872 | tf_op jit(solution)/shard_map/ppermute | solution.py:295
  110.3 24.7 %collective-permute-start.17 = (bf16[4,128,512]{2,1,0:T(8,128)(2,1)S(1)}, bf16[4,128,512]{2,1,0:T(8,128)(2,1)S(1)}, u32[]{:S(2)}, u32[]{:S(2)}) collective-permute-start(bf16[4,128,512]{2,1,0:T(8,128)(2,1)S(1)} %add_convert_fusion.4), channel_id=1, source_target_pairs={{0,1},{1,2},{2,3},{3,4},{4,5},{5,6},{6,7},{7,0},{8,9},{9,10},{10,1... | collective-permute-start | bytes 1572872 | tf_op jit(solution)/shard_map/ppermute | solution.py:295
  110.6 10.4 %collective-permute-start.34 = (bf16[64,512]{1,0:T(8,128)(2,1)S(1)}, bf16[64,512]{1,0:T(8,128)(2,1)S(1)}, u32[]{:S(2)}, u32[]{:S(2)}) collective-permute-start(bf16[64,512]{1,0:T(8,128)(2,1)S(1)} %get-tuple-element.46), channel_id=1, source_target_pairs={{0,7},{1,0},{2,1},{3,2},{4,3},{5,4},{6,5},{7,6},{8,15},{9,8},{10,9... | collective-permute-start | bytes 196616 | tf_op jit(solution)/shard_map/ppermute | solution.py:295
  114.1 10.5 %collective-permute-start.30 = (bf16[64,512]{1,0:T(8,128)(2,1)S(1)}, bf16[64,512]{1,0:T(8,128)(2,1)S(1)}, u32[]{:S(2)}, u32[]{:S(2)}) collective-permute-start(bf16[64,512]{1,0:T(8,128)(2,1)S(1)} %get-tuple-element.48), channel_id=1, source_target_pairs={{0,1},{1,2},{2,3},{3,4},{4,5},{5,6},{6,7},{7,0},{8,9},{9,10},{10,1... | collective-permute-start | bytes 196616 | tf_op jit(solution)/shard_map/ppermute | solution.py:295
  124.7 6.3 %collective-permute-start.31 = (bf16[128,512]{1,0:T(8,128)(2,1)S(1)}, bf16[128,512]{1,0:T(8,128)(2,1)S(1)}, u32[]{:S(2)}, u32[]{:S(2)}) collective-permute-start(bf16[128,512]{1,0:T(8,128)(2,1)S(1)} %pad_maximum_fusion.6), channel_id=1, source_target_pairs={{0,1},{1,2},{2,3},{3,4},{4,5},{5,6},{6,7},{7,0},{8,9},{9,10},{10,1... | collective-permute-start | bytes 393224 | tf_op jit(solution)/shard_map/ppermute | solution.py:295
  124.8 6.3 %collective-permute-start.35 = (bf16[128,512]{1,0:T(8,128)(2,1)S(1)}, bf16[128,512]{1,0:T(8,128)(2,1)S(1)}, u32[]{:S(2)}, u32[]{:S(2)}) collective-permute-start(bf16[128,512]{1,0:T(8,128)(2,1)S(1)} %pad_maximum_fusion.7), channel_id=1, source_target_pairs={{0,7},{1,0},{2,1},{3,2},{4,3},{5,4},{6,5},{7,6},{8,15},{9,8},{10,9... | collective-permute-start | bytes 393224 | tf_op jit(solution)/shard_map/ppermute | solution.py:295
  131.2 15.1 %collective-permute-start.36 = (bf16[128,512]{1,0:T(8,128)(2,1)S(1)}, bf16[128,512]{1,0:T(8,128)(2,1)S(1)}, u32[]{:S(2)}, u32[]{:S(2)}) collective-permute-start(bf16[128,512]{1,0:T(8,128)(2,1)S(1)} %get-tuple-element.43), channel_id=1, source_target_pairs={{0,7},{1,0},{2,1},{3,2},{4,3},{5,4},{6,5},{7,6},{8,15},{9,8},{10,9... | collective-permute-start | bytes 393224 | tf_op jit(solution)/shard_map/ppermute | solution.py:295
  135.0 11.3 %collective-permute-start.32 = (bf16[128,512]{1,0:T(8,128)(2,1)S(1)}, bf16[128,512]{1,0:T(8,128)(2,1)S(1)}, u32[]{:S(2)}, u32[]{:S(2)}) collective-permute-start(bf16[128,512]{1,0:T(8,128)(2,1)S(1)} %get-tuple-element.44), channel_id=1, source_target_pairs={{0,1},{1,2},{2,3},{3,4},{4,5},{5,6},{6,7},{7,0},{8,9},{9,10},{10,1... | collective-permute-start | bytes 393224 | tf_op jit(solution)/shard_map/ppermute | solution.py:295
  135.1 4.4 %collective-permute-start.24 = (bf16[64,512]{1,0:T(8,128)(2,1)S(1)}, bf16[64,512]{1,0:T(8,128)(2,1)S(1)}, u32[]{:S(2)}, u32[]{:S(2)}) collective-permute-start(bf16[64,512]{1,0:T(8,128)(2,1)S(1)} %get-tuple-element.52), channel_id=1, source_target_pairs={{0,24},{1,25},{2,26},{3,27},{4,28},{5,29},{6,30},{7,31},{8,0},{9,1... | collective-permute-start | bytes 196616 | tf_op jit(solution)/shard_map/ppermute | solution.py:300
  137.4 5.5 %collective-permute-start.22 = (bf16[64,512]{1,0:T(8,128)(2,1)S(1)}, bf16[64,512]{1,0:T(8,128)(2,1)S(1)}, u32[]{:S(2)}, u32[]{:S(2)}) collective-permute-start(bf16[64,512]{1,0:T(8,128)(2,1)S(1)} %get-tuple-element.54), channel_id=1, source_target_pairs={{0,8},{1,9},{2,10},{3,11},{4,12},{5,13},{6,14},{7,15},{8,16},{9,17... | collective-permute-start | bytes 196616 | tf_op jit(solution)/shard_map/ppermute | solution.py:300
  142.9 6.9 %collective-permute-start.23 = (bf16[128,512]{1,0:T(8,128)(2,1)S(1)}, bf16[128,512]{1,0:T(8,128)(2,1)S(1)}, u32[]{:S(2)}, u32[]{:S(2)}) collective-permute-start(bf16[128,512]{1,0:T(8,128)(2,1)S(1)} %pad_maximum_fusion.4), channel_id=1, source_target_pairs={{0,8},{1,9},{2,10},{3,11},{4,12},{5,13},{6,14},{7,15},{8,16},{9,17... | collective-permute-start | bytes 393224 | tf_op jit(solution)/shard_map/ppermute | solution.py:300
  143.0 6.8 %collective-permute-start.25 = (bf16[128,512]{1,0:T(8,128)(2,1)S(1)}, bf16[128,512]{1,0:T(8,128)(2,1)S(1)}, u32[]{:S(2)}, u32[]{:S(2)}) collective-permute-start(bf16[128,512]{1,0:T(8,128)(2,1)S(1)} %pad_maximum_fusion.5), channel_id=1, source_target_pairs={{0,24},{1,25},{2,26},{3,27},{4,28},{5,29},{6,30},{7,31},{8,0},{9,1... | collective-permute-start | bytes 393224 | tf_op jit(solution)/shard_map/ppermute | solution.py:300
  146.5 5.8 %collective-permute-start.37 = (bf16[128,512]{1,0:T(8,128)(2,1)S(1)}, bf16[128,512]{1,0:T(8,128)(2,1)S(1)}, u32[]{:S(2)}, u32[]{:S(2)}) collective-permute-start(bf16[128,512]{1,0:T(8,128)(2,1)S(1)} %get-tuple-element.41), channel_id=1, source_target_pairs={{0,7},{1,0},{2,1},{3,2},{4,3},{5,4},{6,5},{7,6},{8,15},{9,8},{10,9... | collective-permute-start | bytes 393224 | tf_op jit(solution)/shard_map/ppermute | solution.py:295
  149.8 6.2 %collective-permute-start.33 = (bf16[128,512]{1,0:T(8,128)(2,1)S(1)}, bf16[128,512]{1,0:T(8,128)(2,1)S(1)}, u32[]{:S(2)}, u32[]{:S(2)}) collective-permute-start(bf16[128,512]{1,0:T(8,128)(2,1)S(1)} %get-tuple-element.42), channel_id=1, source_target_pairs={{0,1},{1,2},{2,3},{3,4},{4,5},{5,6},{6,7},{7,0},{8,9},{9,10},{10,1... | collective-permute-start | bytes 393224 | tf_op jit(solution)/shard_map/ppermute | solution.py:295
  (1 other events, 1.1 us)

commit v3 on v2

--- a/solution.py
+++ b/solution.py
@@ -66,33 +66,42 @@
         at += piece.shape[0]
 
 
-def project_kernel(first, scale, count, *refs):
+def project_kernel(first, scale, count, unrolled, *refs):
     w_ref = refs[0]
     out_ref, rows_ref = refs[-2], refs[-1]
     rows, width = rows_ref.shape
     cuts = width // LANES
-    tile = math.gcd(rows, TILE)
+    tile = math.gcd(refs[1].shape[0], TILE)
+
+    def one_tile(values, to):
+        half = 0.5 * jnp.dot(values, w_ref[:, width:], preferred_element_type=jnp.float32)
+        query = half_silu(half).astype(jnp.bfloat16).astype(jnp.float32) * scale
+        for c in range(cuts):
+            out_ref[pl.ds((first + to) * cuts + c, tile, stride=cuts), :] = query[:, c * LANES : (c + 1) * LANES]
+
+    if unrolled:
+        at = 0
+        for piece in refs[1 : 1 + count]:
+            for begin in range(0, piece.shape[0], tile):
+                one_tile(piece[begin : begin + tile, :], at + begin)
+            at += piece.shape[0]
+        return
     pack_rows(refs[1 : 1 + count], rows_ref)
 
     def step(i, carry):
         begin = pl.multiple_of(i * tile, tile)
-        half = 0.5 * jnp.dot(
-            rows_ref[pl.ds(begin, tile), :], w_ref[:, width:], preferred_element_type=jnp.float32
-        )
-        query = half_silu(half).astype(jnp.bfloat16).astype(jnp.float32) * scale
-        for c in range(cuts):
-            out_ref[pl.ds((first + begin) * cuts + c, tile, stride=cuts), :] = query[:, c * LANES : (c + 1) * LANES]
+        one_tile(rows_ref[pl.ds(begin, tile), :], begin)
         return carry
 
     lax.fori_loop(0, rows // tile, step, 0)
 
 
-def project(table, first, total, pieces, w_in, scale):
+def project(table, first, total, pieces, w_in, scale, unrolled=False):
     width = w_in.shape[0]
     rows = sum(p.shape[0] for p in pieces)
     ins = [w_in, *pieces]
     aliases = {}
-    kernel = functools.partial(project_kernel, first, scale, len(pieces))
+    kernel = functools.partial(project_kernel, first, scale, len(pieces), unrolled)
     if table is not None:
         aliases = {len(ins): 0}
         ins.append(table)
@@ -112,22 +121,18 @@
 
 
 def gate_kernel(count, index_ref, w_ref, *refs):
-    pieces, out_ref, rows_ref, sum_ref = refs[:count], refs[-3], refs[-2], refs[-1]
+    pieces, out_ref = refs[:count], refs[-1]
     cand, width = out_ref.shape
-    tile = math.gcd(rows_ref.shape[0], TILE)
-    pack_rows(pieces, rows_ref)
-    sum_ref[...] = jnp.zeros_like(sum_ref)
+    total = jnp.zeros((cand, width), jnp.float32)
+    first = 0
     index = jnp.broadcast_to(index_ref[...], (LANES, cand)).T[:, :1]
-    ids = lax.broadcasted_iota(jnp.int32, (cand, tile), 1)
-
-    def step(i, carry):
-        begin = pl.multiple_of(i * tile, tile)
-        pick = jnp.where(index - begin == ids, 1.0, 0.0).astype(jnp.bfloat16)
-        sum_ref[...] += jnp.dot(pick, rows_ref[pl.ds(begin, tile), :], preferred_element_type=jnp.float32)
-        return carry
-
-    lax.fori_loop(0, rows_ref.shape[0] // tile, step, 0)
-    normed = sum_ref[...].astype(jnp.bfloat16)
+    for piece in pieces:
+        rows = piece.shape[0]
+        ids = lax.broadcasted_iota(jnp.int32, (cand, rows), 1) + first
+        pick = jnp.where(index == ids, 1.0, 0.0).astype(jnp.bfloat16)
+        total = total + jnp.dot(pick, piece[...], preferred_element_type=jnp.float32)
+        first += rows
+    normed = total.astype(jnp.bfloat16)
     half = 0.5 * jnp.dot(normed, w_ref[:, :width], preferred_element_type=jnp.float32)
     out_ref[...] = half_silu(half).astype(jnp.bfloat16)
 
@@ -141,7 +146,6 @@
         out_shape=jax.ShapeDtypeStruct((cand, width), jnp.bfloat16),
         in_specs=[VMEM] * (2 + len(pieces)),
         out_specs=VMEM,
-        scratch_shapes=[pltpu.VMEM((rows, width), jnp.bfloat16), pltpu.VMEM((cand, width), jnp.float32)],
         cost_estimate=pl.CostEstimate(
             flops=2 * cand * width * (rows + width), bytes_accessed=rows * width * 2, transcendentals=cand * width
         ),
@@ -278,7 +282,6 @@
     g, s = lax.axis_index("grp"), lax.axis_index("shard")
     part_rows = cand_table.shape[0]
     total_rows = groups * part_rows
-    half_part = part_rows // 2
     cuts = width // LANES
 
     def x_shift(value, k):
@@ -311,8 +314,7 @@
         wanted = jnp.concatenate([wanted, z_shift(wanted, -step)])
         step *= 2
     wanted, ahead, behind = lax.optimization_barrier((wanted, ahead, behind))
-    far_top = x_shift(ahead[:half_part], -1)
-    far_bottom = x_shift(behind[half_part:], 1)
+    far = x_shift(ahead, -1)
     ahead_rows = [ahead, swap(ahead)]
     behind_rows = [behind, swap(behind)]
     step = 1
@@ -347,15 +349,16 @@
     table = project(None, 0, total_rows, near_rows, w_in, scale)
     table = project(table, 1 * chip, total_rows, ahead_rows, w_in, scale)
     table = project(table, 3 * chip, total_rows, behind_rows, w_in, scale)
-    far_rows = [far_top, far_bottom, swap(far_top), swap(far_bottom)]
-    table = project(table, 2 * chip, total_rows, far_rows, w_in, scale)
+    far_rows = [far, swap(far)]
+    table = project(table, 2 * chip, total_rows, far_rows, w_in, scale, unrolled=True)
 
     half = cand // 2
     half_z = nz // 2
     z_of = lambda dz, dys=range(NY): [(dy, dz, 0) for dy in dys]
     y_of = lambda dy, dzs=range(nz): [(dy, dz, half) for dz in dzs]
     calls = [
-        [z_of(4, (0, 1)), z_of(4, (2, 3)), y_of(2, range(half_z)), y_of(2, range(half_z, nz))],
+        [z_of(4, (0, 1)), z_of(4, (2, 3))],
+        [y_of(2, range(half_z)), y_of(2, range(half_z, nz))],
         [z_of(3), z_of(5)],
         [y_of(1), y_of(3)],
         [z_of(2), z_of(6)],

time: 157 us -> 154 us (0.981)
  waiting for transfers between devices: 48.2 us -> 45.4 us
    ppermute x19, waiting for transfers between devices: 38.1 us -> 35.4 us  [z_shift(): lax.ppermute(value, 'shard', [(y * nz + z, y * nz + (z + k) % nz) for y i...]
    pallas_call x1, Pallas kernels: 5.1 us -> 2.77 us  [gate_rows(): pl.pallas_call(functools.partial(gate_kernel, len(pieces)), out_shape=jax...]
    pallas_call x5 -> x6, Pallas kernels: 25.1 us -> 26 us  [attend(): pl.pallas_call(functools.partial(attend_kernel, tuple(sizes), math.gcd(ro...]
    ppermute x4 -> x3, starting transfers between devices: 4.44 us -> 4.23 us  [x_shift(): lax.ppermute(value, 'grp', [(x * CORES + c, (x + k) % nx * CORES + c) for...]
  transfers between devices with their start and end apart: 38 -> 36, of which waited for: 13 -> 14; matrix products, arithmetic and copies ran while one was open for 4% -> 4% of each run, Pallas kernels for 18% -> 21%
where the time goes in v3:
time: 154 us
  starting transfers between devices  60.9 us (40%)
  waiting for transfers between devices  45.4 us (29%)
  Pallas kernels  37.4 us (24%)
  other arithmetic  6.56 us (4%)
  local copies, waits for them, and re-layouts  2.79 us (2%)
    ppermute x19, starting transfers between devices, z_shift(): lax.ppermute(value, 'shard', [(y * nz + z, y * nz + (z + k) % nz) for y i...  41.3 us
    ppermute x19, waiting for transfers between devices, z_shift(): lax.ppermute(value, 'shard', [(y * nz + z, y * nz + (z + k) % nz) for y i...  35.4 us
    pallas_call x6, Pallas kernels, attend(): pl.pallas_call(functools.partial(attend_kernel, tuple(sizes), math.gcd(ro...  26 us
    ppermute x10, starting transfers between devices, y_shift(): lax.ppermute(value, 'shard', [(y * nz + z, (y + k) % NY * nz + z) for y i...  15.1 us
    ppermute x10, waiting for transfers between devices, y_shift(): lax.ppermute(value, 'shard', [(y * nz + z, (y + k) % NY * nz + z) for y i...  8.88 us
    pallas_call x4, Pallas kernels, project(): pl.pallas_call(kernel, out_shape=jax.ShapeDtypeStruct((total * width // L...  6.88 us
    ppermute x3, starting transfers between devices, x_shift(): lax.ppermute(value, 'grp', [(x * CORES + c, (x + k) % nx * CORES + c) for...  4.23 us
  transfers between devices with their start and end apart: 36, of which 14 were waited for; matrix products, arithmetic and copies ran while one was open for 4% of the time, Pallas kernels for 21%

profile of v3, /device:TPU:2, one launch (start us, length us, event | category | flops | bytes accessed | tf_op | source)
XLA Modules:
  0.0 153.6 jit_solution(11045605423845906761)
XLA Ops:
  0.0 1.1 copy-done.4
  1.7 1.6 %collective-permute-start.4 = (bf16[512,512]{1,0:T(8,128)(2,1)S(1)}, bf16[512,512]{1,0:T(8,128)(2,1)S(1)}, u32[]{:S(2)}, u32[]{:S(2)}) collective-permute-start(bf16[512,512]{1,0:T(8,128)(2,1)S(1)} %norm.1.refs_1_.refs_0_), channel_id=1, source_target_pairs={{0,64},{32,96},{64,128},{96,160},{128,192},{160,224},{192,0},{224,... | collective-permute-start | bytes 1572872 | tf_op jit(solution)/shard_map/ppermute | solution.py:288
  4.1 5.5 %collective-permute-start = (s32[256]{0:T(256)}, s32[256]{0:T(256)S(1)}, u32[]{:S(2)}, u32[]{:S(2)}) collective-permute-start(s32[256]{0:T(256)} %param.14), channel_id=1, source_target_pairs={{0,7},{1,0},{2,1},{3,2},{4,3},{5,4},{6,5},{7,6},{8,15},{9,8},{10,9... | collective-permute-start | bytes 3080 | tf_op jit(solution)/shard_map/ppermute | solution.py:298
  9.7 0.9 convert_reduce_fusion
  11.9 2.7 %collective-permute-start.1 = (s32[512]{0:T(512)S(1)}, s32[512]{0:T(512)S(1)}, u32[]{:S(2)}, u32[]{:S(2)}) collective-permute-start(s32[512]{0:T(512)S(1)} %pad_add_fusion.3), channel_id=1, source_target_pairs={{0,6},{1,7},{2,0},{3,1},{4,2},{5,3},{6,4},{7,5},{8,14},{9,15},{10,... | collective-permute-start | bytes 6152 | tf_op jit(solution)/shard_map/ppermute | solution.py:298
  15.3 1.1 collective-permute-done.1
  17.1 3.6 %collective-permute-start.2 = (s32[1024]{0:T(1024)S(1)}, s32[1024]{0:T(1024)S(1)}, u32[]{:S(2)}, u32[]{:S(2)}) collective-permute-start(s32[1024]{0:T(1024)S(1)} %pad_add_fusion.2), channel_id=1, source_target_pairs={{0,4},{1,5},{2,6},{3,7},{4,0},{5,1},{6,2},{7,3},{8,12},{9,13},{10,... | collective-permute-start | bytes 12296 | tf_op jit(solution)/shard_map/ppermute | solution.py:298
  20.7 3.8 %collective-permute-done.2 = s32[1024]{0:T(1024)S(1)} collective-permute-done((s32[1024]{0:T(1024)S(1)}, s32[1024]{0:T(1024)S(1)}, u32[]{:S(2)}, u32[]{:S(2)}) %collective-permute-start.2) | collective-permute-done | bytes 4128 | tf_op jit(solution)/shard_map/ppermute | solution.py:298
  25.3 1.8 %collective-permute-start.7 = (bf16[512,512]{1,0:T(8,128)(2,1)S(1)}, bf16[512,512]{1,0:T(8,128)(2,1)}, u32[]{:S(2)}, u32[]{:S(2)}) collective-permute-start(bf16[512,512]{1,0:T(8,128)(2,1)S(1)} %collective-permute-done.3.refs_1_.refs_2_), channel_id=1, source_target_pairs={{0,192},{32,224},{64,0},{96,32},{128,64},{160,96},{192,128},{224,1... | collective-permute-start | bytes 1572872 | tf_op jit(solution)/shard_map/ppermute | solution.py:288
  28.0 3.1 %collective-permute-start.5 = (s32[2048]{0:T(1024)S(1)}, s32[2048]{0:T(1024)S(1)}, u32[]{:S(2)}, u32[]{:S(2)}) collective-permute-start(s32[2048]{0:T(1024)S(1)} %pad_add_fusion.1), channel_id=1, source_target_pairs={{0,24},{1,25},{2,26},{3,27},{4,28},{5,29},{6,30},{7,31},{8,0},{9,1... | collective-permute-start | bytes 24584 | tf_op jit(solution)/shard_map/ppermute | solution.py:303
  31.2 1.2 copy-done.2
  32.5 1.6 %project.4.refs_3_ = f32[16384,128]{1,0:T(8,128)S(1)} custom-call(bf16[512,1024]{1,0:T(8,128)(2,1)S(1)} %copy-done.2, bf16[512,512]{1,0:T(8,128)(2,1)S(1)} %norm.1.refs_1_.refs_0_, bf16[512,512]{1,0:T(8,128)(2,1)S(1)} %collective-permute-done.11.refs_2_.refs_1_), custom_call_target="tpu_custom_call" | custom-call | flops 536870912 | bytes 3145728 | tf_op jit(solution)/shard_map/project/pallas_call | solution.py:108
  34.9 1.1 collective-permute-done.7.refs_1_.refs_4_
  36.0 3.4 %collective-permute-done.6 = s32[4096]{0:T(1024)S(1)} collective-permute-done((s32[4096]{0:T(1024)S(1)}, s32[4096]{0:T(1024)S(1)}, u32[]{:S(2)}, u32[]{:S(2)}) %collective-permute-start.6) | collective-permute-done | bytes 16416 | tf_op jit(solution)/shard_map/ppermute | solution.py:303
  39.5 1.6 %project.5.refs_3_ = f32[16384,128]{1,0:T(8,128)S(1)} custom-call(bf16[512,1024]{1,0:T(8,128)(2,1)S(1)} %copy-done.3, bf16[512,512]{1,0:T(8,128)(2,1)S(1)} %collective-permute-done.3.refs_1_.refs_2_, bf16[512,512]{1,0:T(8,128)(2,1)S(1)} %collective-permute-done.10.refs_2_.refs_3_, f32[16384,128]{1,0:T(8,128)S(1)} %project.4.refs_3_), custom_call_target="tpu_custom_call", output_to_operand_aliasing={{}: (3, {})} | custom-call | flops 536870912 | bytes 3145728 | tf_op jit(solution)/shard_map/project/pallas_call | solution.py:108
  41.1 1.6 %project.6.refs_3_ = f32[16384,128]{1,0:T(8,128)S(1)} custom-call(bf16[512,1024]{1,0:T(8,128)(2,1)S(1)} %copy-done.3, bf16[512,512]{1,0:T(8,128)(2,1)S(1)} %collective-permute-done.4.refs_1_.refs_6_, bf16[512,512]{1,0:T(8,128)(2,1)S(1)} %collective-permute-done.9.refs_2_.refs_7_, f32[16384,128]{1,0:T(8,128)S(1)} %project.5.refs_3_), custom_call_target="tpu_custom_call", output_to_operand_aliasing={{}: (3, {})} | custom-call | flops 536870912 | bytes 3145728 | tf_op jit(solution)/shard_map/project/pallas_call | solution.py:108
  42.7 2.1 %project.7.table_ref = f32[16384,128]{1,0:T(8,128)S(1)} custom-call(bf16[512,1024]{1,0:T(8,128)(2,1)S(1)} %copy-done.3, bf16[512,512]{1,0:T(8,128)(2,1)} %collective-permute-done.7.refs_1_.refs_4_, bf16[512,512]{1,0:T(8,128)(2,1)S(1)} %collective-permute-done.8.refs_2_.refs_5_, f32[16384,128]{1,0:T(8,128)S(1)} %project.6.refs_3_), custom_call_target="tpu_custom_call", output_to_operand_aliasing={{}: (3, {})} | custom-call | flops 536870912 | bytes 3145728 | tf_op jit(solution)/shard_map/project/pallas_call | solution.py:108
  45.1 1.3 attend.7
  46.4 2.4 %collective-permute-start.12 = (bf16[2,128,512]{2,1,0:T(8,128)(2,1)S(1)}, bf16[2,128,512]{2,1,0:T(8,128)(2,1)S(1)}, u32[]{:S(2)}, u32[]{:S(2)}) collective-permute-start(bf16[2,128,512]{2,1,0:T(8,128)(2,1)S(1)} %get-tuple-element.26), channel_id=1, source_target_pairs={{0,1},{1,2},{2,3},{3,4},{4,5},{5,6},{6,7},{7,0},{8,9},{9,10},{10,1... | collective-permute-start | bytes 786440 | tf_op jit(solution)/shard_map/ppermute | solution.py:298
  48.8 4.2 %collective-permute-start.16 = (bf16[2,128,512]{2,1,0:T(8,128)(2,1)S(1)}, bf16[2,128,512]{2,1,0:T(8,128)(2,1)S(1)}, u32[]{:S(2)}, u32[]{:S(2)}) collective-permute-start(bf16[2,128,512]{2,1,0:T(8,128)(2,1)S(1)} %get-tuple-element.31), channel_id=1, source_target_pairs={{0,7},{1,0},{2,1},{3,2},{4,3},{5,4},{6,5},{7,6},{8,15},{9,8},{10,9... | collective-permute-start | bytes 786440 | tf_op jit(solution)/shard_map/ppermute | solution.py:298
  53.0 3.6 %attend.10 = (bf16[4,128,512]{2,1,0:T(8,128)(2,1)S(1)}, bf16[4,128,512]{2,1,0:T(8,128)(2,1)S(1)}) custom-call(s32[8192]{0:T(1024)S(1)} %fusion.24.index_ref, s32[32]{0:T(128)S(1)} %convert_reduce_fusion.1.count_ref, s32[64]{0:T(128)S(1)} %select_reduce_fusion.block_ref, s32[16]{0:T(128)S(1)} %copy-done.10, f32[16384,128]{1,0:T(8,128)S(1)} %project.7.table_ref, ...), custom_call_target="tpu_custom_call" | custom-call | flops 536870912 | bytes 2097152 | tf_op jit(solution)/shard_map/attend/pallas_call | solution.py:221
  56.7 3.2 %collective-permute-start.26 = (bf16[4,128,512]{2,1,0:T(8,128)(2,1)S(1)}, bf16[4,128,512]{2,1,0:T(8,128)(2,1)S(1)}, u32[]{:S(2)}, u32[]{:S(2)}) collective-permute-start(bf16[4,128,512]{2,1,0:T(8,128)(2,1)S(1)} %get-tuple-element.38), channel_id=1, source_target_pairs={{0,24},{1,25},{2,26},{3,27},{4,28},{5,29},{6,30},{7,31},{8,0},{9,1... | collective-permute-start | bytes 1572872 | tf_op jit(solution)/shard_map/ppermute | solution.py:303
  59.9 2.5 %attend.8 = (bf16[4,128,512]{2,1,0:T(8,128)(2,1)S(1)}, bf16[4,128,512]{2,1,0:T(8,128)(2,1)S(1)}) custom-call(s32[8192]{0:T(1024)S(1)} %fusion.24.index_ref, s32[32]{0:T(128)S(1)} %convert_reduce_fusion.1.count_ref, s32[64]{0:T(128)S(1)} %select_reduce_fusion.block_ref, s32[16]{0:T(128)S(1)} %copy-done.9, f32[16384,128]{1,0:T(8,128)S(1)} %project.7.table_ref, ...), custom_call_target="tpu_custom_call" | custom-call | flops 536870912 | bytes 2097152 | tf_op jit(solution)/shard_map/attend/pallas_call | solution.py:221
  62.5 5.2 %attend.11 = (bf16[8,128,512]{2,1,0:T(8,128)(2,1)S(1)}, bf16[8,128,512]{2,1,0:T(8,128)(2,1)S(1)}) custom-call(s32[8192]{0:T(1024)S(1)} %fusion.24.index_ref, s32[32]{0:T(128)S(1)} %convert_reduce_fusion.1.count_ref, s32[64]{0:T(128)S(1)} %select_reduce_fusion.block_ref, s32[32]{0:T(128)S(1)} %copy-done.8, f32[16384,128]{1,0:T(8,128)S(1)} %project.7.table_ref, ...), custom_call_target="tpu_custom_call" | custom-call | flops 1073741824 | bytes 4194304 | tf_op jit(solution)/shard_map/attend/pallas_call | solution.py:221
  67.8 4.5 %attend.9 = (bf16[4,128,512]{2,1,0:T(8,128)(2,1)S(1)}, bf16[4,128,512]{2,1,0:T(8,128)(2,1)S(1)}) custom-call(s32[8192]{0:T(1024)S(1)} %fusion.24.index_ref, s32[32]{0:T(128)S(1)} %convert_reduce_fusion.1.count_ref, s32[64]{0:T(128)S(1)} %select_reduce_fusion.block_ref, s32[16]{0:T(128)S(1)} %copy-done.7, f32[16384,128]{1,0:T(8,128)S(1)} %project.7.table_ref, ...), custom_call_target="tpu_custom_call" | custom-call | flops 536870912 | bytes 2097152 | tf_op jit(solution)/shard_map/attend/pallas_call | solution.py:221
  72.3 9.0 %attend.6 = (bf16[4,128,512]{2,1,0:T(8,128)(2,1)S(1)}, bf16[4,128,512]{2,1,0:T(8,128)(2,1)S(1)}, bf16[4,128,512]{2,1,0:T(8,128)(2,1)S(1)}, bf16[8,128,512]{2,1,0:T(8,128)(2,1)S(1)}) custom-call(s32[8192]{0:T(1024)S(1)} %fusion.24.index_ref, s32[32]{0:T(128)S(1)} %convert_reduce_fusion.1.count_ref, s32[64]{0:T(128)S(1)} %select_reduce_fusion.block_ref, ...), custom_call_target="tpu_custom_call" | custom-call | flops 1342177280 | bytes 5242880 | tf_op jit(solution)/shard_map/attend/pallas_call | solution.py:221
  81.8 1.9 %collective-permute-start.13 = (bf16[4,128,512]{2,1,0:T(8,128)(2,1)S(1)}, bf16[4,128,512]{2,1,0:T(8,128)(2,1)S(1)}, u32[]{:S(2)}, u32[]{:S(2)}) collective-permute-start(bf16[4,128,512]{2,1,0:T(8,128)(2,1)S(1)} %pad_maximum_fusion.2), channel_id=1, source_target_pairs={{0,1},{1,2},{2,3},{3,4},{4,5},{5,6},{6,7},{7,0},{8,9},{9,10},{10,1... | collective-permute-start | bytes 1572872 | tf_op jit(solution)/shard_map/ppermute | solution.py:298
  84.0 1.1 collective-permute-start.27
  85.4 1.1 collective-permute-start.25
  86.4 5.6 %collective-permute-done.17 = bf16[4,128,512]{2,1,0:T(8,128)(2,1)S(1)} collective-permute-done((bf16[4,128,512]{2,1,0:T(8,128)(2,1)S(1)}, bf16[4,128,512]{2,1,0:T(8,128)(2,1)S(1)}, u32[]{:S(2)}, u32[]{:S(2)}) %collective-permute-start.17) | collective-permute-done | bytes 524320 | tf_op jit(solution)/shard_map/ppermute | solution.py:298
  92.2 3.0 %collective-permute-start.18 = (bf16[4,128,512]{2,1,0:T(8,128)(2,1)S(1)}, bf16[4,128,512]{2,1,0:T(8,128)(2,1)S(1)}, u32[]{:S(2)}, u32[]{:S(2)}) collective-permute-start(bf16[4,128,512]{2,1,0:T(8,128)(2,1)S(1)} %add_convert_fusion.3), channel_id=1, source_target_pairs={{0,7},{1,0},{2,1},{3,2},{4,3},{5,4},{6,5},{7,6},{8,15},{9,8},{10,9... | collective-permute-start | bytes 1572872 | tf_op jit(solution)/shard_map/ppermute | solution.py:298
  95.4 2.8 %gate.1.refs_10_ = bf16[256,512]{1,0:T(8,128)(2,1)S(1)} custom-call(s32[1,256]{1,0:T(1,128)S(1)} %bitcast.136, bf16[512,1024]{1,0:T(8,128)(2,1)S(1)} %copy-done.3, bf16[512,512]{1,0:T(8,128)(2,1)S(1)} %norm.1.refs_1_.refs_0_, bf16[512,512]{1,0:T(8,128)(2,1)S(1)} %collective-permute-done.11.refs_2_.refs_1_, ...), custom_call_target="tpu_custom_call" | custom-call | flops 1207959552 | bytes 4194304 | tf_op jit(solution)/shard_map/gate/pallas_call | solution.py:144
  98.2 5.6 %collective-permute-done.18 = bf16[4,128,512]{2,1,0:T(8,128)(2,1)S(1)} collective-permute-done((bf16[4,128,512]{2,1,0:T(8,128)(2,1)S(1)}, bf16[4,128,512]{2,1,0:T(8,128)(2,1)S(1)}, u32[]{:S(2)}, u32[]{:S(2)}) %collective-permute-start.18) | collective-permute-done | bytes 524320 | tf_op jit(solution)/shard_map/ppermute | solution.py:298
  104.0 3.8 %collective-permute-start.19 = (bf16[4,128,512]{2,1,0:T(8,128)(2,1)S(1)}, bf16[4,128,512]{2,1,0:T(8,128)(2,1)S(1)}, u32[]{:S(2)}, u32[]{:S(2)}) collective-permute-start(bf16[4,128,512]{2,1,0:T(8,128)(2,1)S(1)} %add_convert_fusion.2), channel_id=1, source_target_pairs={{0,7},{1,0},{2,1},{3,2},{4,3},{5,4},{6,5},{7,6},{8,15},{9,8},{10,9... | collective-permute-start | bytes 1572872 | tf_op jit(solution)/shard_map/ppermute | solution.py:298
  108.2 3.5 %collective-permute-start.32 = (bf16[64,512]{1,0:T(8,128)(2,1)S(1)}, bf16[64,512]{1,0:T(8,128)(2,1)S(1)}, u32[]{:S(2)}, u32[]{:S(2)}) collective-permute-start(bf16[64,512]{1,0:T(8,128)(2,1)S(1)} %get-tuple-element.46), channel_id=1, source_target_pairs={{0,7},{1,0},{2,1},{3,2},{4,3},{5,4},{6,5},{7,6},{8,15},{9,8},{10,9... | collective-permute-start | bytes 196616 | tf_op jit(solution)/shard_map/ppermute | solution.py:298
  111.7 5.4 %collective-permute-done.32 = bf16[64,512]{1,0:T(8,128)(2,1)S(1)} collective-permute-done((bf16[64,512]{1,0:T(8,128)(2,1)S(1)}, bf16[64,512]{1,0:T(8,128)(2,1)S(1)}, u32[]{:S(2)}, u32[]{:S(2)}) %collective-permute-start.32) | collective-permute-done | bytes 65568 | tf_op jit(solution)/shard_map/ppermute | solution.py:298
  117.0 4.3 %collective-permute-done.28 = bf16[64,512]{1,0:T(8,128)(2,1)S(1)} collective-permute-done((bf16[64,512]{1,0:T(8,128)(2,1)S(1)}, bf16[64,512]{1,0:T(8,128)(2,1)S(1)}, u32[]{:S(2)}, u32[]{:S(2)}) %collective-permute-start.28) | collective-permute-done | bytes 65568 | tf_op jit(solution)/shard_map/ppermute | solution.py:298
  121.5 3.3 %collective-permute-start.33 = (bf16[128,512]{1,0:T(8,128)(2,1)S(1)}, bf16[128,512]{1,0:T(8,128)(2,1)S(1)}, u32[]{:S(2)}, u32[]{:S(2)}) collective-permute-start(bf16[128,512]{1,0:T(8,128)(2,1)S(1)} %pad_maximum_fusion.7), channel_id=1, source_target_pairs={{0,7},{1,0},{2,1},{3,2},{4,3},{5,4},{6,5},{7,6},{8,15},{9,8},{10,9... | collective-permute-start | bytes 393224 | tf_op jit(solution)/shard_map/ppermute | solution.py:298
  124.8 2.8 %collective-permute-done.29 = bf16[128,512]{1,0:T(8,128)(2,1)S(1)} collective-permute-done((bf16[128,512]{1,0:T(8,128)(2,1)S(1)}, bf16[128,512]{1,0:T(8,128)(2,1)S(1)}, u32[]{:S(2)}, u32[]{:S(2)}) %collective-permute-start.29) | collective-permute-done | bytes 131104 | tf_op jit(solution)/shard_map/ppermute | solution.py:298
  127.8 3.5 %collective-permute-start.34 = (bf16[128,512]{1,0:T(8,128)(2,1)S(1)}, bf16[128,512]{1,0:T(8,128)(2,1)S(1)}, u32[]{:S(2)}, u32[]{:S(2)}) collective-permute-start(bf16[128,512]{1,0:T(8,128)(2,1)S(1)} %get-tuple-element.43), channel_id=1, source_target_pairs={{0,7},{1,0},{2,1},{3,2},{4,3},{5,4},{6,5},{7,6},{8,15},{9,8},{10,9... | collective-permute-start | bytes 393224 | tf_op jit(solution)/shard_map/ppermute | solution.py:298
  131.5 2.3 %collective-permute-start.22 = (bf16[64,512]{1,0:T(8,128)(2,1)S(1)}, bf16[64,512]{1,0:T(8,128)(2,1)S(1)}, u32[]{:S(2)}, u32[]{:S(2)}) collective-permute-start(bf16[64,512]{1,0:T(8,128)(2,1)S(1)} %get-tuple-element.52), channel_id=1, source_target_pairs={{0,24},{1,25},{2,26},{3,27},{4,28},{5,29},{6,30},{7,31},{8,0},{9,1... | collective-permute-start | bytes 196616 | tf_op jit(solution)/shard_map/ppermute | solution.py:303
  133.8 2.5 %collective-permute-done.22 = bf16[64,512]{1,0:T(8,128)(2,1)S(1)} collective-permute-done((bf16[64,512]{1,0:T(8,128)(2,1)S(1)}, bf16[64,512]{1,0:T(8,128)(2,1)S(1)}, u32[]{:S(2)}, u32[]{:S(2)}) %collective-permute-start.22) | collective-permute-done | bytes 65568 | tf_op jit(solution)/shard_map/ppermute | solution.py:303
  136.2 3.0 %collective-permute-done.20 = bf16[64,512]{1,0:T(8,128)(2,1)S(1)} collective-permute-done((bf16[64,512]{1,0:T(8,128)(2,1)S(1)}, bf16[64,512]{1,0:T(8,128)(2,1)S(1)}, u32[]{:S(2)}, u32[]{:S(2)}) %collective-permute-start.20) | collective-permute-done | bytes 65568 | tf_op jit(solution)/shard_map/ppermute | solution.py:303
  139.4 3.3 %collective-permute-start.23 = (bf16[128,512]{1,0:T(8,128)(2,1)S(1)}, bf16[128,512]{1,0:T(8,128)(2,1)S(1)}, u32[]{:S(2)}, u32[]{:S(2)}) collective-permute-start(bf16[128,512]{1,0:T(8,128)(2,1)S(1)} %pad_maximum_fusion.5), channel_id=1, source_target_pairs={{0,24},{1,25},{2,26},{3,27},{4,28},{5,29},{6,30},{7,31},{8,0},{9,1... | collective-permute-start | bytes 393224 | tf_op jit(solution)/shard_map/ppermute | solution.py:303
  142.9 3.3 %collective-permute-start.35 = (bf16[128,512]{1,0:T(8,128)(2,1)S(1)}, bf16[128,512]{1,0:T(8,128)(2,1)S(1)}, u32[]{:S(2)}, u32[]{:S(2)}) collective-permute-start(bf16[128,512]{1,0:T(8,128)(2,1)S(1)} %get-tuple-element.41), channel_id=1, source_target_pairs={{0,7},{1,0},{2,1},{3,2},{4,3},{5,4},{6,5},{7,6},{8,15},{9,8},{10,9... | collective-permute-start | bytes 393224 | tf_op jit(solution)/shard_map/ppermute | solution.py:298
  146.2 2.5 %collective-permute-done.35.refs_9_ = bf16[128,512]{1,0:T(8,128)(2,1)S(1)} collective-permute-done((bf16[128,512]{1,0:T(8,128)(2,1)S(1)}, bf16[128,512]{1,0:T(8,128)(2,1)S(1)}, u32[]{:S(2)}, u32[]{:S(2)}) %collective-permute-start.35) | collective-permute-done | bytes 131104 | tf_op jit(solution)/shard_map/ppermute | solution.py:298
  148.7 3.7 %collective-permute-done.31.refs_8_ = bf16[128,512]{1,0:T(8,128)(2,1)S(1)} collective-permute-done((bf16[128,512]{1,0:T(8,128)(2,1)S(1)}, bf16[128,512]{1,0:T(8,128)(2,1)S(1)}, u32[]{:S(2)}, u32[]{:S(2)}) %collective-permute-start.31) | collective-permute-done | bytes 131104 | tf_op jit(solution)/shard_map/ppermute | solution.py:298
  152.3 1.3 finish.1
  (105 shorter events, 9.9 us)
Async XLA Ops:
  0.0 39.5 %copy-start.3 = (bf16[512,1024]{1,0:T(8,128)(2,1)S(1)}, bf16[512,1024]{1,0:T(8,128)(2,1)}, u32[]{:S(2)}) copy-start(bf16[512,1024]{1,0:T(8,128)(2,1)} %w_ref.1) | copy-start | bytes 3145732
  0.0 1.1 copy-start.4
  1.6 29.6 %collective-permute-start.11 = (bf16[512,512]{1,0:T(8,128)(2,1)S(1)}, bf16[512,512]{1,0:T(8,128)(2,1)S(1)}, u32[]{:S(2)}, u32[]{:S(2)}) collective-permute-start(bf16[512,512]{1,0:T(8,128)(2,1)S(1)} %norm.1.refs_1_.refs_0_), channel_id=1, source_target_pairs={{0,32},{32,0},{64,96},{96,64},{128,160},{160,128},{192,224},{224,1... | collective-permute-start | bytes 1572872 | tf_op jit(solution)/shard_map/ppermute | solution.py:293
  1.7 23.5 %collective-permute-start.4 = (bf16[512,512]{1,0:T(8,128)(2,1)S(1)}, bf16[512,512]{1,0:T(8,128)(2,1)S(1)}, u32[]{:S(2)}, u32[]{:S(2)}) collective-permute-start(bf16[512,512]{1,0:T(8,128)(2,1)S(1)} %norm.1.refs_1_.refs_0_), channel_id=1, source_target_pairs={{0,64},{32,96},{64,128},{96,160},{128,192},{160,224},{192,0},{224,... | collective-permute-start | bytes 1572872 | tf_op jit(solution)/shard_map/ppermute | solution.py:288
  3.3 22.0 %collective-permute-start.3 = (bf16[512,512]{1,0:T(8,128)(2,1)S(1)}, bf16[512,512]{1,0:T(8,128)(2,1)S(1)}, u32[]{:S(2)}, u32[]{:S(2)}) collective-permute-start(bf16[512,512]{1,0:T(8,128)(2,1)S(1)} %norm.1.refs_1_.refs_0_), channel_id=1, source_target_pairs={{0,192},{32,224},{64,0},{96,32},{128,64},{160,96},{192,128},{224,1... | collective-permute-start | bytes 1572872 | tf_op jit(solution)/shard_map/ppermute | solution.py:288
  4.1 7.1 %collective-permute-start = (s32[256]{0:T(256)}, s32[256]{0:T(256)S(1)}, u32[]{:S(2)}, u32[]{:S(2)}) collective-permute-start(s32[256]{0:T(256)} %param.14), channel_id=1, source_target_pairs={{0,7},{1,0},{2,1},{3,2},{4,3},{5,4},{6,5},{7,6},{8,15},{9,8},{10,9... | collective-permute-start | bytes 3080 | tf_op jit(solution)/shard_map/ppermute | solution.py:298
  11.9 4.5 %collective-permute-start.1 = (s32[512]{0:T(512)S(1)}, s32[512]{0:T(512)S(1)}, u32[]{:S(2)}, u32[]{:S(2)}) collective-permute-start(s32[512]{0:T(512)S(1)} %pad_add_fusion.3), channel_id=1, source_target_pairs={{0,6},{1,7},{2,0},{3,1},{4,2},{5,3},{6,4},{7,5},{8,14},{9,15},{10,... | collective-permute-start | bytes 6152 | tf_op jit(solution)/shard_map/ppermute | solution.py:298
  17.1 7.5 %collective-permute-start.2 = (s32[1024]{0:T(1024)S(1)}, s32[1024]{0:T(1024)S(1)}, u32[]{:S(2)}, u32[]{:S(2)}) collective-permute-start(s32[1024]{0:T(1024)S(1)} %pad_add_fusion.2), channel_id=1, source_target_pairs={{0,4},{1,5},{2,6},{3,7},{4,0},{5,1},{6,2},{7,3},{8,12},{9,13},{10,... | collective-permute-start | bytes 12296 | tf_op jit(solution)/shard_map/ppermute | solution.py:298
  25.3 10.7 %collective-permute-start.7 = (bf16[512,512]{1,0:T(8,128)(2,1)S(1)}, bf16[512,512]{1,0:T(8,128)(2,1)}, u32[]{:S(2)}, u32[]{:S(2)}) collective-permute-start(bf16[512,512]{1,0:T(8,128)(2,1)S(1)} %collective-permute-done.3.refs_1_.refs_2_), channel_id=1, source_target_pairs={{0,192},{32,224},{64,0},{96,32},{128,64},{160,96},{192,128},{224,1... | collective-permute-start | bytes 1572872 | tf_op jit(solution)/shard_map/ppermute | solution.py:288
  27.9 11.6 %collective-permute-start.10 = (bf16[512,512]{1,0:T(8,128)(2,1)S(1)}, bf16[512,512]{1,0:T(8,128)(2,1)S(1)}, u32[]{:S(2)}, u32[]{:S(2)}) collective-permute-start(bf16[512,512]{1,0:T(8,128)(2,1)S(1)} %collective-permute-done.3.refs_1_.refs_2_), channel_id=1, source_target_pairs={{0,32},{32,0},{64,96},{96,64},{128,160},{160,128},{192,224},{224,1... | collective-permute-start | bytes 1572872 | tf_op jit(solution)/shard_map/ppermute | solution.py:293
  28.0 6.1 %collective-permute-start.5 = (s32[2048]{0:T(1024)S(1)}, s32[2048]{0:T(1024)S(1)}, u32[]{:S(2)}, u32[]{:S(2)}) collective-permute-start(s32[2048]{0:T(1024)S(1)} %pad_add_fusion.1), channel_id=1, source_target_pairs={{0,24},{1,25},{2,26},{3,27},{4,28},{5,29},{6,30},{7,31},{8,0},{9,1... | collective-permute-start | bytes 24584 | tf_op jit(solution)/shard_map/ppermute | solution.py:303
  31.1 10.0 %collective-permute-start.9 = (bf16[512,512]{1,0:T(8,128)(2,1)S(1)}, bf16[512,512]{1,0:T(8,128)(2,1)S(1)}, u32[]{:S(2)}, u32[]{:S(2)}) collective-permute-start(bf16[512,512]{1,0:T(8,128)(2,1)S(1)} %collective-permute-done.4.refs_1_.refs_6_), channel_id=1, source_target_pairs={{0,32},{32,0},{64,96},{96,64},{128,160},{160,128},{192,224},{224,1... | collective-permute-start | bytes 1572872 | tf_op jit(solution)/shard_map/ppermute | solution.py:293
  31.2 1.2 copy-start.2
  34.1 5.3 %collective-permute-start.6 = (s32[4096]{0:T(1024)S(1)}, s32[4096]{0:T(1024)S(1)}, u32[]{:S(2)}, u32[]{:S(2)}) collective-permute-start(s32[4096]{0:T(1024)S(1)} %pad_add_fusion), channel_id=1, source_target_pairs={{0,16},{1,17},{2,18},{3,19},{4,20},{5,21},{6,22},{7,23},{8,24},{9,... | collective-permute-start | bytes 49160 | tf_op jit(solution)/shard_map/ppermute | solution.py:303
  36.0 6.7 %collective-permute-start.8 = (bf16[512,512]{1,0:T(8,128)(2,1)}, bf16[512,512]{1,0:T(8,128)(2,1)S(1)}, u32[]{:S(2)}, u32[]{:S(2)}) collective-permute-start(bf16[512,512]{1,0:T(8,128)(2,1)} %collective-permute-done.7.refs_1_.refs_4_), channel_id=1, source_target_pairs={{0,32},{32,0},{64,96},{96,64},{128,160},{160,128},{192,224},{224,1... | collective-permute-start | bytes 1572872 | tf_op jit(solution)/shard_map/ppermute | solution.py:293
  42.7 2.2 %copy-start = (bf16[2048,512]{1,0:T(8,128)(2,1)S(1)}, bf16[2048,512]{1,0:T(8,128)(2,1)}, u32[]{:S(2)}) copy-start(bf16[2048,512]{1,0:T(8,128)(2,1)} %k_ref.11) | copy-start | bytes 6291460
  42.7 2.4 %copy-start.1 = (bf16[2048,512]{1,0:T(8,128)(2,1)S(1)}, bf16[2048,512]{1,0:T(8,128)(2,1)}, u32[]{:S(2)}) copy-start(bf16[2048,512]{1,0:T(8,128)(2,1)} %v_ref.11) | copy-start | bytes 6291460
  42.7 2.4 %copy-start.11 = (s32[8]{0:T(128)S(1)}, s32[8]{0:T(128)}, u32[]{:S(2)}) copy-start(s32[8]{0:T(128)} %constant.132.clone.order_ref) | copy-start | bytes 100
  45.1 7.9 %copy-start.10 = (s32[16]{0:T(128)S(1)}, s32[16]{0:T(128)}, u32[]{:S(2)}) copy-start(s32[16]{0:T(128)} %constant.133.clone.order_ref) | copy-start | bytes 196
  46.4 13.5 %copy-start.9 = (s32[16]{0:T(128)S(1)}, s32[16]{0:T(128)}, u32[]{:S(2)}) copy-start(s32[16]{0:T(128)} %constant.134.clone.order_ref) | copy-start | bytes 196
  46.4 35.3 %collective-permute-start.12 = (bf16[2,128,512]{2,1,0:T(8,128)(2,1)S(1)}, bf16[2,128,512]{2,1,0:T(8,128)(2,1)S(1)}, u32[]{:S(2)}, u32[]{:S(2)}) collective-permute-start(bf16[2,128,512]{2,1,0:T(8,128)(2,1)S(1)} %get-tuple-element.26), channel_id=1, source_target_pairs={{0,1},{1,2},{2,3},{3,4},{4,5},{5,6},{6,7},{7,0},{8,9},{9,10},{10,1... | collective-permute-start | bytes 786440 | tf_op jit(solution)/shard_map/ppermute | solution.py:298
  48.8 32.5 %collective-permute-start.16 = (bf16[2,128,512]{2,1,0:T(8,128)(2,1)S(1)}, bf16[2,128,512]{2,1,0:T(8,128)(2,1)S(1)}, u32[]{:S(2)}, u32[]{:S(2)}) collective-permute-start(bf16[2,128,512]{2,1,0:T(8,128)(2,1)S(1)} %get-tuple-element.31), channel_id=1, source_target_pairs={{0,7},{1,0},{2,1},{3,2},{4,3},{5,4},{6,5},{7,6},{8,15},{9,8},{10,9... | collective-permute-start | bytes 786440 | tf_op jit(solution)/shard_map/ppermute | solution.py:298
  56.6 5.9 %copy-start.8 = (s32[32]{0:T(128)S(1)}, s32[32]{0:T(128)}, u32[]{:S(2)}) copy-start(s32[32]{0:T(128)} %constant.135.clone.order_ref) | copy-start | bytes 388
  56.6 28.6 %collective-permute-start.24 = (bf16[4,128,512]{2,1,0:T(8,128)(2,1)S(1)}, bf16[4,128,512]{2,1,0:T(8,128)(2,1)S(1)}, u32[]{:S(2)}, u32[]{:S(2)}) collective-permute-start(bf16[4,128,512]{2,1,0:T(8,128)(2,1)S(1)} %get-tuple-element.35), channel_id=1, source_target_pairs={{0,8},{1,9},{2,10},{3,11},{4,12},{5,13},{6,14},{7,15},{8,16},{9,17... | collective-permute-start | bytes 1572872 | tf_op jit(solution)/shard_map/ppermute | solution.py:303
  56.7 27.1 %collective-permute-start.26 = (bf16[4,128,512]{2,1,0:T(8,128)(2,1)S(1)}, bf16[4,128,512]{2,1,0:T(8,128)(2,1)S(1)}, u32[]{:S(2)}, u32[]{:S(2)}) collective-permute-start(bf16[4,128,512]{2,1,0:T(8,128)(2,1)S(1)} %get-tuple-element.38), channel_id=1, source_target_pairs={{0,24},{1,25},{2,26},{3,27},{4,28},{5,29},{6,30},{7,31},{8,0},{9,1... | collective-permute-start | bytes 1572872 | tf_op jit(solution)/shard_map/ppermute | solution.py:303
  62.4 5.4 %copy-start.7 = (s32[16]{0:T(128)S(1)}, s32[16]{0:T(128)}, u32[]{:S(2)}) copy-start(s32[16]{0:T(128)} %constant.136.clone.order_ref) | copy-start | bytes 196
  67.7 4.6 %copy-start.6 = (s32[40]{0:T(128)S(1)}, s32[40]{0:T(128)}, u32[]{:S(2)}) copy-start(s32[40]{0:T(128)} %constant.137.clone.order_ref) | copy-start | bytes 484
  81.5 10.6 %collective-permute-start.17 = (bf16[4,128,512]{2,1,0:T(8,128)(2,1)S(1)}, bf16[4,128,512]{2,1,0:T(8,128)(2,1)S(1)}, u32[]{:S(2)}, u32[]{:S(2)}) collective-permute-start(bf16[4,128,512]{2,1,0:T(8,128)(2,1)S(1)} %pad_maximum_fusion.3), channel_id=1, source_target_pairs={{0,7},{1,0},{2,1},{3,2},{4,3},{5,4},{6,5},{7,6},{8,15},{9,8},{10,9... | collective-permute-start | bytes 1572872 | tf_op jit(solution)/shard_map/ppermute | solution.py:298
  81.8 13.4 %collective-permute-start.13 = (bf16[4,128,512]{2,1,0:T(8,128)(2,1)S(1)}, bf16[4,128,512]{2,1,0:T(8,128)(2,1)S(1)}, u32[]{:S(2)}, u32[]{:S(2)}) collective-permute-start(bf16[4,128,512]{2,1,0:T(8,128)(2,1)S(1)} %pad_maximum_fusion.2), channel_id=1, source_target_pairs={{0,1},{1,2},{2,3},{3,4},{4,5},{5,6},{6,7},{7,0},{8,9},{9,10},{10,1... | collective-permute-start | bytes 1572872 | tf_op jit(solution)/shard_map/ppermute | solution.py:298
  84.0 24.0 %collective-permute-start.27 = (bf16[8,128,512]{2,1,0:T(8,128)(2,1)S(1)}, bf16[8,128,512]{2,1,0:T(8,128)(2,1)S(1)}, u32[]{:S(2)}, u32[]{:S(2)}) collective-permute-start(bf16[8,128,512]{2,1,0:T(8,128)(2,1)S(1)} %pad_maximum_fusion.1), channel_id=1, source_target_pairs={{0,24},{1,25},{2,26},{3,27},{4,28},{5,29},{6,30},{7,31},{8,0},{9,1... | collective-permute-start | bytes 3145736 | tf_op jit(solution)/shard_map/ppermute | solution.py:303
  85.4 22.7 %collective-permute-start.25 = (bf16[8,128,512]{2,1,0:T(8,128)(2,1)S(1)}, bf16[8,128,512]{2,1,0:T(8,128)(2,1)S(1)}, u32[]{:S(2)}, u32[]{:S(2)}) collective-permute-start(bf16[8,128,512]{2,1,0:T(8,128)(2,1)S(1)} %pad_maximum_fusion), channel_id=1, source_target_pairs={{0,8},{1,9},{2,10},{3,11},{4,12},{5,13},{6,14},{7,15},{8,16},{9,17... | collective-permute-start | bytes 3145736 | tf_op jit(solution)/shard_map/ppermute | solution.py:303
  92.2 11.7 %collective-permute-start.18 = (bf16[4,128,512]{2,1,0:T(8,128)(2,1)S(1)}, bf16[4,128,512]{2,1,0:T(8,128)(2,1)S(1)}, u32[]{:S(2)}, u32[]{:S(2)}) collective-permute-start(bf16[4,128,512]{2,1,0:T(8,128)(2,1)S(1)} %add_convert_fusion.3), channel_id=1, source_target_pairs={{0,7},{1,0},{2,1},{3,2},{4,3},{5,4},{6,5},{7,6},{8,15},{9,8},{10,9... | collective-permute-start | bytes 1572872 | tf_op jit(solution)/shard_map/ppermute | solution.py:298
  95.3 12.5 %collective-permute-start.14 = (bf16[4,128,512]{2,1,0:T(8,128)(2,1)S(1)}, bf16[4,128,512]{2,1,0:T(8,128)(2,1)S(1)}, u32[]{:S(2)}, u32[]{:S(2)}) collective-permute-start(bf16[4,128,512]{2,1,0:T(8,128)(2,1)S(1)} %add_convert_fusion.5), channel_id=1, source_target_pairs={{0,1},{1,2},{2,3},{3,4},{4,5},{5,6},{6,7},{7,0},{8,9},{9,10},{10,1... | collective-permute-start | bytes 1572872 | tf_op jit(solution)/shard_map/ppermute | solution.py:298
  95.4 56.9 %copy-start.5 = (bf16[512,512]{1,0:T(8,128)(2,1)S(1)}, bf16[512,512]{1,0:T(8,128)(2,1)}, u32[]{:S(2)}) copy-start(bf16[512,512]{1,0:T(8,128)(2,1)} %refs_11_.1) | copy-start | bytes 1572868
  104.0 27.3 %collective-permute-start.19 = (bf16[4,128,512]{2,1,0:T(8,128)(2,1)S(1)}, bf16[4,128,512]{2,1,0:T(8,128)(2,1)S(1)}, u32[]{:S(2)}, u32[]{:S(2)}) collective-permute-start(bf16[4,128,512]{2,1,0:T(8,128)(2,1)S(1)} %add_convert_fusion.2), channel_id=1, source_target_pairs={{0,7},{1,0},{2,1},{3,2},{4,3},{5,4},{6,5},{7,6},{8,15},{9,8},{10,9... | collective-permute-start | bytes 1572872 | tf_op jit(solution)/shard_map/ppermute | solution.py:298
  107.9 23.4 %collective-permute-start.15 = (bf16[4,128,512]{2,1,0:T(8,128)(2,1)S(1)}, bf16[4,128,512]{2,1,0:T(8,128)(2,1)S(1)}, u32[]{:S(2)}, u32[]{:S(2)}) collective-permute-start(bf16[4,128,512]{2,1,0:T(8,128)(2,1)S(1)} %add_convert_fusion.4), channel_id=1, source_target_pairs={{0,1},{1,2},{2,3},{3,4},{4,5},{5,6},{6,7},{7,0},{8,9},{9,10},{10,1... | collective-permute-start | bytes 1572872 | tf_op jit(solution)/shard_map/ppermute | solution.py:298
  108.2 8.9 %collective-permute-start.32 = (bf16[64,512]{1,0:T(8,128)(2,1)S(1)}, bf16[64,512]{1,0:T(8,128)(2,1)S(1)}, u32[]{:S(2)}, u32[]{:S(2)}) collective-permute-start(bf16[64,512]{1,0:T(8,128)(2,1)S(1)} %get-tuple-element.46), channel_id=1, source_target_pairs={{0,7},{1,0},{2,1},{3,2},{4,3},{5,4},{6,5},{7,6},{8,15},{9,8},{10,9... | collective-permute-start | bytes 196616 | tf_op jit(solution)/shard_map/ppermute | solution.py:298
  111.7 9.7 %collective-permute-start.28 = (bf16[64,512]{1,0:T(8,128)(2,1)S(1)}, bf16[64,512]{1,0:T(8,128)(2,1)S(1)}, u32[]{:S(2)}, u32[]{:S(2)}) collective-permute-start(bf16[64,512]{1,0:T(8,128)(2,1)S(1)} %get-tuple-element.48), channel_id=1, source_target_pairs={{0,1},{1,2},{2,3},{3,4},{4,5},{5,6},{6,7},{7,0},{8,9},{9,10},{10,1... | collective-permute-start | bytes 196616 | tf_op jit(solution)/shard_map/ppermute | solution.py:298
  121.4 6.3 %collective-permute-start.29 = (bf16[128,512]{1,0:T(8,128)(2,1)S(1)}, bf16[128,512]{1,0:T(8,128)(2,1)S(1)}, u32[]{:S(2)}, u32[]{:S(2)}) collective-permute-start(bf16[128,512]{1,0:T(8,128)(2,1)S(1)} %pad_maximum_fusion.6), channel_id=1, source_target_pairs={{0,1},{1,2},{2,3},{3,4},{4,5},{5,6},{6,7},{7,0},{8,9},{9,10},{10,1... | collective-permute-start | bytes 393224 | tf_op jit(solution)/shard_map/ppermute | solution.py:298
  121.5 6.1 %collective-permute-start.33 = (bf16[128,512]{1,0:T(8,128)(2,1)S(1)}, bf16[128,512]{1,0:T(8,128)(2,1)S(1)}, u32[]{:S(2)}, u32[]{:S(2)}) collective-permute-start(bf16[128,512]{1,0:T(8,128)(2,1)S(1)} %pad_maximum_fusion.7), channel_id=1, source_target_pairs={{0,7},{1,0},{2,1},{3,2},{4,3},{5,4},{6,5},{7,6},{8,15},{9,8},{10,9... | collective-permute-start | bytes 393224 | tf_op jit(solution)/shard_map/ppermute | solution.py:298
  127.8 14.9 %collective-permute-start.34 = (bf16[128,512]{1,0:T(8,128)(2,1)S(1)}, bf16[128,512]{1,0:T(8,128)(2,1)S(1)}, u32[]{:S(2)}, u32[]{:S(2)}) collective-permute-start(bf16[128,512]{1,0:T(8,128)(2,1)S(1)} %get-tuple-element.43), channel_id=1, source_target_pairs={{0,7},{1,0},{2,1},{3,2},{4,3},{5,4},{6,5},{7,6},{8,15},{9,8},{10,9... | collective-permute-start | bytes 393224 | tf_op jit(solution)/shard_map/ppermute | solution.py:298
  131.4 11.4 %collective-permute-start.30 = (bf16[128,512]{1,0:T(8,128)(2,1)S(1)}, bf16[128,512]{1,0:T(8,128)(2,1)S(1)}, u32[]{:S(2)}, u32[]{:S(2)}) collective-permute-start(bf16[128,512]{1,0:T(8,128)(2,1)S(1)} %get-tuple-element.44), channel_id=1, source_target_pairs={{0,1},{1,2},{2,3},{3,4},{4,5},{5,6},{6,7},{7,0},{8,9},{9,10},{10,1... | collective-permute-start | bytes 393224 | tf_op jit(solution)/shard_map/ppermute | solution.py:298
  131.5 4.7 %collective-permute-start.22 = (bf16[64,512]{1,0:T(8,128)(2,1)S(1)}, bf16[64,512]{1,0:T(8,128)(2,1)S(1)}, u32[]{:S(2)}, u32[]{:S(2)}) collective-permute-start(bf16[64,512]{1,0:T(8,128)(2,1)S(1)} %get-tuple-element.52), channel_id=1, source_target_pairs={{0,24},{1,25},{2,26},{3,27},{4,28},{5,29},{6,30},{7,31},{8,0},{9,1... | collective-permute-start | bytes 196616 | tf_op jit(solution)/shard_map/ppermute | solution.py:303
  133.7 5.5 %collective-permute-start.20 = (bf16[64,512]{1,0:T(8,128)(2,1)S(1)}, bf16[64,512]{1,0:T(8,128)(2,1)S(1)}, u32[]{:S(2)}, u32[]{:S(2)}) collective-permute-start(bf16[64,512]{1,0:T(8,128)(2,1)S(1)} %get-tuple-element.54), channel_id=1, source_target_pairs={{0,8},{1,9},{2,10},{3,11},{4,12},{5,13},{6,14},{7,15},{8,16},{9,17... | collective-permute-start | bytes 196616 | tf_op jit(solution)/shard_map/ppermute | solution.py:303
  139.3 6.9 %collective-permute-start.21 = (bf16[128,512]{1,0:T(8,128)(2,1)S(1)}, bf16[128,512]{1,0:T(8,128)(2,1)S(1)}, u32[]{:S(2)}, u32[]{:S(2)}) collective-permute-start(bf16[128,512]{1,0:T(8,128)(2,1)S(1)} %pad_maximum_fusion.4), channel_id=1, source_target_pairs={{0,8},{1,9},{2,10},{3,11},{4,12},{5,13},{6,14},{7,15},{8,16},{9,17... | collective-permute-start | bytes 393224 | tf_op jit(solution)/shard_map/ppermute | solution.py:303
  139.4 6.8 %collective-permute-start.23 = (bf16[128,512]{1,0:T(8,128)(2,1)S(1)}, bf16[128,512]{1,0:T(8,128)(2,1)S(1)}, u32[]{:S(2)}, u32[]{:S(2)}) collective-permute-start(bf16[128,512]{1,0:T(8,128)(2,1)S(1)} %pad_maximum_fusion.5), channel_id=1, source_target_pairs={{0,24},{1,25},{2,26},{3,27},{4,28},{5,29},{6,30},{7,31},{8,0},{9,1... | collective-permute-start | bytes 393224 | tf_op jit(solution)/shard_map/ppermute | solution.py:303
  142.9 5.8 %collective-permute-start.35 = (bf16[128,512]{1,0:T(8,128)(2,1)S(1)}, bf16[128,512]{1,0:T(8,128)(2,1)S(1)}, u32[]{:S(2)}, u32[]{:S(2)}) collective-permute-start(bf16[128,512]{1,0:T(8,128)(2,1)S(1)} %get-tuple-element.41), channel_id=1, source_target_pairs={{0,7},{1,0},{2,1},{3,2},{4,3},{5,4},{6,5},{7,6},{8,15},{9,8},{10,9... | collective-permute-start | bytes 393224 | tf_op jit(solution)/shard_map/ppermute | solution.py:298
  146.2 6.2 %collective-permute-start.31 = (bf16[128,512]{1,0:T(8,128)(2,1)S(1)}, bf16[128,512]{1,0:T(8,128)(2,1)S(1)}, u32[]{:S(2)}, u32[]{:S(2)}) collective-permute-start(bf16[128,512]{1,0:T(8,128)(2,1)S(1)} %get-tuple-element.42), channel_id=1, source_target_pairs={{0,1},{1,2},{2,3},{3,4},{4,5},{5,6},{6,7},{7,0},{8,9},{9,10},{10,1... | collective-permute-start | bytes 393224 | tf_op jit(solution)/shard_map/ppermute | solution.py:298

commit v4 on v3

--- a/solution.py
+++ b/solution.py
@@ -66,6 +66,22 @@
         at += piece.shape[0]
 
 
+def halve_kernel(w_ref, out_ref):
+    out_ref[...] = w_ref[:, out_ref.shape[1] :]
+
+
+def query_weights(w_in):
+    width = w_in.shape[0]
+    return pl.pallas_call(
+        halve_kernel,
+        out_shape=jax.ShapeDtypeStruct((width, width), w_in.dtype),
+        in_specs=[VMEM],
+        out_specs=VMEM,
+        compiler_params=pltpu.CompilerParams(vmem_limit_bytes=8 << 20),
+        name="halve",
+    )(w_in)
+
+
 def project_kernel(first, scale, count, unrolled, *refs):
     w_ref = refs[0]
     out_ref, rows_ref = refs[-2], refs[-1]
@@ -74,7 +90,7 @@
     tile = math.gcd(refs[1].shape[0], TILE)
 
     def one_tile(values, to):
-        half = 0.5 * jnp.dot(values, w_ref[:, width:], preferred_element_type=jnp.float32)
+        half = 0.5 * jnp.dot(values, w_ref[...], preferred_element_type=jnp.float32)
         query = half_silu(half).astype(jnp.bfloat16).astype(jnp.float32) * scale
         for c in range(cuts):
             out_ref[pl.ds((first + to) * cuts + c, tile, stride=cuts), :] = query[:, c * LANES : (c + 1) * LANES]
@@ -96,10 +112,10 @@
     lax.fori_loop(0, rows // tile, step, 0)
 
 
-def project(table, first, total, pieces, w_in, scale, unrolled=False):
-    width = w_in.shape[0]
+def project(table, first, total, pieces, w_query, scale, unrolled=False):
+    width = w_query.shape[0]
     rows = sum(p.shape[0] for p in pieces)
-    ins = [w_in, *pieces]
+    ins = [w_query, *pieces]
     aliases = {}
     kernel = functools.partial(project_kernel, first, scale, len(pieces), unrolled)
     if table is not None:
@@ -305,6 +321,7 @@
         )
 
     normed = norm(cand_table)
+    w_query = query_weights(w_in)
     ahead = x_shift(normed, -1)
     behind = x_shift(normed, 1)
     other = swap(normed)
@@ -313,7 +330,6 @@
     while step < nz:
         wanted = jnp.concatenate([wanted, z_shift(wanted, -step)])
         step *= 2
-    wanted, ahead, behind = lax.optimization_barrier((wanted, ahead, behind))
     far = x_shift(ahead, -1)
     ahead_rows = [ahead, swap(ahead)]
     behind_rows = [behind, swap(behind)]
@@ -346,19 +362,18 @@
     scale = 0.5 / math.sqrt(width // H)
     chip = CORES * part_rows
     near_rows = [normed, other]
-    table = project(None, 0, total_rows, near_rows, w_in, scale)
-    table = project(table, 1 * chip, total_rows, ahead_rows, w_in, scale)
-    table = project(table, 3 * chip, total_rows, behind_rows, w_in, scale)
+    table = project(None, 0, total_rows, near_rows, w_query, scale)
+    table = project(table, 1 * chip, total_rows, ahead_rows, w_query, scale)
+    table = project(table, 3 * chip, total_rows, behind_rows, w_query, scale)
     far_rows = [far, swap(far)]
-    table = project(table, 2 * chip, total_rows, far_rows, w_in, scale, unrolled=True)
+    table = project(table, 2 * chip, total_rows, far_rows, w_query, scale, unrolled=True)
 
     half = cand // 2
     half_z = nz // 2
     z_of = lambda dz, dys=range(NY): [(dy, dz, 0) for dy in dys]
     y_of = lambda dy, dzs=range(nz): [(dy, dz, half) for dz in dzs]
     calls = [
-        [z_of(4, (0, 1)), z_of(4, (2, 3))],
-        [y_of(2, range(half_z)), y_of(2, range(half_z, nz))],
+        [z_of(4, (0, 1)), z_of(4, (2, 3)), y_of(2, range(half_z)), y_of(2, range(half_z, nz))],
         [z_of(3), z_of(5)],
         [y_of(1), y_of(3)],
         [z_of(2), z_of(6)],

time: 154 us -> 157 us (1.019)
  the two profiles are of different devices: /device:TPU:2 before, /device:TPU:128 now
where the time goes in v4:
time: 157 us
  waiting for transfers between devices  64.3 us (41%)
  starting transfers between devices  47.7 us (30%)
  Pallas kernels  34.2 us (22%)
  other arithmetic  6.54 us (4%)
  local copies, waits for them, and re-layouts  3.82 us (2%)
    ppermute x19, waiting for transfers between devices, z_shift(): lax.ppermute(value, 'shard', [(y * nz + z, y * nz + (z + k) % nz) for y i...  50.7 us
    pallas_call x5, Pallas kernels, attend(): pl.pallas_call(functools.partial(attend_kernel, tuple(sizes), math.gcd(ro...  25.1 us
    ppermute x19, starting transfers between devices, z_shift(): lax.ppermute(value, 'shard', [(y * nz + z, y * nz + (z + k) % nz) for y i...  24 us
    ppermute x10, starting transfers between devices, y_shift(): lax.ppermute(value, 'shard', [(y * nz + z, (y + k) % NY * nz + z) for y i...  16.9 us
    ppermute x3, waiting for transfers between devices, x_shift(): lax.ppermute(value, 'grp', [(x * CORES + c, (x + k) % nx * CORES + c) for...  7.74 us
    ppermute x3, starting transfers between devices, x_shift(): lax.ppermute(value, 'grp', [(x * CORES + c, (x + k) % nx * CORES + c) for...  6.27 us
    ppermute x10, waiting for transfers between devices, y_shift(): lax.ppermute(value, 'shard', [(y * nz + z, (y + k) % NY * nz + z) for y i...  5.81 us
    pallas_call x4, Pallas kernels, project(): pl.pallas_call(kernel, out_shape=jax.ShapeDtypeStruct((total * width // L...  5.61 us
  transfers between devices with their start and end apart: 36, of which 16 were waited for; matrix products, arithmetic and copies ran while one was open for 4% of the time, Pallas kernels for 15%

profile of v4, /device:TPU:128, one launch (start us, length us, event | category | flops | bytes accessed | tf_op | source)
XLA Modules:
  0.0 157.1 jit_solution(8251063795795668825)
XLA Ops:
  0.0 1.0 copy-done.4
  1.6 1.6 collective-permute-start.8
  3.2 1.7 %collective-permute-start.5 = (bf16[512,512]{1,0:T(8,128)(2,1)S(1)}, bf16[512,512]{1,0:T(8,128)(2,1)S(1)}, u32[]{:S(2)}, u32[]{:S(2)}) collective-permute-start(bf16[512,512]{1,0:T(8,128)(2,1)S(1)} %norm.1.refs_1_.refs_0_), channel_id=1, source_target_pairs={{0,192},{32,224},{64,0},{96,32},{128,64},{160,96},{192,128},{224,1... | collective-permute-start | bytes 1572872 | tf_op jit(solution)/shard_map/ppermute | solution.py:304
  5.1 0.9 convert_reduce_fusion
  7.5 1.3 collective-permute-done
  9.4 7.7 %collective-permute-done.5.refs_1_.refs_2_ = bf16[512,512]{1,0:T(8,128)(2,1)S(1)} collective-permute-done((bf16[512,512]{1,0:T(8,128)(2,1)S(1)}, bf16[512,512]{1,0:T(8,128)(2,1)S(1)}, u32[]{:S(2)}, u32[]{:S(2)}) %collective-permute-start.5) | collective-permute-done | bytes 524320 | tf_op jit(solution)/shard_map/ppermute | solution.py:304
  17.2 3.0 %collective-permute-start.6 = (bf16[512,512]{1,0:T(8,128)(2,1)S(1)}, bf16[512,512]{1,0:T(8,128)(2,1)S(1)}, u32[]{:S(2)}, u32[]{:S(2)}) collective-permute-start(bf16[512,512]{1,0:T(8,128)(2,1)S(1)} %collective-permute-done.5.refs_1_.refs_2_), channel_id=1, source_target_pairs={{0,192},{32,224},{64,0},{96,32},{128,64},{160,96},{192,128},{224,1... | collective-permute-start | bytes 1572872 | tf_op jit(solution)/shard_map/ppermute | solution.py:304
  21.3 7.1 %collective-permute-done.2 = s32[1024]{0:T(1024)S(1)} collective-permute-done((s32[1024]{0:T(1024)S(1)}, s32[1024]{0:T(1024)S(1)}, u32[]{:S(2)}, u32[]{:S(2)}) %collective-permute-start.2) | collective-permute-done | bytes 4128 | tf_op jit(solution)/shard_map/ppermute | solution.py:314
  29.0 3.0 %collective-permute-start.3 = (s32[2048]{0:T(1024)S(1)}, s32[2048]{0:T(1024)S(1)}, u32[]{:S(2)}, u32[]{:S(2)}) collective-permute-start(s32[2048]{0:T(1024)S(1)} %pad_add_fusion), channel_id=1, source_target_pairs={{0,24},{1,25},{2,26},{3,27},{4,28},{5,29},{6,30},{7,31},{8,0},{9,1... | collective-permute-start | bytes 24584 | tf_op jit(solution)/shard_map/ppermute | solution.py:319
  32.0 1.4 collective-permute-done.3
  33.4 2.5 %collective-permute-start.4 = (s32[4096]{0:T(1024)S(1)}, s32[4096]{0:T(1024)S(1)}, u32[]{:S(2)}, u32[]{:S(2)}) collective-permute-start(s32[4096]{0:T(1024)S(1)} %get-tuple-element.51), channel_id=1, source_target_pairs={{0,16},{1,17},{2,18},{3,19},{4,20},{5,21},{6,22},{7,23},{8,24},{9,... | collective-permute-start | bytes 49160 | tf_op jit(solution)/shard_map/ppermute | solution.py:319
  36.5 1.2 copy-done.2
  37.7 0.9 collective-permute-done.4
  38.7 1.6 %project.4.refs_3_ = f32[16384,128]{1,0:T(8,128)S(1)} custom-call(bf16[512,512]{1,0:T(8,128)(2,1)S(1)} %halve.1.refs_0_, bf16[512,512]{1,0:T(8,128)(2,1)S(1)} %norm.1.refs_1_.refs_0_, bf16[512,512]{1,0:T(8,128)(2,1)S(1)} %collective-permute-done.11.refs_2_.refs_1_), custom_call_target="tpu_custom_call" | custom-call | flops 536870912 | bytes 3145728 | tf_op jit(solution)/shard_map/project/pallas_call | solution.py:124
  40.3 1.6 %project.5.refs_3_ = f32[16384,128]{1,0:T(8,128)S(1)} custom-call(bf16[512,512]{1,0:T(8,128)(2,1)S(1)} %halve.1.refs_0_, bf16[512,512]{1,0:T(8,128)(2,1)S(1)} %collective-permute-done.5.refs_1_.refs_2_, bf16[512,512]{1,0:T(8,128)(2,1)S(1)} %collective-permute-done.10.refs_2_.refs_3_, f32[16384,128]{1,0:T(8,128)S(1)} %project.4.refs_3_), custom_call_target="tpu_custom_call", output_to_operand_aliasing={{}: (3, {})} | custom-call | flops 536870912 | bytes 3145728 | tf_op jit(solution)/shard_map/project/pallas_call | solution.py:124
  41.9 1.6 %project.6.refs_3_ = f32[16384,128]{1,0:T(8,128)S(1)} custom-call(bf16[512,512]{1,0:T(8,128)(2,1)S(1)} %halve.1.refs_0_, bf16[512,512]{1,0:T(8,128)(2,1)S(1)} %collective-permute-done.8.refs_1_.refs_6_, bf16[512,512]{1,0:T(8,128)(2,1)S(1)} %collective-permute-done.9.refs_2_.refs_7_, f32[16384,128]{1,0:T(8,128)S(1)} %project.5.refs_3_), custom_call_target="tpu_custom_call", output_to_operand_aliasing={{}: (3, {})} | custom-call | flops 536870912 | bytes 3145728 | tf_op jit(solution)/shard_map/project/pallas_call | solution.py:124
  43.6 0.8 project.7.table_ref
  45.8 2.5 %attend.7 = (bf16[4,128,512]{2,1,0:T(8,128)(2,1)S(1)}, bf16[4,128,512]{2,1,0:T(8,128)(2,1)S(1)}) custom-call(s32[8192]{0:T(1024)S(1)} %fusion.24.index_ref, s32[32]{0:T(128)S(1)} %convert_reduce_fusion.1.count_ref, s32[64]{0:T(128)S(1)} %select_reduce_fusion.block_ref, s32[16]{0:T(128)S(1)} %copy-done.10, f32[16384,128]{1,0:T(8,128)S(1)} %project.7.table_ref, ...), custom_call_target="tpu_custom_call" | custom-call | flops 536870912 | bytes 2097152 | tf_op jit(solution)/shard_map/attend/pallas_call | solution.py:237
  48.4 5.4 %attend.6 = (bf16[2,128,512]{2,1,0:T(8,128)(2,1)S(1)}, bf16[2,128,512]{2,1,0:T(8,128)(2,1)S(1)}, bf16[4,128,512]{2,1,0:T(8,128)(2,1)S(1)}, bf16[4,128,512]{2,1,0:T(8,128)(2,1)S(1)}) custom-call(s32[8192]{0:T(1024)S(1)} %fusion.24.index_ref, s32[32]{0:T(128)S(1)} %convert_reduce_fusion.1.count_ref, s32[64]{0:T(128)S(1)} %select_reduce_fusion.block_ref, ...), custom_call_target="tpu_custom_call" | custom-call | flops 805306368 | bytes 3145728 | tf_op jit(solution)/shard_map/attend/pallas_call | solution.py:237
  53.7 3.6 %collective-permute-start.12 = (bf16[2,128,512]{2,1,0:T(8,128)(2,1)S(1)}, bf16[2,128,512]{2,1,0:T(8,128)(2,1)S(1)}, u32[]{:S(2)}, u32[]{:S(2)}) collective-permute-start(bf16[2,128,512]{2,1,0:T(8,128)(2,1)S(1)} %get-tuple-element.20), channel_id=1, source_target_pairs={{0,1},{1,2},{2,3},{3,4},{4,5},{5,6},{6,7},{7,0},{8,9},{9,10},{10,1... | collective-permute-start | bytes 786440 | tf_op jit(solution)/shard_map/ppermute | solution.py:314
  57.3 2.5 %collective-permute-start.24 = (bf16[4,128,512]{2,1,0:T(8,128)(2,1)S(1)}, bf16[4,128,512]{2,1,0:T(8,128)(2,1)S(1)}, u32[]{:S(2)}, u32[]{:S(2)}) collective-permute-start(bf16[4,128,512]{2,1,0:T(8,128)(2,1)S(1)} %get-tuple-element.29), channel_id=1, source_target_pairs={{0,8},{1,9},{2,10},{3,11},{4,12},{5,13},{6,14},{7,15},{8,16},{9,17... | collective-permute-start | bytes 1572872 | tf_op jit(solution)/shard_map/ppermute | solution.py:319
  59.9 1.2 collective-permute-start.26
  61.1 6.8 %attend.9 = (bf16[8,128,512]{2,1,0:T(8,128)(2,1)S(1)}, bf16[8,128,512]{2,1,0:T(8,128)(2,1)S(1)}) custom-call(s32[8192]{0:T(1024)S(1)} %fusion.24.index_ref, s32[32]{0:T(128)S(1)} %convert_reduce_fusion.1.count_ref, s32[64]{0:T(128)S(1)} %select_reduce_fusion.block_ref, s32[32]{0:T(128)S(1)} %copy-done.8, f32[16384,128]{1,0:T(8,128)S(1)} %project.7.table_ref, ...), custom_call_target="tpu_custom_call" | custom-call | flops 1073741824 | bytes 4194304 | tf_op jit(solution)/shard_map/attend/pallas_call | solution.py:237
  67.9 3.9 %attend.8 = (bf16[4,128,512]{2,1,0:T(8,128)(2,1)S(1)}, bf16[4,128,512]{2,1,0:T(8,128)(2,1)S(1)}) custom-call(s32[8192]{0:T(1024)S(1)} %fusion.24.index_ref, s32[32]{0:T(128)S(1)} %convert_reduce_fusion.1.count_ref, s32[64]{0:T(128)S(1)} %select_reduce_fusion.block_ref, s32[16]{0:T(128)S(1)} %copy-done.7, f32[16384,128]{1,0:T(8,128)S(1)} %project.7.table_ref, ...), custom_call_target="tpu_custom_call" | custom-call | flops 536870912 | bytes 2097152 | tf_op jit(solution)/shard_map/attend/pallas_call | solution.py:237
  71.9 6.5 %attend.5 = (bf16[4,128,512]{2,1,0:T(8,128)(2,1)S(1)}, bf16[4,128,512]{2,1,0:T(8,128)(2,1)S(1)}, bf16[4,128,512]{2,1,0:T(8,128)(2,1)S(1)}, bf16[8,128,512]{2,1,0:T(8,128)(2,1)S(1)}) custom-call(s32[8192]{0:T(1024)S(1)} %fusion.24.index_ref, s32[32]{0:T(128)S(1)} %convert_reduce_fusion.1.count_ref, s32[64]{0:T(128)S(1)} %select_reduce_fusion.block_ref, ...), custom_call_target="tpu_custom_call" | custom-call | flops 1342177280 | bytes 5242880 | tf_op jit(solution)/shard_map/attend/pallas_call | solution.py:237
  78.8 2.1 %collective-permute-start.13 = (bf16[4,128,512]{2,1,0:T(8,128)(2,1)S(1)}, bf16[4,128,512]{2,1,0:T(8,128)(2,1)S(1)}, u32[]{:S(2)}, u32[]{:S(2)}) collective-permute-start(bf16[4,128,512]{2,1,0:T(8,128)(2,1)S(1)} %pad_maximum_fusion.2), channel_id=1, source_target_pairs={{0,1},{1,2},{2,3},{3,4},{4,5},{5,6},{6,7},{7,0},{8,9},{9,10},{10,1... | collective-permute-start | bytes 1572872 | tf_op jit(solution)/shard_map/ppermute | solution.py:314
  81.2 1.6 collective-permute-start.27
  83.6 9.1 %collective-permute-done.17 = bf16[4,128,512]{2,1,0:T(8,128)(2,1)S(1)} collective-permute-done((bf16[4,128,512]{2,1,0:T(8,128)(2,1)S(1)}, bf16[4,128,512]{2,1,0:T(8,128)(2,1)S(1)}, u32[]{:S(2)}, u32[]{:S(2)}) %collective-permute-start.17) | collective-permute-done | bytes 524320 | tf_op jit(solution)/shard_map/ppermute | solution.py:314
  92.8 1.0 collective-permute-start.18
  94.3 1.1 collective-permute-start.14
  95.4 1.7 %gate.1.refs_10_ = bf16[256,512]{1,0:T(8,128)(2,1)S(1)} custom-call(s32[1,256]{1,0:T(1,128)S(1)} %bitcast.136, bf16[512,1024]{1,0:T(8,128)(2,1)S(1)} %copy-done.3, bf16[512,512]{1,0:T(8,128)(2,1)S(1)} %norm.1.refs_1_.refs_0_, bf16[512,512]{1,0:T(8,128)(2,1)S(1)} %collective-permute-done.11.refs_2_.refs_1_, ...), custom_call_target="tpu_custom_call" | custom-call | flops 1207959552 | bytes 4194304 | tf_op jit(solution)/shard_map/gate/pallas_call | solution.py:160
  97.1 10.5 %collective-permute-done.18 = bf16[4,128,512]{2,1,0:T(8,128)(2,1)S(1)} collective-permute-done((bf16[4,128,512]{2,1,0:T(8,128)(2,1)S(1)}, bf16[4,128,512]{2,1,0:T(8,128)(2,1)S(1)}, u32[]{:S(2)}, u32[]{:S(2)}) %collective-permute-start.18) | collective-permute-done | bytes 524320 | tf_op jit(solution)/shard_map/ppermute | solution.py:314
  107.8 2.1 %collective-permute-start.19 = (bf16[4,128,512]{2,1,0:T(8,128)(2,1)S(1)}, bf16[4,128,512]{2,1,0:T(8,128)(2,1)S(1)}, u32[]{:S(2)}, u32[]{:S(2)}) collective-permute-start(bf16[4,128,512]{2,1,0:T(8,128)(2,1)S(1)} %add_convert_fusion.2), channel_id=1, source_target_pairs={{0,7},{1,0},{2,1},{3,2},{4,3},{5,4},{6,5},{7,6},{8,15},{9,8},{10,9... | collective-permute-start | bytes 1572872 | tf_op jit(solution)/shard_map/ppermute | solution.py:314
  110.7 3.3 %collective-permute-start.32 = (bf16[64,512]{1,0:T(8,128)(2,1)S(1)}, bf16[64,512]{1,0:T(8,128)(2,1)S(1)}, u32[]{:S(2)}, u32[]{:S(2)}) collective-permute-start(bf16[64,512]{1,0:T(8,128)(2,1)S(1)} %get-tuple-element.40), channel_id=1, source_target_pairs={{0,7},{1,0},{2,1},{3,2},{4,3},{5,4},{6,5},{7,6},{8,15},{9,8},{10,9... | collective-permute-start | bytes 196616 | tf_op jit(solution)/shard_map/ppermute | solution.py:314
  114.0 9.2 %collective-permute-done.32 = bf16[64,512]{1,0:T(8,128)(2,1)S(1)} collective-permute-done((bf16[64,512]{1,0:T(8,128)(2,1)S(1)}, bf16[64,512]{1,0:T(8,128)(2,1)S(1)}, u32[]{:S(2)}, u32[]{:S(2)}) %collective-permute-start.32) | collective-permute-done | bytes 65568 | tf_op jit(solution)/shard_map/ppermute | solution.py:314
  123.1 3.9 %collective-permute-done.28 = bf16[64,512]{1,0:T(8,128)(2,1)S(1)} collective-permute-done((bf16[64,512]{1,0:T(8,128)(2,1)S(1)}, bf16[64,512]{1,0:T(8,128)(2,1)S(1)}, u32[]{:S(2)}, u32[]{:S(2)}) %collective-permute-start.28) | collective-permute-done | bytes 65568 | tf_op jit(solution)/shard_map/ppermute | solution.py:314
  127.2 3.3 %collective-permute-start.33 = (bf16[128,512]{1,0:T(8,128)(2,1)S(1)}, bf16[128,512]{1,0:T(8,128)(2,1)S(1)}, u32[]{:S(2)}, u32[]{:S(2)}) collective-permute-start(bf16[128,512]{1,0:T(8,128)(2,1)S(1)} %pad_maximum_fusion.7), channel_id=1, source_target_pairs={{0,7},{1,0},{2,1},{3,2},{4,3},{5,4},{6,5},{7,6},{8,15},{9,8},{10,9... | collective-permute-start | bytes 393224 | tf_op jit(solution)/shard_map/ppermute | solution.py:314
  130.5 2.8 %collective-permute-done.29 = bf16[128,512]{1,0:T(8,128)(2,1)S(1)} collective-permute-done((bf16[128,512]{1,0:T(8,128)(2,1)S(1)}, bf16[128,512]{1,0:T(8,128)(2,1)S(1)}, u32[]{:S(2)}, u32[]{:S(2)}) %collective-permute-start.29) | collective-permute-done | bytes 131104 | tf_op jit(solution)/shard_map/ppermute | solution.py:314
  133.5 3.4 %collective-permute-start.34 = (bf16[128,512]{1,0:T(8,128)(2,1)S(1)}, bf16[128,512]{1,0:T(8,128)(2,1)S(1)}, u32[]{:S(2)}, u32[]{:S(2)}) collective-permute-start(bf16[128,512]{1,0:T(8,128)(2,1)S(1)} %get-tuple-element.37), channel_id=1, source_target_pairs={{0,7},{1,0},{2,1},{3,2},{4,3},{5,4},{6,5},{7,6},{8,15},{9,8},{10,9... | collective-permute-start | bytes 393224 | tf_op jit(solution)/shard_map/ppermute | solution.py:314
  137.1 2.0 %collective-permute-start.20 = (bf16[64,512]{1,0:T(8,128)(2,1)S(1)}, bf16[64,512]{1,0:T(8,128)(2,1)S(1)}, u32[]{:S(2)}, u32[]{:S(2)}) collective-permute-start(bf16[64,512]{1,0:T(8,128)(2,1)S(1)} %get-tuple-element.48), channel_id=1, source_target_pairs={{0,8},{1,9},{2,10},{3,11},{4,12},{5,13},{6,14},{7,15},{8,16},{9,17... | collective-permute-start | bytes 196616 | tf_op jit(solution)/shard_map/ppermute | solution.py:319
  139.1 2.2 %collective-permute-done.22 = bf16[64,512]{1,0:T(8,128)(2,1)S(1)} collective-permute-done((bf16[64,512]{1,0:T(8,128)(2,1)S(1)}, bf16[64,512]{1,0:T(8,128)(2,1)S(1)}, u32[]{:S(2)}, u32[]{:S(2)}) %collective-permute-start.22) | collective-permute-done | bytes 65568 | tf_op jit(solution)/shard_map/ppermute | solution.py:319
  141.4 1.3 collective-permute-done.20
  142.8 1.5 collective-permute-start.21
  144.3 1.9 %collective-permute-start.23 = (bf16[128,512]{1,0:T(8,128)(2,1)S(1)}, bf16[128,512]{1,0:T(8,128)(2,1)S(1)}, u32[]{:S(2)}, u32[]{:S(2)}) collective-permute-start(bf16[128,512]{1,0:T(8,128)(2,1)S(1)} %pad_maximum_fusion.5), channel_id=1, source_target_pairs={{0,24},{1,25},{2,26},{3,27},{4,28},{5,29},{6,30},{7,31},{8,0},{9,1... | collective-permute-start | bytes 393224 | tf_op jit(solution)/shard_map/ppermute | solution.py:319
  146.3 3.3 %collective-permute-start.35 = (bf16[128,512]{1,0:T(8,128)(2,1)S(1)}, bf16[128,512]{1,0:T(8,128)(2,1)S(1)}, u32[]{:S(2)}, u32[]{:S(2)}) collective-permute-start(bf16[128,512]{1,0:T(8,128)(2,1)S(1)} %get-tuple-element.35), channel_id=1, source_target_pairs={{0,7},{1,0},{2,1},{3,2},{4,3},{5,4},{6,5},{7,6},{8,15},{9,8},{10,9... | collective-permute-start | bytes 393224 | tf_op jit(solution)/shard_map/ppermute | solution.py:314
  149.6 2.5 %collective-permute-done.35.refs_9_ = bf16[128,512]{1,0:T(8,128)(2,1)S(1)} collective-permute-done((bf16[128,512]{1,0:T(8,128)(2,1)S(1)}, bf16[128,512]{1,0:T(8,128)(2,1)S(1)}, u32[]{:S(2)}, u32[]{:S(2)}) %collective-permute-start.35) | collective-permute-done | bytes 131104 | tf_op jit(solution)/shard_map/ppermute | solution.py:314
  152.1 3.7 %collective-permute-done.31.refs_8_ = bf16[128,512]{1,0:T(8,128)(2,1)S(1)} collective-permute-done((bf16[128,512]{1,0:T(8,128)(2,1)S(1)}, bf16[128,512]{1,0:T(8,128)(2,1)S(1)}, u32[]{:S(2)}, u32[]{:S(2)}) %collective-permute-start.31) | collective-permute-done | bytes 131104 | tf_op jit(solution)/shard_map/ppermute | solution.py:314
  155.8 1.3 finish.1
  (106 shorter events, 10.6 us)
Async XLA Ops:
  0.0 1.0 copy-start.4
  1.5 37.2 %collective-permute-start.11 = (bf16[512,512]{1,0:T(8,128)(2,1)S(1)}, bf16[512,512]{1,0:T(8,128)(2,1)S(1)}, u32[]{:S(2)}, u32[]{:S(2)}) collective-permute-start(bf16[512,512]{1,0:T(8,128)(2,1)S(1)} %norm.1.refs_1_.refs_0_), channel_id=1, source_target_pairs={{0,32},{32,0},{64,96},{96,64},{128,160},{160,128},{192,224},{224,1... | collective-permute-start | bytes 1572872 | tf_op jit(solution)/shard_map/ppermute | solution.py:309
  1.6 34.2 %collective-permute-start.8 = (bf16[512,512]{1,0:T(8,128)(2,1)S(1)}, bf16[512,512]{1,0:T(8,128)(2,1)S(1)}, u32[]{:S(2)}, u32[]{:S(2)}) collective-permute-start(bf16[512,512]{1,0:T(8,128)(2,1)S(1)} %norm.1.refs_1_.refs_0_), channel_id=1, source_target_pairs={{0,64},{32,96},{64,128},{96,160},{128,192},{160,224},{192,0},{224,... | collective-permute-start | bytes 1572872 | tf_op jit(solution)/shard_map/ppermute | solution.py:304
  3.2 14.0 %collective-permute-start.5 = (bf16[512,512]{1,0:T(8,128)(2,1)S(1)}, bf16[512,512]{1,0:T(8,128)(2,1)S(1)}, u32[]{:S(2)}, u32[]{:S(2)}) collective-permute-start(bf16[512,512]{1,0:T(8,128)(2,1)S(1)} %norm.1.refs_1_.refs_0_), channel_id=1, source_target_pairs={{0,192},{32,224},{64,0},{96,32},{128,64},{160,96},{192,128},{224,1... | collective-permute-start | bytes 1572872 | tf_op jit(solution)/shard_map/ppermute | solution.py:304
  4.9 3.8 %collective-permute-start = (s32[256]{0:T(256)}, s32[256]{0:T(256)S(1)}, u32[]{:S(2)}, u32[]{:S(2)}) collective-permute-start(s32[256]{0:T(256)} %param.13), channel_id=1, source_target_pairs={{0,7},{1,0},{2,1},{3,2},{4,3},{5,4},{6,5},{7,6},{8,15},{9,8},{10,9... | collective-permute-start | bytes 3080 | tf_op jit(solution)/shard_map/ppermute | solution.py:314
  9.4 10.7 %collective-permute-start.1 = (s32[512]{0:T(512)S(1)}, s32[512]{0:T(512)S(1)}, u32[]{:S(2)}, u32[]{:S(2)}) collective-permute-start(s32[512]{0:T(512)S(1)} %pad_add_fusion.2), channel_id=1, source_target_pairs={{0,6},{1,7},{2,0},{3,1},{4,2},{5,3},{6,4},{7,5},{8,14},{9,15},{10,... | collective-permute-start | bytes 6152 | tf_op jit(solution)/shard_map/ppermute | solution.py:314
  17.2 18.7 %collective-permute-start.6 = (bf16[512,512]{1,0:T(8,128)(2,1)S(1)}, bf16[512,512]{1,0:T(8,128)(2,1)S(1)}, u32[]{:S(2)}, u32[]{:S(2)}) collective-permute-start(bf16[512,512]{1,0:T(8,128)(2,1)S(1)} %collective-permute-done.5.refs_1_.refs_2_), channel_id=1, source_target_pairs={{0,192},{32,224},{64,0},{96,32},{128,64},{160,96},{192,128},{224,1... | collective-permute-start | bytes 1572872 | tf_op jit(solution)/shard_map/ppermute | solution.py:304
  20.8 7.5 %collective-permute-start.2 = (s32[1024]{0:T(1024)S(1)}, s32[1024]{0:T(1024)S(1)}, u32[]{:S(2)}, u32[]{:S(2)}) collective-permute-start(s32[1024]{0:T(1024)S(1)} %pad_add_fusion.1), channel_id=1, source_target_pairs={{0,4},{1,5},{2,6},{3,7},{4,0},{5,1},{6,2},{7,3},{8,12},{9,13},{10,... | collective-permute-start | bytes 12296 | tf_op jit(solution)/shard_map/ppermute | solution.py:314
  29.0 4.4 %collective-permute-start.3 = (s32[2048]{0:T(1024)S(1)}, s32[2048]{0:T(1024)S(1)}, u32[]{:S(2)}, u32[]{:S(2)}) collective-permute-start(s32[2048]{0:T(1024)S(1)} %pad_add_fusion), channel_id=1, source_target_pairs={{0,24},{1,25},{2,26},{3,27},{4,28},{5,29},{6,30},{7,31},{8,0},{9,1... | collective-permute-start | bytes 24584 | tf_op jit(solution)/shard_map/ppermute | solution.py:319
  32.0 8.3 %collective-permute-start.10 = (bf16[512,512]{1,0:T(8,128)(2,1)S(1)}, bf16[512,512]{1,0:T(8,128)(2,1)S(1)}, u32[]{:S(2)}, u32[]{:S(2)}) collective-permute-start(bf16[512,512]{1,0:T(8,128)(2,1)S(1)} %collective-permute-done.5.refs_1_.refs_2_), channel_id=1, source_target_pairs={{0,32},{32,0},{64,96},{96,64},{128,160},{160,128},{192,224},{224,1... | collective-permute-start | bytes 1572872 | tf_op jit(solution)/shard_map/ppermute | solution.py:309
  33.4 5.2 %collective-permute-start.4 = (s32[4096]{0:T(1024)S(1)}, s32[4096]{0:T(1024)S(1)}, u32[]{:S(2)}, u32[]{:S(2)}) collective-permute-start(s32[4096]{0:T(1024)S(1)} %get-tuple-element.51), channel_id=1, source_target_pairs={{0,16},{1,17},{2,18},{3,19},{4,20},{5,21},{6,22},{7,23},{8,24},{9,... | collective-permute-start | bytes 49160 | tf_op jit(solution)/shard_map/ppermute | solution.py:319
  35.9 6.1 %collective-permute-start.9 = (bf16[512,512]{1,0:T(8,128)(2,1)S(1)}, bf16[512,512]{1,0:T(8,128)(2,1)S(1)}, u32[]{:S(2)}, u32[]{:S(2)}) collective-permute-start(bf16[512,512]{1,0:T(8,128)(2,1)S(1)} %collective-permute-done.8.refs_1_.refs_6_), channel_id=1, source_target_pairs={{0,32},{32,0},{64,96},{96,64},{128,160},{160,128},{192,224},{224,1... | collective-permute-start | bytes 1572872 | tf_op jit(solution)/shard_map/ppermute | solution.py:309
  35.9 7.7 %collective-permute-start.7 = (bf16[512,512]{1,0:T(8,128)(2,1)S(1)}, bf16[512,512]{1,0:T(8,128)(2,1)S(1)}, u32[]{:S(2)}, u32[]{:S(2)}) collective-permute-start(bf16[512,512]{1,0:T(8,128)(2,1)S(1)} %collective-permute-done.6.refs_1_.refs_4_), channel_id=1, source_target_pairs={{0,32},{32,0},{64,96},{96,64},{128,160},{160,128},{192,224},{224,1... | collective-permute-start | bytes 1572872 | tf_op jit(solution)/shard_map/ppermute | solution.py:309
  36.5 1.2 copy-start.2
  43.5 1.6 %copy-start = (bf16[2048,512]{1,0:T(8,128)(2,1)S(1)}, bf16[2048,512]{1,0:T(8,128)(2,1)}, u32[]{:S(2)}) copy-start(bf16[2048,512]{1,0:T(8,128)(2,1)} %k_ref.9) | copy-start | bytes 6291460
  43.5 2.2 %copy-start.1 = (bf16[2048,512]{1,0:T(8,128)(2,1)S(1)}, bf16[2048,512]{1,0:T(8,128)(2,1)}, u32[]{:S(2)}) copy-start(bf16[2048,512]{1,0:T(8,128)(2,1)} %v_ref.9) | copy-start | bytes 6291460
  43.6 2.2 %copy-start.10 = (s32[16]{0:T(128)S(1)}, s32[16]{0:T(128)}, u32[]{:S(2)}) copy-start(s32[16]{0:T(128)} %constant.131.clone.order_ref) | copy-start | bytes 196
  45.8 2.6 %copy-start.9 = (s32[24]{0:T(128)S(1)}, s32[24]{0:T(128)}, u32[]{:S(2)}) copy-start(s32[24]{0:T(128)} %constant.130.clone.order_ref) | copy-start | bytes 292
  48.3 12.8 %copy-start.8 = (s32[32]{0:T(128)S(1)}, s32[32]{0:T(128)}, u32[]{:S(2)}) copy-start(s32[32]{0:T(128)} %constant.132.clone.order_ref) | copy-start | bytes 388
  53.7 14.2 %copy-start.7 = (s32[16]{0:T(128)S(1)}, s32[16]{0:T(128)}, u32[]{:S(2)}) copy-start(s32[16]{0:T(128)} %constant.133.clone.order_ref) | copy-start | bytes 196
  53.7 24.9 %collective-permute-start.12 = (bf16[2,128,512]{2,1,0:T(8,128)(2,1)S(1)}, bf16[2,128,512]{2,1,0:T(8,128)(2,1)S(1)}, u32[]{:S(2)}, u32[]{:S(2)}) collective-permute-start(bf16[2,128,512]{2,1,0:T(8,128)(2,1)S(1)} %get-tuple-element.20), channel_id=1, source_target_pairs={{0,1},{1,2},{2,3},{3,4},{4,5},{5,6},{6,7},{7,0},{8,9},{9,10},{10,1... | collective-permute-start | bytes 786440 | tf_op jit(solution)/shard_map/ppermute | solution.py:314
  57.3 21.1 %collective-permute-start.16 = (bf16[2,128,512]{2,1,0:T(8,128)(2,1)S(1)}, bf16[2,128,512]{2,1,0:T(8,128)(2,1)S(1)}, u32[]{:S(2)}, u32[]{:S(2)}) collective-permute-start(bf16[2,128,512]{2,1,0:T(8,128)(2,1)S(1)} %get-tuple-element.25), channel_id=1, source_target_pairs={{0,7},{1,0},{2,1},{3,2},{4,3},{5,4},{6,5},{7,6},{8,15},{9,8},{10,9... | collective-permute-start | bytes 786440 | tf_op jit(solution)/shard_map/ppermute | solution.py:314
  57.3 25.4 %collective-permute-start.24 = (bf16[4,128,512]{2,1,0:T(8,128)(2,1)S(1)}, bf16[4,128,512]{2,1,0:T(8,128)(2,1)S(1)}, u32[]{:S(2)}, u32[]{:S(2)}) collective-permute-start(bf16[4,128,512]{2,1,0:T(8,128)(2,1)S(1)} %get-tuple-element.29), channel_id=1, source_target_pairs={{0,8},{1,9},{2,10},{3,11},{4,12},{5,13},{6,14},{7,15},{8,16},{9,17... | collective-permute-start | bytes 1572872 | tf_op jit(solution)/shard_map/ppermute | solution.py:319
  59.9 21.0 %collective-permute-start.26 = (bf16[4,128,512]{2,1,0:T(8,128)(2,1)S(1)}, bf16[4,128,512]{2,1,0:T(8,128)(2,1)S(1)}, u32[]{:S(2)}, u32[]{:S(2)}) collective-permute-start(bf16[4,128,512]{2,1,0:T(8,128)(2,1)S(1)} %get-tuple-element.32), channel_id=1, source_target_pairs={{0,24},{1,25},{2,26},{3,27},{4,28},{5,29},{6,30},{7,31},{8,0},{9,1... | collective-permute-start | bytes 1572872 | tf_op jit(solution)/shard_map/ppermute | solution.py:319
  67.8 4.1 %copy-start.6 = (s32[40]{0:T(128)S(1)}, s32[40]{0:T(128)}, u32[]{:S(2)}) copy-start(s32[40]{0:T(128)} %constant.134.clone.order_ref) | copy-start | bytes 484
  78.4 17.0 %copy-start.3 = (bf16[512,1024]{1,0:T(8,128)(2,1)S(1)}, bf16[512,1024]{1,0:T(8,128)(2,1)}, u32[]{:S(2)}) copy-start(bf16[512,1024]{1,0:T(8,128)(2,1)} %w_ref.3) | copy-start | bytes 3145732
  78.6 14.1 %collective-permute-start.17 = (bf16[4,128,512]{2,1,0:T(8,128)(2,1)S(1)}, bf16[4,128,512]{2,1,0:T(8,128)(2,1)S(1)}, u32[]{:S(2)}, u32[]{:S(2)}) collective-permute-start(bf16[4,128,512]{2,1,0:T(8,128)(2,1)S(1)} %pad_maximum_fusion.3), channel_id=1, source_target_pairs={{0,7},{1,0},{2,1},{3,2},{4,3},{5,4},{6,5},{7,6},{8,15},{9,8},{10,9... | collective-permute-start | bytes 1572872 | tf_op jit(solution)/shard_map/ppermute | solution.py:314
  78.8 15.3 %collective-permute-start.13 = (bf16[4,128,512]{2,1,0:T(8,128)(2,1)S(1)}, bf16[4,128,512]{2,1,0:T(8,128)(2,1)S(1)}, u32[]{:S(2)}, u32[]{:S(2)}) collective-permute-start(bf16[4,128,512]{2,1,0:T(8,128)(2,1)S(1)} %pad_maximum_fusion.2), channel_id=1, source_target_pairs={{0,1},{1,2},{2,3},{3,4},{4,5},{5,6},{6,7},{7,0},{8,9},{9,10},{10,1... | collective-permute-start | bytes 1572872 | tf_op jit(solution)/shard_map/ppermute | solution.py:314
  81.2 29.4 %collective-permute-start.27 = (bf16[8,128,512]{2,1,0:T(8,128)(2,1)S(1)}, bf16[8,128,512]{2,1,0:T(8,128)(2,1)S(1)}, u32[]{:S(2)}, u32[]{:S(2)}) collective-permute-start(bf16[8,128,512]{2,1,0:T(8,128)(2,1)S(1)} %pad_maximum_fusion.1), channel_id=1, source_target_pairs={{0,24},{1,25},{2,26},{3,27},{4,28},{5,29},{6,30},{7,31},{8,0},{9,1... | collective-permute-start | bytes 3145736 | tf_op jit(solution)/shard_map/ppermute | solution.py:319
  83.0 27.6 %collective-permute-start.25 = (bf16[8,128,512]{2,1,0:T(8,128)(2,1)S(1)}, bf16[8,128,512]{2,1,0:T(8,128)(2,1)S(1)}, u32[]{:S(2)}, u32[]{:S(2)}) collective-permute-start(bf16[8,128,512]{2,1,0:T(8,128)(2,1)S(1)} %pad_maximum_fusion), channel_id=1, source_target_pairs={{0,8},{1,9},{2,10},{3,11},{4,12},{5,13},{6,14},{7,15},{8,16},{9,17... | collective-permute-start | bytes 3145736 | tf_op jit(solution)/shard_map/ppermute | solution.py:319
  92.8 14.8 %collective-permute-start.18 = (bf16[4,128,512]{2,1,0:T(8,128)(2,1)S(1)}, bf16[4,128,512]{2,1,0:T(8,128)(2,1)S(1)}, u32[]{:S(2)}, u32[]{:S(2)}) collective-permute-start(bf16[4,128,512]{2,1,0:T(8,128)(2,1)S(1)} %add_convert_fusion.3), channel_id=1, source_target_pairs={{0,7},{1,0},{2,1},{3,2},{4,3},{5,4},{6,5},{7,6},{8,15},{9,8},{10,9... | collective-permute-start | bytes 1572872 | tf_op jit(solution)/shard_map/ppermute | solution.py:314
  94.3 16.0 %collective-permute-start.14 = (bf16[4,128,512]{2,1,0:T(8,128)(2,1)S(1)}, bf16[4,128,512]{2,1,0:T(8,128)(2,1)S(1)}, u32[]{:S(2)}, u32[]{:S(2)}) collective-permute-start(bf16[4,128,512]{2,1,0:T(8,128)(2,1)S(1)} %add_convert_fusion.5), channel_id=1, source_target_pairs={{0,1},{1,2},{2,3},{3,4},{4,5},{5,6},{6,7},{7,0},{8,9},{9,10},{10,1... | collective-permute-start | bytes 1572872 | tf_op jit(solution)/shard_map/ppermute | solution.py:314
  95.4 60.4 %copy-start.5 = (bf16[512,512]{1,0:T(8,128)(2,1)S(1)}, bf16[512,512]{1,0:T(8,128)(2,1)}, u32[]{:S(2)}) copy-start(bf16[512,512]{1,0:T(8,128)(2,1)} %refs_11_.1) | copy-start | bytes 1572868
  107.8 29.1 %collective-permute-start.19 = (bf16[4,128,512]{2,1,0:T(8,128)(2,1)S(1)}, bf16[4,128,512]{2,1,0:T(8,128)(2,1)S(1)}, u32[]{:S(2)}, u32[]{:S(2)}) collective-permute-start(bf16[4,128,512]{2,1,0:T(8,128)(2,1)S(1)} %add_convert_fusion.2), channel_id=1, source_target_pairs={{0,7},{1,0},{2,1},{3,2},{4,3},{5,4},{6,5},{7,6},{8,15},{9,8},{10,9... | collective-permute-start | bytes 1572872 | tf_op jit(solution)/shard_map/ppermute | solution.py:314
  110.4 26.5 %collective-permute-start.15 = (bf16[4,128,512]{2,1,0:T(8,128)(2,1)S(1)}, bf16[4,128,512]{2,1,0:T(8,128)(2,1)S(1)}, u32[]{:S(2)}, u32[]{:S(2)}) collective-permute-start(bf16[4,128,512]{2,1,0:T(8,128)(2,1)S(1)} %add_convert_fusion.4), channel_id=1, source_target_pairs={{0,1},{1,2},{2,3},{3,4},{4,5},{5,6},{6,7},{7,0},{8,9},{9,10},{10,1... | collective-permute-start | bytes 1572872 | tf_op jit(solution)/shard_map/ppermute | solution.py:314
  110.7 12.5 %collective-permute-start.32 = (bf16[64,512]{1,0:T(8,128)(2,1)S(1)}, bf16[64,512]{1,0:T(8,128)(2,1)S(1)}, u32[]{:S(2)}, u32[]{:S(2)}) collective-permute-start(bf16[64,512]{1,0:T(8,128)(2,1)S(1)} %get-tuple-element.40), channel_id=1, source_target_pairs={{0,7},{1,0},{2,1},{3,2},{4,3},{5,4},{6,5},{7,6},{8,15},{9,8},{10,9... | collective-permute-start | bytes 196616 | tf_op jit(solution)/shard_map/ppermute | solution.py:314
  113.9 13.1 %collective-permute-start.28 = (bf16[64,512]{1,0:T(8,128)(2,1)S(1)}, bf16[64,512]{1,0:T(8,128)(2,1)S(1)}, u32[]{:S(2)}, u32[]{:S(2)}) collective-permute-start(bf16[64,512]{1,0:T(8,128)(2,1)S(1)} %get-tuple-element.42), channel_id=1, source_target_pairs={{0,1},{1,2},{2,3},{3,4},{4,5},{5,6},{6,7},{7,0},{8,9},{9,10},{10,1... | collective-permute-start | bytes 196616 | tf_op jit(solution)/shard_map/ppermute | solution.py:314
  127.1 6.3 %collective-permute-start.29 = (bf16[128,512]{1,0:T(8,128)(2,1)S(1)}, bf16[128,512]{1,0:T(8,128)(2,1)S(1)}, u32[]{:S(2)}, u32[]{:S(2)}) collective-permute-start(bf16[128,512]{1,0:T(8,128)(2,1)S(1)} %pad_maximum_fusion.6), channel_id=1, source_target_pairs={{0,1},{1,2},{2,3},{3,4},{4,5},{5,6},{6,7},{7,0},{8,9},{9,10},{10,1... | collective-permute-start | bytes 393224 | tf_op jit(solution)/shard_map/ppermute | solution.py:314
  127.2 6.1 %collective-permute-start.33 = (bf16[128,512]{1,0:T(8,128)(2,1)S(1)}, bf16[128,512]{1,0:T(8,128)(2,1)S(1)}, u32[]{:S(2)}, u32[]{:S(2)}) collective-permute-start(bf16[128,512]{1,0:T(8,128)(2,1)S(1)} %pad_maximum_fusion.7), channel_id=1, source_target_pairs={{0,7},{1,0},{2,1},{3,2},{4,3},{5,4},{6,5},{7,6},{8,15},{9,8},{10,9... | collective-permute-start | bytes 393224 | tf_op jit(solution)/shard_map/ppermute | solution.py:314
  133.5 12.7 %collective-permute-start.34 = (bf16[128,512]{1,0:T(8,128)(2,1)S(1)}, bf16[128,512]{1,0:T(8,128)(2,1)S(1)}, u32[]{:S(2)}, u32[]{:S(2)}) collective-permute-start(bf16[128,512]{1,0:T(8,128)(2,1)S(1)} %get-tuple-element.37), channel_id=1, source_target_pairs={{0,7},{1,0},{2,1},{3,2},{4,3},{5,4},{6,5},{7,6},{8,15},{9,8},{10,9... | collective-permute-start | bytes 393224 | tf_op jit(solution)/shard_map/ppermute | solution.py:314
  136.9 9.3 %collective-permute-start.30 = (bf16[128,512]{1,0:T(8,128)(2,1)S(1)}, bf16[128,512]{1,0:T(8,128)(2,1)S(1)}, u32[]{:S(2)}, u32[]{:S(2)}) collective-permute-start(bf16[128,512]{1,0:T(8,128)(2,1)S(1)} %get-tuple-element.38), channel_id=1, source_target_pairs={{0,1},{1,2},{2,3},{3,4},{4,5},{5,6},{6,7},{7,0},{8,9},{9,10},{10,1... | collective-permute-start | bytes 393224 | tf_op jit(solution)/shard_map/ppermute | solution.py:314
  137.0 4.3 %collective-permute-start.22 = (bf16[64,512]{1,0:T(8,128)(2,1)S(1)}, bf16[64,512]{1,0:T(8,128)(2,1)S(1)}, u32[]{:S(2)}, u32[]{:S(2)}) collective-permute-start(bf16[64,512]{1,0:T(8,128)(2,1)S(1)} %get-tuple-element.46), channel_id=1, source_target_pairs={{0,24},{1,25},{2,26},{3,27},{4,28},{5,29},{6,30},{7,31},{8,0},{9,1... | collective-permute-start | bytes 196616 | tf_op jit(solution)/shard_map/ppermute | solution.py:319
  137.1 5.6 %collective-permute-start.20 = (bf16[64,512]{1,0:T(8,128)(2,1)S(1)}, bf16[64,512]{1,0:T(8,128)(2,1)S(1)}, u32[]{:S(2)}, u32[]{:S(2)}) collective-permute-start(bf16[64,512]{1,0:T(8,128)(2,1)S(1)} %get-tuple-element.48), channel_id=1, source_target_pairs={{0,8},{1,9},{2,10},{3,11},{4,12},{5,13},{6,14},{7,15},{8,16},{9,17... | collective-permute-start | bytes 196616 | tf_op jit(solution)/shard_map/ppermute | solution.py:319
  142.8 6.9 %collective-permute-start.21 = (bf16[128,512]{1,0:T(8,128)(2,1)S(1)}, bf16[128,512]{1,0:T(8,128)(2,1)S(1)}, u32[]{:S(2)}, u32[]{:S(2)}) collective-permute-start(bf16[128,512]{1,0:T(8,128)(2,1)S(1)} %pad_maximum_fusion.4), channel_id=1, source_target_pairs={{0,8},{1,9},{2,10},{3,11},{4,12},{5,13},{6,14},{7,15},{8,16},{9,17... | collective-permute-start | bytes 393224 | tf_op jit(solution)/shard_map/ppermute | solution.py:319
  144.3 5.4 %collective-permute-start.23 = (bf16[128,512]{1,0:T(8,128)(2,1)S(1)}, bf16[128,512]{1,0:T(8,128)(2,1)S(1)}, u32[]{:S(2)}, u32[]{:S(2)}) collective-permute-start(bf16[128,512]{1,0:T(8,128)(2,1)S(1)} %pad_maximum_fusion.5), channel_id=1, source_target_pairs={{0,24},{1,25},{2,26},{3,27},{4,28},{5,29},{6,30},{7,31},{8,0},{9,1... | collective-permute-start | bytes 393224 | tf_op jit(solution)/shard_map/ppermute | solution.py:319
  146.3 5.8 %collective-permute-start.35 = (bf16[128,512]{1,0:T(8,128)(2,1)S(1)}, bf16[128,512]{1,0:T(8,128)(2,1)S(1)}, u32[]{:S(2)}, u32[]{:S(2)}) collective-permute-start(bf16[128,512]{1,0:T(8,128)(2,1)S(1)} %get-tuple-element.35), channel_id=1, source_target_pairs={{0,7},{1,0},{2,1},{3,2},{4,3},{5,4},{6,5},{7,6},{8,15},{9,8},{10,9... | collective-permute-start | bytes 393224 | tf_op jit(solution)/shard_map/ppermute | solution.py:314
  149.6 6.2 %collective-permute-start.31 = (bf16[128,512]{1,0:T(8,128)(2,1)S(1)}, bf16[128,512]{1,0:T(8,128)(2,1)S(1)}, u32[]{:S(2)}, u32[]{:S(2)}) collective-permute-start(bf16[128,512]{1,0:T(8,128)(2,1)S(1)} %get-tuple-element.36), channel_id=1, source_target_pairs={{0,1},{1,2},{2,3},{3,4},{4,5},{5,6},{6,7},{7,0},{8,9},{9,10},{10,1... | collective-permute-start | bytes 393224 | tf_op jit(solution)/shard_map/ppermute | solution.py:314

commit v5 on v4

--- a/solution.py
+++ b/solution.py
@@ -362,9 +362,9 @@
     scale = 0.5 / math.sqrt(width // H)
     chip = CORES * part_rows
     near_rows = [normed, other]
-    table = project(None, 0, total_rows, near_rows, w_query, scale)
-    table = project(table, 1 * chip, total_rows, ahead_rows, w_query, scale)
-    table = project(table, 3 * chip, total_rows, behind_rows, w_query, scale)
+    table = project(None, 0, total_rows, near_rows, w_query, scale, unrolled=True)
+    table = project(table, 1 * chip, total_rows, ahead_rows, w_query, scale, unrolled=True)
+    table = project(table, 3 * chip, total_rows, behind_rows, w_query, scale, unrolled=True)
     far_rows = [far, swap(far)]
     table = project(table, 2 * chip, total_rows, far_rows, w_query, scale, unrolled=True)
 

time: 157 us -> 155 us (0.987)
  the two profiles are of different devices: /device:TPU:128 before, /device:TPU:4 now
where the time goes in v5:
time: 155 us
  starting transfers between devices  66.2 us (43%)
  waiting for transfers between devices  46 us (30%)
  Pallas kernels  31.9 us (21%)
  other arithmetic  6.54 us (4%)
  local copies, waits for them, and re-layouts  3.83 us (2%)
    ppermute x19, starting transfers between devices, z_shift(): lax.ppermute(value, 'shard', [(y * nz + z, y * nz + (z + k) % nz) for y i...  42.9 us
    ppermute x19, waiting for transfers between devices, z_shift(): lax.ppermute(value, 'shard', [(y * nz + z, y * nz + (z + k) % nz) for y i...  36.7 us
    pallas_call x5, Pallas kernels, attend(): pl.pallas_call(functools.partial(attend_kernel, tuple(sizes), math.gcd(ro...  25.1 us
    ppermute x10, starting transfers between devices, y_shift(): lax.ppermute(value, 'shard', [(y * nz + z, (y + k) % NY * nz + z) for y i...  20.3 us
    ppermute x10, waiting for transfers between devices, y_shift(): lax.ppermute(value, 'shard', [(y * nz + z, (y + k) % NY * nz + z) for y i...  6.42 us
    unnamed x25, local copies, waits for them, and re-layouts  3.66 us
    pallas_call x4, Pallas kernels, project(): pl.pallas_call(kernel, out_shape=jax.ShapeDtypeStruct((total * width // L...  3.34 us
  transfers between devices with their start and end apart: 36, of which 15 were waited for; matrix products, arithmetic and copies ran while one was open for 4% of the time, Pallas kernels for 14%

profile of v5, /device:TPU:4, one launch (start us, length us, event | category | flops | bytes accessed | tf_op | source)
XLA Modules:
  0.0 155.0 jit_solution(12615708585949763043)
XLA Ops:
  0.0 1.0 copy-done.4
  1.6 1.3 collective-permute-start.8
  2.9 0.8 collective-permute-start.5
  3.7 5.9 %collective-permute-start = (s32[256]{0:T(256)}, s32[256]{0:T(256)S(1)}, u32[]{:S(2)}, u32[]{:S(2)}) collective-permute-start(s32[256]{0:T(256)} %param.13), channel_id=1, source_target_pairs={{0,7},{1,0},{2,1},{3,2},{4,3},{5,4},{6,5},{7,6},{8,15},{9,8},{10,9... | collective-permute-start | bytes 3080 | tf_op jit(solution)/shard_map/ppermute | solution.py:314
  9.6 0.9 convert_reduce_fusion
  12.7 1.8 %collective-permute-start.1 = (s32[512]{0:T(512)S(1)}, s32[512]{0:T(512)S(1)}, u32[]{:S(2)}, u32[]{:S(2)}) collective-permute-start(s32[512]{0:T(512)S(1)} %pad_add_fusion.2), channel_id=1, source_target_pairs={{0,6},{1,7},{2,0},{3,1},{4,2},{5,3},{6,4},{7,5},{8,14},{9,15},{10,... | collective-permute-start | bytes 6152 | tf_op jit(solution)/shard_map/ppermute | solution.py:314
  14.5 2.8 %collective-permute-done.5.refs_1_.refs_2_ = bf16[512,512]{1,0:T(8,128)(2,1)S(1)} collective-permute-done((bf16[512,512]{1,0:T(8,128)(2,1)S(1)}, bf16[512,512]{1,0:T(8,128)(2,1)S(1)}, u32[]{:S(2)}, u32[]{:S(2)}) %collective-permute-start.5) | collective-permute-done | bytes 524320 | tf_op jit(solution)/shard_map/ppermute | solution.py:304
  18.4 7.2 %collective-permute-start.2 = (s32[1024]{0:T(1024)S(1)}, s32[1024]{0:T(1024)S(1)}, u32[]{:S(2)}, u32[]{:S(2)}) collective-permute-start(s32[1024]{0:T(1024)S(1)} %pad_add_fusion.1), channel_id=1, source_target_pairs={{0,4},{1,5},{2,6},{3,7},{4,0},{5,1},{6,2},{7,3},{8,12},{9,13},{10,... | collective-permute-start | bytes 12296 | tf_op jit(solution)/shard_map/ppermute | solution.py:314
  25.6 1.6 %collective-permute-done.2 = s32[1024]{0:T(1024)S(1)} collective-permute-done((s32[1024]{0:T(1024)S(1)}, s32[1024]{0:T(1024)S(1)}, u32[]{:S(2)}, u32[]{:S(2)}) %collective-permute-start.2) | collective-permute-done | bytes 4128 | tf_op jit(solution)/shard_map/ppermute | solution.py:314
  27.9 3.0 %collective-permute-start.3 = (s32[2048]{0:T(1024)S(1)}, s32[2048]{0:T(1024)S(1)}, u32[]{:S(2)}, u32[]{:S(2)}) collective-permute-start(s32[2048]{0:T(1024)S(1)} %pad_add_fusion), channel_id=1, source_target_pairs={{0,24},{1,25},{2,26},{3,27},{4,28},{5,29},{6,30},{7,31},{8,0},{9,1... | collective-permute-start | bytes 24584 | tf_op jit(solution)/shard_map/ppermute | solution.py:319
  30.9 1.4 collective-permute-done.3
  32.2 2.5 %collective-permute-start.4 = (s32[4096]{0:T(1024)S(1)}, s32[4096]{0:T(1024)S(1)}, u32[]{:S(2)}, u32[]{:S(2)}) collective-permute-start(s32[4096]{0:T(1024)S(1)} %get-tuple-element.51), channel_id=1, source_target_pairs={{0,16},{1,17},{2,18},{3,19},{4,20},{5,21},{6,22},{7,23},{8,24},{9,... | collective-permute-start | bytes 49160 | tf_op jit(solution)/shard_map/ppermute | solution.py:319
  35.3 1.2 copy-done.2
  36.6 0.9 collective-permute-done.4
  38.4 0.8 project.5.refs_3_
  39.3 0.8 project.6.refs_3_
  40.2 0.8 project.7.table_ref
  42.3 3.0 %attend.7 = (bf16[4,128,512]{2,1,0:T(8,128)(2,1)S(1)}, bf16[4,128,512]{2,1,0:T(8,128)(2,1)S(1)}) custom-call(s32[8192]{0:T(1024)S(1)} %fusion.24.index_ref, s32[32]{0:T(128)S(1)} %convert_reduce_fusion.1.count_ref, s32[64]{0:T(128)S(1)} %select_reduce_fusion.block_ref, s32[16]{0:T(128)S(1)} %copy-done.10, f32[16384,128]{1,0:T(8,128)S(1)} %project.7.table_ref, ...), custom_call_target="tpu_custom_call" | custom-call | flops 536870912 | bytes 2097152 | tf_op jit(solution)/shard_map/attend/pallas_call | solution.py:237
  45.5 4.5 %attend.6 = (bf16[2,128,512]{2,1,0:T(8,128)(2,1)S(1)}, bf16[2,128,512]{2,1,0:T(8,128)(2,1)S(1)}, bf16[4,128,512]{2,1,0:T(8,128)(2,1)S(1)}, bf16[4,128,512]{2,1,0:T(8,128)(2,1)S(1)}) custom-call(s32[8192]{0:T(1024)S(1)} %fusion.24.index_ref, s32[32]{0:T(128)S(1)} %convert_reduce_fusion.1.count_ref, s32[64]{0:T(128)S(1)} %select_reduce_fusion.block_ref, ...), custom_call_target="tpu_custom_call" | custom-call | flops 805306368 | bytes 3145728 | tf_op jit(solution)/shard_map/attend/pallas_call | solution.py:237
  49.9 2.2 %collective-permute-start.12 = (bf16[2,128,512]{2,1,0:T(8,128)(2,1)S(1)}, bf16[2,128,512]{2,1,0:T(8,128)(2,1)S(1)}, u32[]{:S(2)}, u32[]{:S(2)}) collective-permute-start(bf16[2,128,512]{2,1,0:T(8,128)(2,1)S(1)} %get-tuple-element.20), channel_id=1, source_target_pairs={{0,1},{1,2},{2,3},{3,4},{4,5},{5,6},{6,7},{7,0},{8,9},{9,10},{10,1... | collective-permute-start | bytes 786440 | tf_op jit(solution)/shard_map/ppermute | solution.py:314
  52.1 3.5 %collective-permute-start.16 = (bf16[2,128,512]{2,1,0:T(8,128)(2,1)S(1)}, bf16[2,128,512]{2,1,0:T(8,128)(2,1)S(1)}, u32[]{:S(2)}, u32[]{:S(2)}) collective-permute-start(bf16[2,128,512]{2,1,0:T(8,128)(2,1)S(1)} %get-tuple-element.25), channel_id=1, source_target_pairs={{0,7},{1,0},{2,1},{3,2},{4,3},{5,4},{6,5},{7,6},{8,15},{9,8},{10,9... | collective-permute-start | bytes 786440 | tf_op jit(solution)/shard_map/ppermute | solution.py:314
  55.8 4.4 %collective-permute-start.26 = (bf16[4,128,512]{2,1,0:T(8,128)(2,1)S(1)}, bf16[4,128,512]{2,1,0:T(8,128)(2,1)S(1)}, u32[]{:S(2)}, u32[]{:S(2)}) collective-permute-start(bf16[4,128,512]{2,1,0:T(8,128)(2,1)S(1)} %get-tuple-element.32), channel_id=1, source_target_pairs={{0,24},{1,25},{2,26},{3,27},{4,28},{5,29},{6,30},{7,31},{8,0},{9,1... | collective-permute-start | bytes 1572872 | tf_op jit(solution)/shard_map/ppermute | solution.py:319
  60.1 4.7 %attend.9 = (bf16[8,128,512]{2,1,0:T(8,128)(2,1)S(1)}, bf16[8,128,512]{2,1,0:T(8,128)(2,1)S(1)}) custom-call(s32[8192]{0:T(1024)S(1)} %fusion.24.index_ref, s32[32]{0:T(128)S(1)} %convert_reduce_fusion.1.count_ref, s32[64]{0:T(128)S(1)} %select_reduce_fusion.block_ref, s32[32]{0:T(128)S(1)} %copy-done.8, f32[16384,128]{1,0:T(8,128)S(1)} %project.7.table_ref, ...), custom_call_target="tpu_custom_call" | custom-call | flops 1073741824 | bytes 4194304 | tf_op jit(solution)/shard_map/attend/pallas_call | solution.py:237
  64.9 3.9 %attend.8 = (bf16[4,128,512]{2,1,0:T(8,128)(2,1)S(1)}, bf16[4,128,512]{2,1,0:T(8,128)(2,1)S(1)}) custom-call(s32[8192]{0:T(1024)S(1)} %fusion.24.index_ref, s32[32]{0:T(128)S(1)} %convert_reduce_fusion.1.count_ref, s32[64]{0:T(128)S(1)} %select_reduce_fusion.block_ref, s32[16]{0:T(128)S(1)} %copy-done.7, f32[16384,128]{1,0:T(8,128)S(1)} %project.7.table_ref, ...), custom_call_target="tpu_custom_call" | custom-call | flops 536870912 | bytes 2097152 | tf_op jit(solution)/shard_map/attend/pallas_call | solution.py:237
  68.9 9.0 %attend.5 = (bf16[4,128,512]{2,1,0:T(8,128)(2,1)S(1)}, bf16[4,128,512]{2,1,0:T(8,128)(2,1)S(1)}, bf16[4,128,512]{2,1,0:T(8,128)(2,1)S(1)}, bf16[8,128,512]{2,1,0:T(8,128)(2,1)S(1)}) custom-call(s32[8192]{0:T(1024)S(1)} %fusion.24.index_ref, s32[32]{0:T(128)S(1)} %convert_reduce_fusion.1.count_ref, s32[64]{0:T(128)S(1)} %select_reduce_fusion.block_ref, ...), custom_call_target="tpu_custom_call" | custom-call | flops 1342177280 | bytes 5242880 | tf_op jit(solution)/shard_map/attend/pallas_call | solution.py:237
  78.1 1.1 collective-permute-start.17
  79.3 1.1 collective-permute-start.13
  80.7 4.2 %collective-permute-start.27 = (bf16[8,128,512]{2,1,0:T(8,128)(2,1)S(1)}, bf16[8,128,512]{2,1,0:T(8,128)(2,1)S(1)}, u32[]{:S(2)}, u32[]{:S(2)}) collective-permute-start(bf16[8,128,512]{2,1,0:T(8,128)(2,1)S(1)} %pad_maximum_fusion.1), channel_id=1, source_target_pairs={{0,24},{1,25},{2,26},{3,27},{4,28},{5,29},{6,30},{7,31},{8,0},{9,1... | collective-permute-start | bytes 3145736 | tf_op jit(solution)/shard_map/ppermute | solution.py:319
  85.4 4.3 %collective-permute-done.17 = bf16[4,128,512]{2,1,0:T(8,128)(2,1)S(1)} collective-permute-done((bf16[4,128,512]{2,1,0:T(8,128)(2,1)S(1)}, bf16[4,128,512]{2,1,0:T(8,128)(2,1)S(1)}, u32[]{:S(2)}, u32[]{:S(2)}) %collective-permute-start.17) | collective-permute-done | bytes 524320 | tf_op jit(solution)/shard_map/ppermute | solution.py:314
  89.8 2.7 %collective-permute-start.18 = (bf16[4,128,512]{2,1,0:T(8,128)(2,1)S(1)}, bf16[4,128,512]{2,1,0:T(8,128)(2,1)S(1)}, u32[]{:S(2)}, u32[]{:S(2)}) collective-permute-start(bf16[4,128,512]{2,1,0:T(8,128)(2,1)S(1)} %add_convert_fusion.3), channel_id=1, source_target_pairs={{0,7},{1,0},{2,1},{3,2},{4,3},{5,4},{6,5},{7,6},{8,15},{9,8},{10,9... | collective-permute-start | bytes 1572872 | tf_op jit(solution)/shard_map/ppermute | solution.py:314
  92.5 1.6 %collective-permute-done.13 = bf16[4,128,512]{2,1,0:T(8,128)(2,1)S(1)} collective-permute-done((bf16[4,128,512]{2,1,0:T(8,128)(2,1)S(1)}, bf16[4,128,512]{2,1,0:T(8,128)(2,1)S(1)}, u32[]{:S(2)}, u32[]{:S(2)}) %collective-permute-start.13) | collective-permute-done | bytes 524320 | tf_op jit(solution)/shard_map/ppermute | solution.py:314
  94.4 1.7 %gate.1.refs_10_ = bf16[256,512]{1,0:T(8,128)(2,1)S(1)} custom-call(s32[1,256]{1,0:T(1,128)S(1)} %bitcast.136, bf16[512,1024]{1,0:T(8,128)(2,1)S(1)} %copy-done.3, bf16[512,512]{1,0:T(8,128)(2,1)S(1)} %norm.1.refs_1_.refs_0_, bf16[512,512]{1,0:T(8,128)(2,1)S(1)} %collective-permute-done.11.refs_2_.refs_1_, ...), custom_call_target="tpu_custom_call" | custom-call | flops 1207959552 | bytes 4194304 | tf_op jit(solution)/shard_map/gate/pallas_call | solution.py:160
  96.1 8.1 %collective-permute-done.18 = bf16[4,128,512]{2,1,0:T(8,128)(2,1)S(1)} collective-permute-done((bf16[4,128,512]{2,1,0:T(8,128)(2,1)S(1)}, bf16[4,128,512]{2,1,0:T(8,128)(2,1)S(1)}, u32[]{:S(2)}, u32[]{:S(2)}) %collective-permute-start.18) | collective-permute-done | bytes 524320 | tf_op jit(solution)/shard_map/ppermute | solution.py:314
  104.4 3.8 %collective-permute-start.19 = (bf16[4,128,512]{2,1,0:T(8,128)(2,1)S(1)}, bf16[4,128,512]{2,1,0:T(8,128)(2,1)S(1)}, u32[]{:S(2)}, u32[]{:S(2)}) collective-permute-start(bf16[4,128,512]{2,1,0:T(8,128)(2,1)S(1)} %add_convert_fusion.2), channel_id=1, source_target_pairs={{0,7},{1,0},{2,1},{3,2},{4,3},{5,4},{6,5},{7,6},{8,15},{9,8},{10,9... | collective-permute-start | bytes 1572872 | tf_op jit(solution)/shard_map/ppermute | solution.py:314
  108.6 3.3 %collective-permute-start.32 = (bf16[64,512]{1,0:T(8,128)(2,1)S(1)}, bf16[64,512]{1,0:T(8,128)(2,1)S(1)}, u32[]{:S(2)}, u32[]{:S(2)}) collective-permute-start(bf16[64,512]{1,0:T(8,128)(2,1)S(1)} %get-tuple-element.40), channel_id=1, source_target_pairs={{0,7},{1,0},{2,1},{3,2},{4,3},{5,4},{6,5},{7,6},{8,15},{9,8},{10,9... | collective-permute-start | bytes 196616 | tf_op jit(solution)/shard_map/ppermute | solution.py:314
  111.9 8.5 %collective-permute-done.32 = bf16[64,512]{1,0:T(8,128)(2,1)S(1)} collective-permute-done((bf16[64,512]{1,0:T(8,128)(2,1)S(1)}, bf16[64,512]{1,0:T(8,128)(2,1)S(1)}, u32[]{:S(2)}, u32[]{:S(2)}) %collective-permute-start.32) | collective-permute-done | bytes 65568 | tf_op jit(solution)/shard_map/ppermute | solution.py:314
  120.4 3.6 %collective-permute-done.28 = bf16[64,512]{1,0:T(8,128)(2,1)S(1)} collective-permute-done((bf16[64,512]{1,0:T(8,128)(2,1)S(1)}, bf16[64,512]{1,0:T(8,128)(2,1)S(1)}, u32[]{:S(2)}, u32[]{:S(2)}) %collective-permute-start.28) | collective-permute-done | bytes 65568 | tf_op jit(solution)/shard_map/ppermute | solution.py:314
  124.2 3.3 %collective-permute-start.33 = (bf16[128,512]{1,0:T(8,128)(2,1)S(1)}, bf16[128,512]{1,0:T(8,128)(2,1)S(1)}, u32[]{:S(2)}, u32[]{:S(2)}) collective-permute-start(bf16[128,512]{1,0:T(8,128)(2,1)S(1)} %pad_maximum_fusion.7), channel_id=1, source_target_pairs={{0,7},{1,0},{2,1},{3,2},{4,3},{5,4},{6,5},{7,6},{8,15},{9,8},{10,9... | collective-permute-start | bytes 393224 | tf_op jit(solution)/shard_map/ppermute | solution.py:314
  127.5 2.8 %collective-permute-done.29 = bf16[128,512]{1,0:T(8,128)(2,1)S(1)} collective-permute-done((bf16[128,512]{1,0:T(8,128)(2,1)S(1)}, bf16[128,512]{1,0:T(8,128)(2,1)S(1)}, u32[]{:S(2)}, u32[]{:S(2)}) %collective-permute-start.29) | collective-permute-done | bytes 131104 | tf_op jit(solution)/shard_map/ppermute | solution.py:314
  130.5 3.4 %collective-permute-start.34 = (bf16[128,512]{1,0:T(8,128)(2,1)S(1)}, bf16[128,512]{1,0:T(8,128)(2,1)S(1)}, u32[]{:S(2)}, u32[]{:S(2)}) collective-permute-start(bf16[128,512]{1,0:T(8,128)(2,1)S(1)} %get-tuple-element.37), channel_id=1, source_target_pairs={{0,7},{1,0},{2,1},{3,2},{4,3},{5,4},{6,5},{7,6},{8,15},{9,8},{10,9... | collective-permute-start | bytes 393224 | tf_op jit(solution)/shard_map/ppermute | solution.py:314
  134.1 2.0 %collective-permute-start.20 = (bf16[64,512]{1,0:T(8,128)(2,1)S(1)}, bf16[64,512]{1,0:T(8,128)(2,1)S(1)}, u32[]{:S(2)}, u32[]{:S(2)}) collective-permute-start(bf16[64,512]{1,0:T(8,128)(2,1)S(1)} %get-tuple-element.48), channel_id=1, source_target_pairs={{0,8},{1,9},{2,10},{3,11},{4,12},{5,13},{6,14},{7,15},{8,16},{9,17... | collective-permute-start | bytes 196616 | tf_op jit(solution)/shard_map/ppermute | solution.py:319
  136.1 2.2 %collective-permute-done.22 = bf16[64,512]{1,0:T(8,128)(2,1)S(1)} collective-permute-done((bf16[64,512]{1,0:T(8,128)(2,1)S(1)}, bf16[64,512]{1,0:T(8,128)(2,1)S(1)}, u32[]{:S(2)}, u32[]{:S(2)}) %collective-permute-start.22) | collective-permute-done | bytes 65568 | tf_op jit(solution)/shard_map/ppermute | solution.py:319
  138.3 1.9 %collective-permute-done.20 = bf16[64,512]{1,0:T(8,128)(2,1)S(1)} collective-permute-done((bf16[64,512]{1,0:T(8,128)(2,1)S(1)}, bf16[64,512]{1,0:T(8,128)(2,1)S(1)}, u32[]{:S(2)}, u32[]{:S(2)}) %collective-permute-start.20) | collective-permute-done | bytes 65568 | tf_op jit(solution)/shard_map/ppermute | solution.py:319
  140.8 3.2 %collective-permute-start.23 = (bf16[128,512]{1,0:T(8,128)(2,1)S(1)}, bf16[128,512]{1,0:T(8,128)(2,1)S(1)}, u32[]{:S(2)}, u32[]{:S(2)}) collective-permute-start(bf16[128,512]{1,0:T(8,128)(2,1)S(1)} %pad_maximum_fusion.5), channel_id=1, source_target_pairs={{0,24},{1,25},{2,26},{3,27},{4,28},{5,29},{6,30},{7,31},{8,0},{9,1... | collective-permute-start | bytes 393224 | tf_op jit(solution)/shard_map/ppermute | solution.py:319
  144.2 3.4 %collective-permute-start.35 = (bf16[128,512]{1,0:T(8,128)(2,1)S(1)}, bf16[128,512]{1,0:T(8,128)(2,1)S(1)}, u32[]{:S(2)}, u32[]{:S(2)}) collective-permute-start(bf16[128,512]{1,0:T(8,128)(2,1)S(1)} %get-tuple-element.35), channel_id=1, source_target_pairs={{0,7},{1,0},{2,1},{3,2},{4,3},{5,4},{6,5},{7,6},{8,15},{9,8},{10,9... | collective-permute-start | bytes 393224 | tf_op jit(solution)/shard_map/ppermute | solution.py:314
  147.6 2.5 %collective-permute-done.35.refs_9_ = bf16[128,512]{1,0:T(8,128)(2,1)S(1)} collective-permute-done((bf16[128,512]{1,0:T(8,128)(2,1)S(1)}, bf16[128,512]{1,0:T(8,128)(2,1)S(1)}, u32[]{:S(2)}, u32[]{:S(2)}) %collective-permute-start.35) | collective-permute-done | bytes 131104 | tf_op jit(solution)/shard_map/ppermute | solution.py:314
  150.1 3.7 %collective-permute-done.31.refs_8_ = bf16[128,512]{1,0:T(8,128)(2,1)S(1)} collective-permute-done((bf16[128,512]{1,0:T(8,128)(2,1)S(1)}, bf16[128,512]{1,0:T(8,128)(2,1)S(1)}, u32[]{:S(2)}, u32[]{:S(2)}) %collective-permute-start.31) | collective-permute-done | bytes 131104 | tf_op jit(solution)/shard_map/ppermute | solution.py:314
  153.7 1.3 finish.1
  (106 shorter events, 10.9 us)
Async XLA Ops:
  0.0 1.0 copy-start.4
  1.5 36.0 %collective-permute-start.11 = (bf16[512,512]{1,0:T(8,128)(2,1)S(1)}, bf16[512,512]{1,0:T(8,128)(2,1)S(1)}, u32[]{:S(2)}, u32[]{:S(2)}) collective-permute-start(bf16[512,512]{1,0:T(8,128)(2,1)S(1)} %norm.1.refs_1_.refs_0_), channel_id=1, source_target_pairs={{0,32},{32,0},{64,96},{96,64},{128,160},{160,128},{192,224},{224,1... | collective-permute-start | bytes 1572872 | tf_op jit(solution)/shard_map/ppermute | solution.py:309
  1.6 33.1 %collective-permute-start.8 = (bf16[512,512]{1,0:T(8,128)(2,1)S(1)}, bf16[512,512]{1,0:T(8,128)(2,1)S(1)}, u32[]{:S(2)}, u32[]{:S(2)}) collective-permute-start(bf16[512,512]{1,0:T(8,128)(2,1)S(1)} %norm.1.refs_1_.refs_0_), channel_id=1, source_target_pairs={{0,64},{32,96},{64,128},{96,160},{128,192},{160,224},{192,0},{224,... | collective-permute-start | bytes 1572872 | tf_op jit(solution)/shard_map/ppermute | solution.py:304
  2.9 14.4 %collective-permute-start.5 = (bf16[512,512]{1,0:T(8,128)(2,1)S(1)}, bf16[512,512]{1,0:T(8,128)(2,1)S(1)}, u32[]{:S(2)}, u32[]{:S(2)}) collective-permute-start(bf16[512,512]{1,0:T(8,128)(2,1)S(1)} %norm.1.refs_1_.refs_0_), channel_id=1, source_target_pairs={{0,192},{32,224},{64,0},{96,32},{128,64},{160,96},{192,128},{224,1... | collective-permute-start | bytes 1572872 | tf_op jit(solution)/shard_map/ppermute | solution.py:304
  3.7 8.3 %collective-permute-start = (s32[256]{0:T(256)}, s32[256]{0:T(256)S(1)}, u32[]{:S(2)}, u32[]{:S(2)}) collective-permute-start(s32[256]{0:T(256)} %param.13), channel_id=1, source_target_pairs={{0,7},{1,0},{2,1},{3,2},{4,3},{5,4},{6,5},{7,6},{8,15},{9,8},{10,9... | collective-permute-start | bytes 3080 | tf_op jit(solution)/shard_map/ppermute | solution.py:314
  12.7 5.0 %collective-permute-start.1 = (s32[512]{0:T(512)S(1)}, s32[512]{0:T(512)S(1)}, u32[]{:S(2)}, u32[]{:S(2)}) collective-permute-start(s32[512]{0:T(512)S(1)} %pad_add_fusion.2), channel_id=1, source_target_pairs={{0,6},{1,7},{2,0},{3,1},{4,2},{5,3},{6,4},{7,5},{8,14},{9,15},{10,... | collective-permute-start | bytes 6152 | tf_op jit(solution)/shard_map/ppermute | solution.py:314
  17.3 17.4 %collective-permute-start.6 = (bf16[512,512]{1,0:T(8,128)(2,1)S(1)}, bf16[512,512]{1,0:T(8,128)(2,1)S(1)}, u32[]{:S(2)}, u32[]{:S(2)}) collective-permute-start(bf16[512,512]{1,0:T(8,128)(2,1)S(1)} %collective-permute-done.5.refs_1_.refs_2_), channel_id=1, source_target_pairs={{0,192},{32,224},{64,0},{96,32},{128,64},{160,96},{192,128},{224,1... | collective-permute-start | bytes 1572872 | tf_op jit(solution)/shard_map/ppermute | solution.py:304
  18.4 8.8 %collective-permute-start.2 = (s32[1024]{0:T(1024)S(1)}, s32[1024]{0:T(1024)S(1)}, u32[]{:S(2)}, u32[]{:S(2)}) collective-permute-start(s32[1024]{0:T(1024)S(1)} %pad_add_fusion.1), channel_id=1, source_target_pairs={{0,4},{1,5},{2,6},{3,7},{4,0},{5,1},{6,2},{7,3},{8,12},{9,13},{10,... | collective-permute-start | bytes 12296 | tf_op jit(solution)/shard_map/ppermute | solution.py:314
  27.9 4.4 %collective-permute-start.3 = (s32[2048]{0:T(1024)S(1)}, s32[2048]{0:T(1024)S(1)}, u32[]{:S(2)}, u32[]{:S(2)}) collective-permute-start(s32[2048]{0:T(1024)S(1)} %pad_add_fusion), channel_id=1, source_target_pairs={{0,24},{1,25},{2,26},{3,27},{4,28},{5,29},{6,30},{7,31},{8,0},{9,1... | collective-permute-start | bytes 24584 | tf_op jit(solution)/shard_map/ppermute | solution.py:319
  30.9 7.5 %collective-permute-start.10 = (bf16[512,512]{1,0:T(8,128)(2,1)S(1)}, bf16[512,512]{1,0:T(8,128)(2,1)S(1)}, u32[]{:S(2)}, u32[]{:S(2)}) collective-permute-start(bf16[512,512]{1,0:T(8,128)(2,1)S(1)} %collective-permute-done.5.refs_1_.refs_2_), channel_id=1, source_target_pairs={{0,32},{32,0},{64,96},{96,64},{128,160},{160,128},{192,224},{224,1... | collective-permute-start | bytes 1572872 | tf_op jit(solution)/shard_map/ppermute | solution.py:309
  32.2 5.2 %collective-permute-start.4 = (s32[4096]{0:T(1024)S(1)}, s32[4096]{0:T(1024)S(1)}, u32[]{:S(2)}, u32[]{:S(2)}) collective-permute-start(s32[4096]{0:T(1024)S(1)} %get-tuple-element.51), channel_id=1, source_target_pairs={{0,16},{1,17},{2,18},{3,19},{4,20},{5,21},{6,22},{7,23},{8,24},{9,... | collective-permute-start | bytes 49160 | tf_op jit(solution)/shard_map/ppermute | solution.py:319
  34.7 4.5 %collective-permute-start.9 = (bf16[512,512]{1,0:T(8,128)(2,1)S(1)}, bf16[512,512]{1,0:T(8,128)(2,1)S(1)}, u32[]{:S(2)}, u32[]{:S(2)}) collective-permute-start(bf16[512,512]{1,0:T(8,128)(2,1)S(1)} %collective-permute-done.8.refs_1_.refs_6_), channel_id=1, source_target_pairs={{0,32},{32,0},{64,96},{96,64},{128,160},{160,128},{192,224},{224,1... | collective-permute-start | bytes 1572872 | tf_op jit(solution)/shard_map/ppermute | solution.py:309
  34.7 5.4 %collective-permute-start.7 = (bf16[512,512]{1,0:T(8,128)(2,1)S(1)}, bf16[512,512]{1,0:T(8,128)(2,1)S(1)}, u32[]{:S(2)}, u32[]{:S(2)}) collective-permute-start(bf16[512,512]{1,0:T(8,128)(2,1)S(1)} %collective-permute-done.6.refs_1_.refs_4_), channel_id=1, source_target_pairs={{0,32},{32,0},{64,96},{96,64},{128,160},{160,128},{192,224},{224,1... | collective-permute-start | bytes 1572872 | tf_op jit(solution)/shard_map/ppermute | solution.py:309
  35.3 1.2 copy-start.2
  40.1 1.6 %copy-start = (bf16[2048,512]{1,0:T(8,128)(2,1)S(1)}, bf16[2048,512]{1,0:T(8,128)(2,1)}, u32[]{:S(2)}) copy-start(bf16[2048,512]{1,0:T(8,128)(2,1)} %k_ref.9) | copy-start | bytes 6291460
  40.1 2.2 %copy-start.1 = (bf16[2048,512]{1,0:T(8,128)(2,1)S(1)}, bf16[2048,512]{1,0:T(8,128)(2,1)}, u32[]{:S(2)}) copy-start(bf16[2048,512]{1,0:T(8,128)(2,1)} %v_ref.9) | copy-start | bytes 6291460
  40.1 2.2 %copy-start.10 = (s32[16]{0:T(128)S(1)}, s32[16]{0:T(128)}, u32[]{:S(2)}) copy-start(s32[16]{0:T(128)} %constant.131.clone.order_ref) | copy-start | bytes 196
  42.3 3.1 %copy-start.9 = (s32[24]{0:T(128)S(1)}, s32[24]{0:T(128)}, u32[]{:S(2)}) copy-start(s32[24]{0:T(128)} %constant.130.clone.order_ref) | copy-start | bytes 292
  45.4 14.8 %copy-start.8 = (s32[32]{0:T(128)S(1)}, s32[32]{0:T(128)}, u32[]{:S(2)}) copy-start(s32[32]{0:T(128)} %constant.132.clone.order_ref) | copy-start | bytes 388
  49.9 15.0 %copy-start.7 = (s32[16]{0:T(128)S(1)}, s32[16]{0:T(128)}, u32[]{:S(2)}) copy-start(s32[16]{0:T(128)} %constant.133.clone.order_ref) | copy-start | bytes 196
  49.9 29.2 %collective-permute-start.12 = (bf16[2,128,512]{2,1,0:T(8,128)(2,1)S(1)}, bf16[2,128,512]{2,1,0:T(8,128)(2,1)S(1)}, u32[]{:S(2)}, u32[]{:S(2)}) collective-permute-start(bf16[2,128,512]{2,1,0:T(8,128)(2,1)S(1)} %get-tuple-element.20), channel_id=1, source_target_pairs={{0,1},{1,2},{2,3},{3,4},{4,5},{5,6},{6,7},{7,0},{8,9},{9,10},{10,1... | collective-permute-start | bytes 786440 | tf_op jit(solution)/shard_map/ppermute | solution.py:314
  52.1 25.9 %collective-permute-start.16 = (bf16[2,128,512]{2,1,0:T(8,128)(2,1)S(1)}, bf16[2,128,512]{2,1,0:T(8,128)(2,1)S(1)}, u32[]{:S(2)}, u32[]{:S(2)}) collective-permute-start(bf16[2,128,512]{2,1,0:T(8,128)(2,1)S(1)} %get-tuple-element.25), channel_id=1, source_target_pairs={{0,7},{1,0},{2,1},{3,2},{4,3},{5,4},{6,5},{7,6},{8,15},{9,8},{10,9... | collective-permute-start | bytes 786440 | tf_op jit(solution)/shard_map/ppermute | solution.py:314
  55.6 29.2 %collective-permute-start.24 = (bf16[4,128,512]{2,1,0:T(8,128)(2,1)S(1)}, bf16[4,128,512]{2,1,0:T(8,128)(2,1)S(1)}, u32[]{:S(2)}, u32[]{:S(2)}) collective-permute-start(bf16[4,128,512]{2,1,0:T(8,128)(2,1)S(1)} %get-tuple-element.29), channel_id=1, source_target_pairs={{0,8},{1,9},{2,10},{3,11},{4,12},{5,13},{6,14},{7,15},{8,16},{9,17... | collective-permute-start | bytes 1572872 | tf_op jit(solution)/shard_map/ppermute | solution.py:319
  55.8 24.6 %collective-permute-start.26 = (bf16[4,128,512]{2,1,0:T(8,128)(2,1)S(1)}, bf16[4,128,512]{2,1,0:T(8,128)(2,1)S(1)}, u32[]{:S(2)}, u32[]{:S(2)}) collective-permute-start(bf16[4,128,512]{2,1,0:T(8,128)(2,1)S(1)} %get-tuple-element.32), channel_id=1, source_target_pairs={{0,24},{1,25},{2,26},{3,27},{4,28},{5,29},{6,30},{7,31},{8,0},{9,1... | collective-permute-start | bytes 1572872 | tf_op jit(solution)/shard_map/ppermute | solution.py:319
  64.8 4.1 %copy-start.6 = (s32[40]{0:T(128)S(1)}, s32[40]{0:T(128)}, u32[]{:S(2)}) copy-start(s32[40]{0:T(128)} %constant.134.clone.order_ref) | copy-start | bytes 484
  77.9 16.4 %copy-start.3 = (bf16[512,1024]{1,0:T(8,128)(2,1)S(1)}, bf16[512,1024]{1,0:T(8,128)(2,1)}, u32[]{:S(2)}) copy-start(bf16[512,1024]{1,0:T(8,128)(2,1)} %w_ref.3) | copy-start | bytes 3145732
  78.1 11.6 %collective-permute-start.17 = (bf16[4,128,512]{2,1,0:T(8,128)(2,1)S(1)}, bf16[4,128,512]{2,1,0:T(8,128)(2,1)S(1)}, u32[]{:S(2)}, u32[]{:S(2)}) collective-permute-start(bf16[4,128,512]{2,1,0:T(8,128)(2,1)S(1)} %pad_maximum_fusion.3), channel_id=1, source_target_pairs={{0,7},{1,0},{2,1},{3,2},{4,3},{5,4},{6,5},{7,6},{8,15},{9,8},{10,9... | collective-permute-start | bytes 1572872 | tf_op jit(solution)/shard_map/ppermute | solution.py:314
  79.3 14.8 %collective-permute-start.13 = (bf16[4,128,512]{2,1,0:T(8,128)(2,1)S(1)}, bf16[4,128,512]{2,1,0:T(8,128)(2,1)S(1)}, u32[]{:S(2)}, u32[]{:S(2)}) collective-permute-start(bf16[4,128,512]{2,1,0:T(8,128)(2,1)S(1)} %pad_maximum_fusion.2), channel_id=1, source_target_pairs={{0,1},{1,2},{2,3},{3,4},{4,5},{5,6},{6,7},{7,0},{8,9},{9,10},{10,1... | collective-permute-start | bytes 1572872 | tf_op jit(solution)/shard_map/ppermute | solution.py:314
  80.7 27.8 %collective-permute-start.27 = (bf16[8,128,512]{2,1,0:T(8,128)(2,1)S(1)}, bf16[8,128,512]{2,1,0:T(8,128)(2,1)S(1)}, u32[]{:S(2)}, u32[]{:S(2)}) collective-permute-start(bf16[8,128,512]{2,1,0:T(8,128)(2,1)S(1)} %pad_maximum_fusion.1), channel_id=1, source_target_pairs={{0,24},{1,25},{2,26},{3,27},{4,28},{5,29},{6,30},{7,31},{8,0},{9,1... | collective-permute-start | bytes 3145736 | tf_op jit(solution)/shard_map/ppermute | solution.py:319
  85.1 23.3 %collective-permute-start.25 = (bf16[8,128,512]{2,1,0:T(8,128)(2,1)S(1)}, bf16[8,128,512]{2,1,0:T(8,128)(2,1)S(1)}, u32[]{:S(2)}, u32[]{:S(2)}) collective-permute-start(bf16[8,128,512]{2,1,0:T(8,128)(2,1)S(1)} %pad_maximum_fusion), channel_id=1, source_target_pairs={{0,8},{1,9},{2,10},{3,11},{4,12},{5,13},{6,14},{7,15},{8,16},{9,17... | collective-permute-start | bytes 3145736 | tf_op jit(solution)/shard_map/ppermute | solution.py:319
  89.8 14.4 %collective-permute-start.18 = (bf16[4,128,512]{2,1,0:T(8,128)(2,1)S(1)}, bf16[4,128,512]{2,1,0:T(8,128)(2,1)S(1)}, u32[]{:S(2)}, u32[]{:S(2)}) collective-permute-start(bf16[4,128,512]{2,1,0:T(8,128)(2,1)S(1)} %add_convert_fusion.3), channel_id=1, source_target_pairs={{0,7},{1,0},{2,1},{3,2},{4,3},{5,4},{6,5},{7,6},{8,15},{9,8},{10,9... | collective-permute-start | bytes 1572872 | tf_op jit(solution)/shard_map/ppermute | solution.py:314
  94.2 13.9 %collective-permute-start.14 = (bf16[4,128,512]{2,1,0:T(8,128)(2,1)S(1)}, bf16[4,128,512]{2,1,0:T(8,128)(2,1)S(1)}, u32[]{:S(2)}, u32[]{:S(2)}) collective-permute-start(bf16[4,128,512]{2,1,0:T(8,128)(2,1)S(1)} %add_convert_fusion.5), channel_id=1, source_target_pairs={{0,1},{1,2},{2,3},{3,4},{4,5},{5,6},{6,7},{7,0},{8,9},{9,10},{10,1... | collective-permute-start | bytes 1572872 | tf_op jit(solution)/shard_map/ppermute | solution.py:314
  94.3 59.4 %copy-start.5 = (bf16[512,512]{1,0:T(8,128)(2,1)S(1)}, bf16[512,512]{1,0:T(8,128)(2,1)}, u32[]{:S(2)}) copy-start(bf16[512,512]{1,0:T(8,128)(2,1)} %refs_11_.1) | copy-start | bytes 1572868
  104.4 29.5 %collective-permute-start.19 = (bf16[4,128,512]{2,1,0:T(8,128)(2,1)S(1)}, bf16[4,128,512]{2,1,0:T(8,128)(2,1)S(1)}, u32[]{:S(2)}, u32[]{:S(2)}) collective-permute-start(bf16[4,128,512]{2,1,0:T(8,128)(2,1)S(1)} %add_convert_fusion.2), channel_id=1, source_target_pairs={{0,7},{1,0},{2,1},{3,2},{4,3},{5,4},{6,5},{7,6},{8,15},{9,8},{10,9... | collective-permute-start | bytes 1572872 | tf_op jit(solution)/shard_map/ppermute | solution.py:314
  108.3 25.6 %collective-permute-start.15 = (bf16[4,128,512]{2,1,0:T(8,128)(2,1)S(1)}, bf16[4,128,512]{2,1,0:T(8,128)(2,1)S(1)}, u32[]{:S(2)}, u32[]{:S(2)}) collective-permute-start(bf16[4,128,512]{2,1,0:T(8,128)(2,1)S(1)} %add_convert_fusion.4), channel_id=1, source_target_pairs={{0,1},{1,2},{2,3},{3,4},{4,5},{5,6},{6,7},{7,0},{8,9},{9,10},{10,1... | collective-permute-start | bytes 1572872 | tf_op jit(solution)/shard_map/ppermute | solution.py:314
  108.6 11.8 %collective-permute-start.32 = (bf16[64,512]{1,0:T(8,128)(2,1)S(1)}, bf16[64,512]{1,0:T(8,128)(2,1)S(1)}, u32[]{:S(2)}, u32[]{:S(2)}) collective-permute-start(bf16[64,512]{1,0:T(8,128)(2,1)S(1)} %get-tuple-element.40), channel_id=1, source_target_pairs={{0,7},{1,0},{2,1},{3,2},{4,3},{5,4},{6,5},{7,6},{8,15},{9,8},{10,9... | collective-permute-start | bytes 196616 | tf_op jit(solution)/shard_map/ppermute | solution.py:314
  111.8 12.1 %collective-permute-start.28 = (bf16[64,512]{1,0:T(8,128)(2,1)S(1)}, bf16[64,512]{1,0:T(8,128)(2,1)S(1)}, u32[]{:S(2)}, u32[]{:S(2)}) collective-permute-start(bf16[64,512]{1,0:T(8,128)(2,1)S(1)} %get-tuple-element.42), channel_id=1, source_target_pairs={{0,1},{1,2},{2,3},{3,4},{4,5},{5,6},{6,7},{7,0},{8,9},{9,10},{10,1... | collective-permute-start | bytes 196616 | tf_op jit(solution)/shard_map/ppermute | solution.py:314
  124.1 6.3 %collective-permute-start.29 = (bf16[128,512]{1,0:T(8,128)(2,1)S(1)}, bf16[128,512]{1,0:T(8,128)(2,1)S(1)}, u32[]{:S(2)}, u32[]{:S(2)}) collective-permute-start(bf16[128,512]{1,0:T(8,128)(2,1)S(1)} %pad_maximum_fusion.6), channel_id=1, source_target_pairs={{0,1},{1,2},{2,3},{3,4},{4,5},{5,6},{6,7},{7,0},{8,9},{9,10},{10,1... | collective-permute-start | bytes 393224 | tf_op jit(solution)/shard_map/ppermute | solution.py:314
  124.2 6.1 %collective-permute-start.33 = (bf16[128,512]{1,0:T(8,128)(2,1)S(1)}, bf16[128,512]{1,0:T(8,128)(2,1)S(1)}, u32[]{:S(2)}, u32[]{:S(2)}) collective-permute-start(bf16[128,512]{1,0:T(8,128)(2,1)S(1)} %pad_maximum_fusion.7), channel_id=1, source_target_pairs={{0,7},{1,0},{2,1},{3,2},{4,3},{5,4},{6,5},{7,6},{8,15},{9,8},{10,9... | collective-permute-start | bytes 393224 | tf_op jit(solution)/shard_map/ppermute | solution.py:314
  130.5 13.5 %collective-permute-start.34 = (bf16[128,512]{1,0:T(8,128)(2,1)S(1)}, bf16[128,512]{1,0:T(8,128)(2,1)S(1)}, u32[]{:S(2)}, u32[]{:S(2)}) collective-permute-start(bf16[128,512]{1,0:T(8,128)(2,1)S(1)} %get-tuple-element.37), channel_id=1, source_target_pairs={{0,7},{1,0},{2,1},{3,2},{4,3},{5,4},{6,5},{7,6},{8,15},{9,8},{10,9... | collective-permute-start | bytes 393224 | tf_op jit(solution)/shard_map/ppermute | solution.py:314
  133.9 10.1 %collective-permute-start.30 = (bf16[128,512]{1,0:T(8,128)(2,1)S(1)}, bf16[128,512]{1,0:T(8,128)(2,1)S(1)}, u32[]{:S(2)}, u32[]{:S(2)}) collective-permute-start(bf16[128,512]{1,0:T(8,128)(2,1)S(1)} %get-tuple-element.38), channel_id=1, source_target_pairs={{0,1},{1,2},{2,3},{3,4},{4,5},{5,6},{6,7},{7,0},{8,9},{9,10},{10,1... | collective-permute-start | bytes 393224 | tf_op jit(solution)/shard_map/ppermute | solution.py:314
  134.0 4.3 %collective-permute-start.22 = (bf16[64,512]{1,0:T(8,128)(2,1)S(1)}, bf16[64,512]{1,0:T(8,128)(2,1)S(1)}, u32[]{:S(2)}, u32[]{:S(2)}) collective-permute-start(bf16[64,512]{1,0:T(8,128)(2,1)S(1)} %get-tuple-element.46), channel_id=1, source_target_pairs={{0,24},{1,25},{2,26},{3,27},{4,28},{5,29},{6,30},{7,31},{8,0},{9,1... | collective-permute-start | bytes 196616 | tf_op jit(solution)/shard_map/ppermute | solution.py:319
  134.1 6.2 %collective-permute-start.20 = (bf16[64,512]{1,0:T(8,128)(2,1)S(1)}, bf16[64,512]{1,0:T(8,128)(2,1)S(1)}, u32[]{:S(2)}, u32[]{:S(2)}) collective-permute-start(bf16[64,512]{1,0:T(8,128)(2,1)S(1)} %get-tuple-element.48), channel_id=1, source_target_pairs={{0,8},{1,9},{2,10},{3,11},{4,12},{5,13},{6,14},{7,15},{8,16},{9,17... | collective-permute-start | bytes 196616 | tf_op jit(solution)/shard_map/ppermute | solution.py:319
  140.3 7.2 %collective-permute-start.21 = (bf16[128,512]{1,0:T(8,128)(2,1)S(1)}, bf16[128,512]{1,0:T(8,128)(2,1)S(1)}, u32[]{:S(2)}, u32[]{:S(2)}) collective-permute-start(bf16[128,512]{1,0:T(8,128)(2,1)S(1)} %pad_maximum_fusion.4), channel_id=1, source_target_pairs={{0,8},{1,9},{2,10},{3,11},{4,12},{5,13},{6,14},{7,15},{8,16},{9,17... | collective-permute-start | bytes 393224 | tf_op jit(solution)/shard_map/ppermute | solution.py:319
  140.8 6.7 %collective-permute-start.23 = (bf16[128,512]{1,0:T(8,128)(2,1)S(1)}, bf16[128,512]{1,0:T(8,128)(2,1)S(1)}, u32[]{:S(2)}, u32[]{:S(2)}) collective-permute-start(bf16[128,512]{1,0:T(8,128)(2,1)S(1)} %pad_maximum_fusion.5), channel_id=1, source_target_pairs={{0,24},{1,25},{2,26},{3,27},{4,28},{5,29},{6,30},{7,31},{8,0},{9,1... | collective-permute-start | bytes 393224 | tf_op jit(solution)/shard_map/ppermute | solution.py:319
  144.2 5.9 %collective-permute-start.35 = (bf16[128,512]{1,0:T(8,128)(2,1)S(1)}, bf16[128,512]{1,0:T(8,128)(2,1)S(1)}, u32[]{:S(2)}, u32[]{:S(2)}) collective-permute-start(bf16[128,512]{1,0:T(8,128)(2,1)S(1)} %get-tuple-element.35), channel_id=1, source_target_pairs={{0,7},{1,0},{2,1},{3,2},{4,3},{5,4},{6,5},{7,6},{8,15},{9,8},{10,9... | collective-permute-start | bytes 393224 | tf_op jit(solution)/shard_map/ppermute | solution.py:314
  147.6 6.2 %collective-permute-start.31 = (bf16[128,512]{1,0:T(8,128)(2,1)S(1)}, bf16[128,512]{1,0:T(8,128)(2,1)S(1)}, u32[]{:S(2)}, u32[]{:S(2)}) collective-permute-start(bf16[128,512]{1,0:T(8,128)(2,1)S(1)} %get-tuple-element.36), channel_id=1, source_target_pairs={{0,1},{1,2},{2,3},{3,4},{4,5},{5,6},{6,7},{7,0},{8,9},{9,10},{10,1... | collective-permute-start | bytes 393224 | tf_op jit(solution)/shard_map/ppermute | solution.py:314
